TPU v7x, 32 devices: a whole 2x2x4 slice. The times are simulated.
32 devices in a mesh: sub: 8 (over z, y), iter: 4 (over x, core).
Axes of the slice: x: 2, y: 2, z: 4, core: 2. Of those that a mesh axis runs over, the one named last changes fastest.
Arguments:
- fields: float32 [4, 16, 128, 128], P('iter', 'sub'), may hold values from -6 to 6
- labels: int32 [16, 128, 128], P('sub'), may hold values from 0 to 3
- traces: float32 [4, 8, 4, 128, 128], P('iter', 'sub'), may hold values from -6 to 6
- new_guess: float32 [2, 8, 4, 128, 128], P(None, 'sub'), may hold values from -6 to 6
- cond_table: float32 [4], replicated, may hold values from 0.2 to 5
- cap_table: float32 [4], replicated, may hold values from 0.5 to 4
Outputs:
- end_fields: float32 [4, 16, 128, 128], P('iter', 'sub')
- corrected: float32 [4, 8, 4, 128, 128], P('iter', 'sub')
All inputs are finite; a program needn't handle non-finite values.
Results may differ from a plain program's by a relative error of at most 0.00002.
Values sent between devices are 32-bit elements; how exact they have to be, the bound alone decides.
No kernel may reach another device: no remote copies, remote signals or barrier semaphores. Data moves between devices by JAX's collectives and lax.ppermute only.
A program may use at most 64 MiB of HBM per device.

v0:
```python
import jax
import jax.numpy as jnp
from jax import lax
from jax.sharding import PartitionSpec as P

SWEEPS = 3
TICKS = 3


def shifted(value, axis, steps):
    count = lax.axis_size(axis)
    leading, last = (max(0, -steps), min(count, count - steps))
    return lax.ppermute(value, axis, [(source, source + steps) for source in range(leading, last)])


def harmonic(first, second):
    return 2.0 * first * second / (first + second)


def setup(labels, cond_table, cap_table, left_mask, right_mask):
    conduct = jnp.zeros(labels.shape, jnp.float32)
    capacity = jnp.zeros(labels.shape, jnp.float32)
    for cls in range(cond_table.shape[0]):
        hit = labels == cls
        conduct = jnp.where(hit, cond_table[cls], conduct)
        capacity = jnp.where(hit, cap_table[cls], capacity)
    face_x = harmonic(conduct[:, 1:], conduct[:, :-1])
    face_y = harmonic(conduct[:, :, 1:], conduct[:, :, :-1])
    face_z = harmonic(conduct[:, :, :, 1:], conduct[:, :, :, :-1])
    end_first = 2.0 * conduct[:, 0]
    end_last = 2.0 * conduct[:, -1]
    sum_x = jnp.pad(face_x, ((0, 0), (1, 0), (0, 0), (0, 0))) + jnp.pad(
        face_x, ((0, 0), (0, 1), (0, 0), (0, 0))
    )
    sum_x = sum_x.at[:, 0].add(end_first).at[:, -1].add(end_last)
    sum_y = jnp.pad(face_y, ((0, 0), (0, 0), (1, 0), (0, 0))) + jnp.pad(
        face_y, ((0, 0), (0, 0), (0, 1), (0, 0))
    )
    sum_y = sum_y.at[:, :, 0].add(2.0 * conduct[:, :, 0]).at[:, :, -1].add(2.0 * conduct[:, :, -1])
    sum_z = jnp.pad(face_z, ((0, 0), (0, 0), (0, 0), (1, 0))) + jnp.pad(
        face_z, ((0, 0), (0, 0), (0, 0), (0, 1))
    )
    sum_z = (
        sum_z.at[:, :, :, 0]
        .add(2.0 * conduct[:, :, :, 0])
        .at[:, :, :, -1]
        .add(2.0 * conduct[:, :, :, -1])
    )
    diag_d = capacity + sum_x + sum_y + sum_z
    diag_n = diag_d.at[:, 0].add(-left_mask[:, None, None] * end_first)
    diag_n = diag_n.at[:, -1].add(-right_mask[:, None, None] * end_last)
    return (capacity, face_x, face_y, face_z, end_first, end_last, diag_d, diag_n)


def relax(value, rhs, diag, face_x, face_y, face_z):
    for sweep in range(SWEEPS):
        near = jnp.pad(face_x * value[:, :-1], ((0, 0), (1, 0), (0, 0), (0, 0)))
        near = near + jnp.pad(face_x * value[:, 1:], ((0, 0), (0, 1), (0, 0), (0, 0)))
        near = near + jnp.pad(face_y * value[:, :, :-1], ((0, 0), (0, 0), (1, 0), (0, 0)))
        near = near + jnp.pad(face_y * value[:, :, 1:], ((0, 0), (0, 0), (0, 1), (0, 0)))
        near = near + jnp.pad(face_z * value[:, :, :, :-1], ((0, 0), (0, 0), (0, 0), (1, 0)))
        near = near + jnp.pad(face_z * value[:, :, :, 1:], ((0, 0), (0, 0), (0, 0), (0, 1)))
        value = (rhs + near) / diag
    return value


def dirichlet(state, left_trace, right_trace, coeffs):
    capacity, face_x, face_y, face_z, end_first, end_last, diag_d, diag_n = coeffs
    firsts = []
    lasts = []
    for step in range(left_trace.shape[1]):
        rhs = capacity * state
        rhs = rhs.at[:, 0].add(end_first * left_trace[:, step])
        rhs = rhs.at[:, -1].add(end_last * right_trace[:, step])
        state = relax(state, rhs, diag_d, face_x, face_y, face_z)
        firsts.append(state[:, 0])
        lasts.append(state[:, -1])
    return (state, jnp.stack(firsts, axis=1), jnp.stack(lasts, axis=1))


def neumann(left_jump, right_jump, coeffs):
    capacity, face_x, face_y, face_z, end_first, end_last, diag_d, diag_n = coeffs
    psi = jnp.zeros(diag_n.shape, jnp.float32)
    firsts = []
    lasts = []
    for step in range(left_jump.shape[1]):
        rhs = capacity * psi
        rhs = rhs.at[:, 0].add(left_jump[:, step])
        rhs = rhs.at[:, -1].add(right_jump[:, step])
        psi = relax(psi, rhs, diag_n, face_x, face_y, face_z)
        firsts.append(psi[:, 0])
        lasts.append(psi[:, -1])
    return (jnp.stack(firsts, axis=1), jnp.stack(lasts, axis=1))


def local(fields, labels, traces, new_guess, cond_table, cap_table):
    sub_count = lax.axis_size("sub")
    sub_pos = lax.axis_index("sub")
    group_pos = lax.axis_index("iter")
    left_mask = jnp.reshape((sub_pos > 0).astype(jnp.float32), (1,))
    right_mask = jnp.reshape((sub_pos < sub_count - 1).astype(jnp.float32), (1,))
    right_wide = right_mask[:, None, None, None]
    coeffs = setup(labels[None], cond_table, cap_table, left_mask, right_mask)
    end_first, end_last = (coeffs[4], coeffs[5])
    state = fields
    right_trace = traces[0] * right_wide
    corrected = right_trace
    for tick in range(TICKS):
        left_trace = shifted(right_trace, "sub", 1)
        state, firsts, lasts = dirichlet(state, left_trace, right_trace, coeffs)
        q_first = end_first[:, None] * (firsts - left_trace)
        q_last = end_last[:, None] * (lasts - right_trace)
        from_right = shifted(q_first, "sub", -1)
        right_jump = (q_last + from_right) * right_wide
        left_jump = shifted(right_jump, "sub", 1)
        psi_first, psi_last = neumann(left_jump, right_jump, coeffs)
        psi_right = shifted(psi_first, "sub", -1)
        corrected = (right_trace + 0.25 * (psi_last + psi_right)) * right_wide
        if tick + 1 < TICKS:
            passed = shifted(corrected, "iter", 1)
            right_trace = jnp.where(group_pos == 0, new_guess[tick] * right_wide, passed)
    return (state, corrected[None])


def solution(mesh):
    return jax.shard_map(
        local,
        mesh=mesh,
        in_specs=(
            P("iter", "sub", None, None),
            P("sub", None, None),
            P("iter", "sub", None, None, None),
            P(None, "sub", None, None, None),
            P(),
            P(),
        ),
        out_specs=(P("iter", "sub", None, None), P("iter", "sub", None, None, None)),
        check_vma=False,
    )
```

profile of v0, /device:TPU:10, one launch (start us, length us, event | category | flops | bytes accessed | tf_op | source)
XLA Modules:
  0.0 214.0 jit_solution(14599693469554456210)
XLA Ops:
  1.7 3.4 %collective-permute-start = (f32[1,4,128,128]{3,2,1,0:T(8,128)S(1)}, f32[1,4,128,128]{3,2,1,0:T(8,128)S(1)}, u32[]{:S(2)}, u32[]{:S(2)}) collective-permute-start(f32[1,4,128,128]{3,2,1,0:T(8,128)S(1)} %multiply_bitcast_fusion), channel_id=1, source_target_pairs={{0,4},{4,8},{8,12},{12,16},{16,20},{20,24},{24,28},{1,5},{5,9},{9,... | collective-permute-start | bytes 786440 | tf_op jit(solution)/shard_map/ppermute | solution.py:13
  6.4 2.6 %broadcast_multiply_fusion.2 = (f32[2,128,128]{2,1,0:T(8,128)S(1)}, pred[2,128,128]{2,1,0:T(8,128)(4,1)S(1)}, pred[2,128,128]{2,1,0:T(8,128)(4,1)S(1)}, pred[2,1...) fusion(f32[]{:T(128)} %bitcast.3, f32[]{:T(128)} %bitcast.2, f32[]{:T(128)} %bitcast.1, f32[]{:T(128)} %bitcast, ...), kind=kLoop, calls=%fused_computation.656 | loop fusion | flops 294912 | bytes 393232 | tf_op jit(solution)/shard_map/mul | solution.py:87
  9.0 5.0 %fusion.107 = (f32[1,2,128,128]{3,2,1,0:T(8,128)S(1)}, f32[1,2,128,128]{3,2,1,0:T(8,128)S(1)}) fusion(pred[2,128,128]{2,1,0:T(8,128)(4,1)S(1)} %get-tuple-element.718, pred[2,128,128]{2,1,0:T(8,128)(4,1)S(1)} %get-tuple-element.717, pred[2,128,128]{2,1,0:T(8,128)(4,1)S(1)} %get-tuple-element.716, pred[2,128,128]{2,1,0:T(8,128)(4,1)S(1)} %get-tuple-element.715, ...), kind=kLoop, calls=%fused_computation.709 | loop fusion | flops 294912 | bytes 393248 | tf_op jit(solution)/shard_map/mul | solution.py:87
  16.6 2.6 %pad_add_fusion = (f32[1,2,128,128]{3,2,1,0:T(8,128)S(1)}, f32[1,2,128,128]{3,2,1,0:T(8,128)S(1)}) fusion(f32[1,1,128,128]{3,2,1,0:T(8,128)S(1)} %get-tuple-element.709, f32[1,2,128,128]{3,2,1,0:T(8,128)S(1)} %copy-done, pred[2,128,128]{2,1,0:T(8,128)(4,1)S(1)} %get-tuple-element.718, pred[2,128,128]{2,1,0:T(8,128)(4,1)S(1)} %get-tuple-element.717, ...), kind=kLoop, calls=%fused_computation.38 | loop fusion | flops 196608 | bytes 589840 | tf_op jit(solution)/shard_map/add | solution.py:32
  19.3 2.7 %add_divide_fusion.71 = (f32[1,2,128,128]{3,2,1,0:T(8,128)S(1)}, f32[1,2,128,128]{3,2,1,0:T(8,128)S(1)}) fusion(f32[1,2,128,128]{3,2,1,0:T(8,128)S(1)} %get-tuple-element.1208, f32[1,2,128,127]{3,2,1,0:T(8,128)S(1)} %get-tuple-element.1004, f32[1,2,128,127]{3,2,1,0:T(8,128)S(1)} %get-tuple-element.1003, f32[1,2,127,128]{3,2,1,0:T(8,128)S(1)} %get-tuple-element.1002, ...), kind=kLoop, calls=%fused_computation.412 | loop fusion | flops 458752 | bytes 1568784 | tf_op jit(solution)/shard_map/div | solution.py:63
  22.4 2.7 %bitcast_multiply_fusion.19 = (f32[1,2,128,128]{3,2,1,0:T(8,128)S(1)}, f32[1,2,128,128]{3,2,1,0:T(8,128)S(1)}) fusion(pred[2,128,128]{2,1,0:T(8,128)(4,1)S(1)} %get-tuple-element.718, pred[2,128,128]{2,1,0:T(8,128)(4,1)S(1)} %get-tuple-element.717, pred[2,128,128]{2,1,0:T(8,128)(4,1)S(1)} %get-tuple-element.716, ...), kind=kLoop, calls=%fused_computation.335 | loop fusion | flops 393216 | bytes 1306640 | tf_op jit(solution)/shard_map/mul | solution.py:72
  25.9 2.7 %bitcast_multiply_fusion.18 = (f32[1,2,128,128]{3,2,1,0:T(8,128)S(1)}, f32[1,2,128,128]{3,2,1,0:T(8,128)S(1)}) fusion(pred[2,128,128]{2,1,0:T(8,128)(4,1)S(1)} %get-tuple-element.718, pred[2,128,128]{2,1,0:T(8,128)(4,1)S(1)} %get-tuple-element.717, pred[2,128,128]{2,1,0:T(8,128)(4,1)S(1)} %get-tuple-element.716, ...), kind=kLoop, calls=%fused_computation.334 | loop fusion | flops 393216 | bytes 1306640 | tf_op jit(solution)/shard_map/mul | solution.py:72
  29.4 2.7 %bitcast_multiply_fusion.17 = (f32[1,2,128,128]{3,2,1,0:T(8,128)S(1)}, f32[1,2,128,128]{3,2,1,0:T(8,128)S(1)}) fusion(pred[2,128,128]{2,1,0:T(8,128)(4,1)S(1)} %get-tuple-element.718, pred[2,128,128]{2,1,0:T(8,128)(4,1)S(1)} %get-tuple-element.717, pred[2,128,128]{2,1,0:T(8,128)(4,1)S(1)} %get-tuple-element.716, ...), kind=kLoop, calls=%fused_computation.333 | loop fusion | flops 393216 | bytes 1306640 | tf_op jit(solution)/shard_map/mul | solution.py:72
  32.8 2.7 %bitcast_multiply_fusion.16 = (f32[1,2,128,128]{3,2,1,0:T(8,128)S(1)}, f32[1,2,128,128]{3,2,1,0:T(8,128)S(1)}) fusion(pred[2,128,128]{2,1,0:T(8,128)(4,1)S(1)} %get-tuple-element.718, pred[2,128,128]{2,1,0:T(8,128)(4,1)S(1)} %get-tuple-element.717, pred[2,128,128]{2,1,0:T(8,128)(4,1)S(1)} %get-tuple-element.716, ...), kind=kLoop, calls=%fused_computation.332 | loop fusion | flops 393216 | bytes 1306640 | tf_op jit(solution)/shard_map/mul | solution.py:72
  35.6 3.4 %collective-permute-start.1 = (f32[1,4,128,128]{3,2,1,0:T(8,128)S(1)}, f32[1,4,128,128]{3,2,1,0:T(8,128)S(1)}, u32[]{:S(2)}, u32[]{:S(2)}) collective-permute-start(f32[1,4,128,128]{3,2,1,0:T(8,128)S(1)} %fusion.3), channel_id=1, source_target_pairs={{4,0},{8,4},{12,8},{16,12},{20,16},{24,20},{28,24},{5,1},{9,5},{13... | collective-permute-start | bytes 786440 | tf_op jit(solution)/shard_map/ppermute | solution.py:13
  39.0 6.3 %collective-permute-done.1 = f32[1,4,128,128]{3,2,1,0:T(8,128)S(1)} collective-permute-done((f32[1,4,128,128]{3,2,1,0:T(8,128)S(1)}, f32[1,4,128,128]{3,2,1,0:T(8,128)S(1)}, u32[]{:S(2)}, u32[]{:S(2)}) %collective-permute-start.1) | collective-permute-done | bytes 262176 | tf_op jit(solution)/shard_map/ppermute | solution.py:13
  45.4 4.3 %collective-permute-start.2 = (f32[1,4,128,128]{3,2,1,0:T(8,128)S(1)}, f32[1,4,128,128]{3,2,1,0:T(8,128)S(1)}, u32[]{:S(2)}, u32[]{:S(2)}) collective-permute-start(f32[1,4,128,128]{3,2,1,0:T(8,128)S(1)} %fusion.2), channel_id=1, source_target_pairs={{0,4},{4,8},{8,12},{12,16},{16,20},{20,24},{24,28},{1,5},{5,9},{9,... | collective-permute-start | bytes 786440 | tf_op jit(solution)/shard_map/ppermute | solution.py:13
  49.8 5.3 %collective-permute-done.2 = f32[1,4,128,128]{3,2,1,0:T(8,128)S(1)} collective-permute-done((f32[1,4,128,128]{3,2,1,0:T(8,128)S(1)}, f32[1,4,128,128]{3,2,1,0:T(8,128)S(1)}, u32[]{:S(2)}, u32[]{:S(2)}) %collective-permute-start.2) | collective-permute-done | bytes 262176 | tf_op jit(solution)/shard_map/ppermute | solution.py:13
  55.7 2.7 %bitcast_multiply_fusion.15 = (f32[1,2,128,128]{3,2,1,0:T(8,128)S(1)}, f32[1,2,128,128]{3,2,1,0:T(8,128)S(1)}) fusion(pred[2,128,128]{2,1,0:T(8,128)(4,1)S(1)} %get-tuple-element.718, pred[2,128,128]{2,1,0:T(8,128)(4,1)S(1)} %get-tuple-element.717, pred[2,128,128]{2,1,0:T(8,128)(4,1)S(1)} %get-tuple-element.716, ...), kind=kLoop, calls=%fused_computation.331 | loop fusion | flops 393216 | bytes 1306640 | tf_op jit(solution)/shard_map/mul | solution.py:87
  59.2 2.7 %bitcast_multiply_fusion.14 = (f32[1,2,128,128]{3,2,1,0:T(8,128)S(1)}, f32[1,2,128,128]{3,2,1,0:T(8,128)S(1)}) fusion(pred[2,128,128]{2,1,0:T(8,128)(4,1)S(1)} %get-tuple-element.718, pred[2,128,128]{2,1,0:T(8,128)(4,1)S(1)} %get-tuple-element.717, pred[2,128,128]{2,1,0:T(8,128)(4,1)S(1)} %get-tuple-element.716, ...), kind=kLoop, calls=%fused_computation.330 | loop fusion | flops 393216 | bytes 1306640 | tf_op jit(solution)/shard_map/mul | solution.py:87
  62.6 2.7 %bitcast_multiply_fusion.13 = (f32[1,2,128,128]{3,2,1,0:T(8,128)S(1)}, f32[1,2,128,128]{3,2,1,0:T(8,128)S(1)}) fusion(pred[2,128,128]{2,1,0:T(8,128)(4,1)S(1)} %get-tuple-element.718, pred[2,128,128]{2,1,0:T(8,128)(4,1)S(1)} %get-tuple-element.717, pred[2,128,128]{2,1,0:T(8,128)(4,1)S(1)} %get-tuple-element.716, ...), kind=kLoop, calls=%fused_computation.329 | loop fusion | flops 393216 | bytes 1306640 | tf_op jit(solution)/shard_map/mul | solution.py:87
  66.3 3.3 %collective-permute-start.3 = (f32[1,4,128,128]{3,2,1,0:T(8,128)S(1)}, f32[1,4,128,128]{3,2,1,0:T(8,128)S(1)}, u32[]{:S(2)}, u32[]{:S(2)}) collective-permute-start(f32[1,4,128,128]{3,2,1,0:T(8,128)S(1)} %pad_maximum_fusion), channel_id=1, source_target_pairs={{4,0},{8,4},{12,8},{16,12},{20,16},{24,20},{28,24},{5,1},{9,5},{13... | collective-permute-start | bytes 786440 | tf_op jit(solution)/shard_map/ppermute | solution.py:13
  69.6 4.9 %collective-permute-done.3 = f32[1,4,128,128]{3,2,1,0:T(8,128)S(1)} collective-permute-done((f32[1,4,128,128]{3,2,1,0:T(8,128)S(1)}, f32[1,4,128,128]{3,2,1,0:T(8,128)S(1)}, u32[]{:S(2)}, u32[]{:S(2)}) %collective-permute-start.3) | collective-permute-done | bytes 262176 | tf_op jit(solution)/shard_map/ppermute | solution.py:13
  74.6 2.1 collective-permute-start.4
  76.7 5.8 %collective-permute-done.4 = f32[1,4,128,128]{3,2,1,0:T(8,128)S(1)} collective-permute-done((f32[1,4,128,128]{3,2,1,0:T(8,128)S(1)}, f32[1,4,128,128]{3,2,1,0:T(8,128)S(1)}, u32[]{:S(2)}, u32[]{:S(2)}) %collective-permute-start.4) | collective-permute-done | bytes 262176 | tf_op jit(solution)/shard_map/ppermute | solution.py:13
  82.5 4.3 %collective-permute-start.5 = (f32[1,4,128,128]{3,2,1,0:T(8,128)S(1)}, f32[1,4,128,128]{3,2,1,0:T(8,128)S(1)}, u32[]{:S(2)}, u32[]{:S(2)}) collective-permute-start(f32[1,4,128,128]{3,2,1,0:T(8,128)S(1)} %bitcast_select_fusion.1), channel_id=1, source_target_pairs={{0,4},{4,8},{8,12},{12,16},{16,20},{20,24},{24,28},{1,5},{5,9},{9,... | collective-permute-start | bytes 786440 | tf_op jit(solution)/shard_map/ppermute | solution.py:13
  86.8 4.8 %collective-permute-done.5 = f32[1,4,128,128]{3,2,1,0:T(8,128)S(1)} collective-permute-done((f32[1,4,128,128]{3,2,1,0:T(8,128)S(1)}, f32[1,4,128,128]{3,2,1,0:T(8,128)S(1)}, u32[]{:S(2)}, u32[]{:S(2)}) %collective-permute-start.5) | collective-permute-done | bytes 262176 | tf_op jit(solution)/shard_map/ppermute | solution.py:13
  92.2 2.7 %bitcast_multiply_fusion.12 = (f32[1,2,128,128]{3,2,1,0:T(8,128)S(1)}, f32[1,2,128,128]{3,2,1,0:T(8,128)S(1)}) fusion(pred[2,128,128]{2,1,0:T(8,128)(4,1)S(1)} %get-tuple-element.718, pred[2,128,128]{2,1,0:T(8,128)(4,1)S(1)} %get-tuple-element.717, pred[2,128,128]{2,1,0:T(8,128)(4,1)S(1)} %get-tuple-element.716, ...), kind=kLoop, calls=%fused_computation.328 | loop fusion | flops 393216 | bytes 1306640 | tf_op jit(solution)/shard_map/mul | solution.py:72
  95.7 2.7 %bitcast_multiply_fusion.11 = (f32[1,2,128,128]{3,2,1,0:T(8,128)S(1)}, f32[1,2,128,128]{3,2,1,0:T(8,128)S(1)}) fusion(pred[2,128,128]{2,1,0:T(8,128)(4,1)S(1)} %get-tuple-element.718, pred[2,128,128]{2,1,0:T(8,128)(4,1)S(1)} %get-tuple-element.717, pred[2,128,128]{2,1,0:T(8,128)(4,1)S(1)} %get-tuple-element.716, ...), kind=kLoop, calls=%fused_computation.327 | loop fusion | flops 393216 | bytes 1306640 | tf_op jit(solution)/shard_map/mul | solution.py:72
  99.1 2.7 %bitcast_multiply_fusion.10 = (f32[1,2,128,128]{3,2,1,0:T(8,128)S(1)}, f32[1,2,128,128]{3,2,1,0:T(8,128)S(1)}) fusion(pred[2,128,128]{2,1,0:T(8,128)(4,1)S(1)} %get-tuple-element.718, pred[2,128,128]{2,1,0:T(8,128)(4,1)S(1)} %get-tuple-element.717, pred[2,128,128]{2,1,0:T(8,128)(4,1)S(1)} %get-tuple-element.716, ...), kind=kLoop, calls=%fused_computation.326 | loop fusion | flops 393216 | bytes 1306640 | tf_op jit(solution)/shard_map/mul | solution.py:72
  102.6 2.7 %bitcast_multiply_fusion.9 = (f32[1,2,128,128]{3,2,1,0:T(8,128)S(1)}, f32[1,2,128,128]{3,2,1,0:T(8,128)S(1)}) fusion(pred[2,128,128]{2,1,0:T(8,128)(4,1)S(1)} %get-tuple-element.718, pred[2,128,128]{2,1,0:T(8,128)(4,1)S(1)} %get-tuple-element.717, pred[2,128,128]{2,1,0:T(8,128)(4,1)S(1)} %get-tuple-element.716, ...), kind=kLoop, calls=%fused_computation.325 | loop fusion | flops 393216 | bytes 1306640 | tf_op jit(solution)/shard_map/mul | solution.py:72
  105.3 3.3 %collective-permute-start.6 = (f32[1,4,128,128]{3,2,1,0:T(8,128)S(1)}, f32[1,4,128,128]{3,2,1,0:T(8,128)S(1)}, u32[]{:S(2)}, u32[]{:S(2)}) collective-permute-start(f32[1,4,128,128]{3,2,1,0:T(8,128)S(1)} %fusion.10), channel_id=1, source_target_pairs={{4,0},{8,4},{12,8},{16,12},{20,16},{24,20},{28,24},{5,1},{9,5},{13... | collective-permute-start | bytes 786440 | tf_op jit(solution)/shard_map/ppermute | solution.py:13
  108.7 7.8 %collective-permute-done.6 = f32[1,4,128,128]{3,2,1,0:T(8,128)S(1)} collective-permute-done((f32[1,4,128,128]{3,2,1,0:T(8,128)S(1)}, f32[1,4,128,128]{3,2,1,0:T(8,128)S(1)}, u32[]{:S(2)}, u32[]{:S(2)}) %collective-permute-start.6) | collective-permute-done | bytes 262176 | tf_op jit(solution)/shard_map/ppermute | solution.py:13
  116.5 2.1 collective-permute-start.7
  118.6 7.1 %collective-permute-done.7 = f32[1,4,128,128]{3,2,1,0:T(8,128)S(1)} collective-permute-done((f32[1,4,128,128]{3,2,1,0:T(8,128)S(1)}, f32[1,4,128,128]{3,2,1,0:T(8,128)S(1)}, u32[]{:S(2)}, u32[]{:S(2)}) %collective-permute-start.7) | collective-permute-done | bytes 262176 | tf_op jit(solution)/shard_map/ppermute | solution.py:13
  126.2 2.7 %bitcast_multiply_fusion.8 = (f32[1,2,128,128]{3,2,1,0:T(8,128)S(1)}, f32[1,2,128,128]{3,2,1,0:T(8,128)S(1)}) fusion(pred[2,128,128]{2,1,0:T(8,128)(4,1)S(1)} %get-tuple-element.718, pred[2,128,128]{2,1,0:T(8,128)(4,1)S(1)} %get-tuple-element.717, pred[2,128,128]{2,1,0:T(8,128)(4,1)S(1)} %get-tuple-element.716, ...), kind=kLoop, calls=%fused_computation.324 | loop fusion | flops 393216 | bytes 1306640 | tf_op jit(solution)/shard_map/mul | solution.py:87
  129.6 2.7 %bitcast_multiply_fusion.7 = (f32[1,2,128,128]{3,2,1,0:T(8,128)S(1)}, f32[1,2,128,128]{3,2,1,0:T(8,128)S(1)}) fusion(pred[2,128,128]{2,1,0:T(8,128)(4,1)S(1)} %get-tuple-element.718, pred[2,128,128]{2,1,0:T(8,128)(4,1)S(1)} %get-tuple-element.717, pred[2,128,128]{2,1,0:T(8,128)(4,1)S(1)} %get-tuple-element.716, ...), kind=kLoop, calls=%fused_computation.323 | loop fusion | flops 393216 | bytes 1306640 | tf_op jit(solution)/shard_map/mul | solution.py:87
  133.0 2.7 %bitcast_multiply_fusion.6 = (f32[1,2,128,128]{3,2,1,0:T(8,128)S(1)}, f32[1,2,128,128]{3,2,1,0:T(8,128)S(1)}) fusion(pred[2,128,128]{2,1,0:T(8,128)(4,1)S(1)} %get-tuple-element.718, pred[2,128,128]{2,1,0:T(8,128)(4,1)S(1)} %get-tuple-element.717, pred[2,128,128]{2,1,0:T(8,128)(4,1)S(1)} %get-tuple-element.716, ...), kind=kLoop, calls=%fused_computation.322 | loop fusion | flops 393216 | bytes 1306640 | tf_op jit(solution)/shard_map/mul | solution.py:87
  136.7 1.9 collective-permute-start.8
  138.6 6.3 %collective-permute-done.8 = f32[1,4,128,128]{3,2,1,0:T(8,128)S(1)} collective-permute-done((f32[1,4,128,128]{3,2,1,0:T(8,128)S(1)}, f32[1,4,128,128]{3,2,1,0:T(8,128)S(1)}, u32[]{:S(2)}, u32[]{:S(2)}) %collective-permute-start.8) | collective-permute-done | bytes 262176 | tf_op jit(solution)/shard_map/ppermute | solution.py:13
  146.9 5.8 %collective-permute-done.9 = f32[1,4,128,128]{3,2,1,0:T(8,128)S(1)} collective-permute-done((f32[1,4,128,128]{3,2,1,0:T(8,128)S(1)}, f32[1,4,128,128]{3,2,1,0:T(8,128)S(1)}, u32[]{:S(2)}, u32[]{:S(2)}) %collective-permute-start.9) | collective-permute-done | bytes 262176 | tf_op jit(solution)/shard_map/ppermute | solution.py:13
  152.7 2.9 %collective-permute-start.10 = (f32[1,4,128,128]{3,2,1,0:T(8,128)S(1)}, f32[1,4,128,128]{3,2,1,0:T(8,128)S(1)}, u32[]{:S(2)}, u32[]{:S(2)}) collective-permute-start(f32[1,4,128,128]{3,2,1,0:T(8,128)S(1)} %bitcast_select_fusion), channel_id=1, source_target_pairs={{0,4},{4,8},{8,12},{12,16},{16,20},{20,24},{24,28},{1,5},{5,9},{9,... | collective-permute-start | bytes 786440 | tf_op jit(solution)/shard_map/ppermute | solution.py:13
  155.7 6.2 %collective-permute-done.10 = f32[1,4,128,128]{3,2,1,0:T(8,128)S(1)} collective-permute-done((f32[1,4,128,128]{3,2,1,0:T(8,128)S(1)}, f32[1,4,128,128]{3,2,1,0:T(8,128)S(1)}, u32[]{:S(2)}, u32[]{:S(2)}) %collective-permute-start.10) | collective-permute-done | bytes 262176 | tf_op jit(solution)/shard_map/ppermute | solution.py:13
  162.5 2.7 %bitcast_multiply_fusion.5 = (f32[1,2,128,128]{3,2,1,0:T(8,128)S(1)}, f32[1,2,128,128]{3,2,1,0:T(8,128)S(1)}) fusion(pred[2,128,128]{2,1,0:T(8,128)(4,1)S(1)} %get-tuple-element.718, pred[2,128,128]{2,1,0:T(8,128)(4,1)S(1)} %get-tuple-element.717, pred[2,128,128]{2,1,0:T(8,128)(4,1)S(1)} %get-tuple-element.716, ...), kind=kLoop, calls=%fused_computation.321 | loop fusion | flops 393216 | bytes 1306640 | tf_op jit(solution)/shard_map/mul | solution.py:72
  166.0 2.7 %bitcast_multiply_fusion.4 = (f32[1,2,128,128]{3,2,1,0:T(8,128)S(1)}, f32[1,2,128,128]{3,2,1,0:T(8,128)S(1)}) fusion(pred[2,128,128]{2,1,0:T(8,128)(4,1)S(1)} %get-tuple-element.718, pred[2,128,128]{2,1,0:T(8,128)(4,1)S(1)} %get-tuple-element.717, pred[2,128,128]{2,1,0:T(8,128)(4,1)S(1)} %get-tuple-element.716, ...), kind=kLoop, calls=%fused_computation.320 | loop fusion | flops 393216 | bytes 1306640 | tf_op jit(solution)/shard_map/mul | solution.py:72
  169.4 2.7 %bitcast_multiply_fusion.3 = (f32[1,2,128,128]{3,2,1,0:T(8,128)S(1)}, f32[1,2,128,128]{3,2,1,0:T(8,128)S(1)}) fusion(pred[2,128,128]{2,1,0:T(8,128)(4,1)S(1)} %get-tuple-element.718, pred[2,128,128]{2,1,0:T(8,128)(4,1)S(1)} %get-tuple-element.717, pred[2,128,128]{2,1,0:T(8,128)(4,1)S(1)} %get-tuple-element.716, ...), kind=kLoop, calls=%fused_computation.319 | loop fusion | flops 393216 | bytes 1306640 | tf_op jit(solution)/shard_map/mul | solution.py:72
  175.6 9.1 %collective-permute-done.11 = f32[1,4,128,128]{3,2,1,0:T(8,128)S(1)} collective-permute-done((f32[1,4,128,128]{3,2,1,0:T(8,128)S(1)}, f32[1,4,128,128]{3,2,1,0:T(8,128)S(1)}, u32[]{:S(2)}, u32[]{:S(2)}) %collective-permute-start.11) | collective-permute-done | bytes 262176 | tf_op jit(solution)/shard_map/ppermute | solution.py:13
  184.9 1.9 collective-permute-start.12
  186.8 7.2 %collective-permute-done.12 = f32[1,4,128,128]{3,2,1,0:T(8,128)S(1)} collective-permute-done((f32[1,4,128,128]{3,2,1,0:T(8,128)S(1)}, f32[1,4,128,128]{3,2,1,0:T(8,128)S(1)}, u32[]{:S(2)}, u32[]{:S(2)}) %collective-permute-start.12) | collective-permute-done | bytes 262176 | tf_op jit(solution)/shard_map/ppermute | solution.py:13
  194.5 2.7 %bitcast_multiply_fusion.2 = (f32[1,2,128,128]{3,2,1,0:T(8,128)S(1)}, f32[1,2,128,128]{3,2,1,0:T(8,128)S(1)}) fusion(pred[2,128,128]{2,1,0:T(8,128)(4,1)S(1)} %get-tuple-element.718, pred[2,128,128]{2,1,0:T(8,128)(4,1)S(1)} %get-tuple-element.717, pred[2,128,128]{2,1,0:T(8,128)(4,1)S(1)} %get-tuple-element.716, ...), kind=kLoop, calls=%fused_computation.318 | loop fusion | flops 393216 | bytes 1306640 | tf_op jit(solution)/shard_map/mul | solution.py:87
  198.0 2.7 %bitcast_multiply_fusion.1 = (f32[1,2,128,128]{3,2,1,0:T(8,128)S(1)}, f32[1,2,128,128]{3,2,1,0:T(8,128)S(1)}) fusion(pred[2,128,128]{2,1,0:T(8,128)(4,1)S(1)} %get-tuple-element.718, pred[2,128,128]{2,1,0:T(8,128)(4,1)S(1)} %get-tuple-element.717, pred[2,128,128]{2,1,0:T(8,128)(4,1)S(1)} %get-tuple-element.716, ...), kind=kLoop, calls=%fused_computation.317 | loop fusion | flops 393216 | bytes 1306640 | tf_op jit(solution)/shard_map/mul | solution.py:87
  201.4 2.7 %bitcast_multiply_fusion = (f32[1,2,128,128]{3,2,1,0:T(8,128)S(1)}, f32[1,2,128,128]{3,2,1,0:T(8,128)S(1)}) fusion(pred[2,128,128]{2,1,0:T(8,128)(4,1)S(1)} %get-tuple-element.718, pred[2,128,128]{2,1,0:T(8,128)(4,1)S(1)} %get-tuple-element.717, pred[2,128,128]{2,1,0:T(8,128)(4,1)S(1)} %get-tuple-element.716, ...), kind=kLoop, calls=%fused_computation.316 | loop fusion | flops 393216 | bytes 1306640 | tf_op jit(solution)/shard_map/mul | solution.py:87
  206.9 6.3 %collective-permute-done.13 = f32[1,4,128,128]{3,2,1,0:T(8,128)S(1)} collective-permute-done((f32[1,4,128,128]{3,2,1,0:T(8,128)S(1)}, f32[1,4,128,128]{3,2,1,0:T(8,128)S(1)}, u32[]{:S(2)}, u32[]{:S(2)}) %collective-permute-start.13) | collective-permute-done | bytes 262176 | tf_op jit(solution)/shard_map/ppermute | solution.py:13
  (356 shorter events, 28.6 us)
Async XLA Ops:
  0.6 4.5 %copy-start.5 = (f32[4]{0:T(128)S(1)}, f32[4]{0:T(128)}, u32[]{:S(2)}) copy-start(f32[4]{0:T(128)} %param.122) | copy-start | bytes 52
  0.7 5.1 %copy-start.6 = (f32[4]{0:T(128)S(1)}, f32[4]{0:T(128)}, u32[]{:S(2)}) copy-start(f32[4]{0:T(128)} %param.123) | copy-start | bytes 52
  0.7 5.7 %copy-start.4 = (s32[2,128,128]{2,1,0:T(8,128)S(1)}, s32[2,128,128]{2,1,0:T(8,128)}, u32[]{:S(2)}) copy-start(s32[2,128,128]{2,1,0:T(8,128)} %param.119) | copy-start | bytes 393220
  1.7 17.5 %collective-permute-start = (f32[1,4,128,128]{3,2,1,0:T(8,128)S(1)}, f32[1,4,128,128]{3,2,1,0:T(8,128)S(1)}, u32[]{:S(2)}, u32[]{:S(2)}) collective-permute-start(f32[1,4,128,128]{3,2,1,0:T(8,128)S(1)} %multiply_bitcast_fusion), channel_id=1, source_target_pairs={{0,4},{4,8},{8,12},{12,16},{16,20},{20,24},{24,28},{1,5},{5,9},{9,... | collective-permute-start | bytes 786440 | tf_op jit(solution)/shard_map/ppermute | solution.py:13
  14.5 0.9 copy-start
  35.5 9.9 %copy-start.1 = (f32[1,1,4,128,128]{4,3,2,1,0:T(8,128)S(1)}, f32[1,1,4,128,128]{4,3,2,1,0:T(8,128)}, u32[]{:S(2)}) copy-start(f32[1,1,4,128,128]{4,3,2,1,0:T(8,128)} %param.120) | copy-start | bytes 786436
  35.6 9.8 %collective-permute-start.1 = (f32[1,4,128,128]{3,2,1,0:T(8,128)S(1)}, f32[1,4,128,128]{3,2,1,0:T(8,128)S(1)}, u32[]{:S(2)}, u32[]{:S(2)}) collective-permute-start(f32[1,4,128,128]{3,2,1,0:T(8,128)S(1)} %fusion.3), channel_id=1, source_target_pairs={{4,0},{8,4},{12,8},{16,12},{20,16},{24,20},{28,24},{5,1},{9,5},{13... | collective-permute-start | bytes 786440 | tf_op jit(solution)/shard_map/ppermute | solution.py:13
  45.4 9.7 %collective-permute-start.2 = (f32[1,4,128,128]{3,2,1,0:T(8,128)S(1)}, f32[1,4,128,128]{3,2,1,0:T(8,128)S(1)}, u32[]{:S(2)}, u32[]{:S(2)}) collective-permute-start(f32[1,4,128,128]{3,2,1,0:T(8,128)S(1)} %fusion.2), channel_id=1, source_target_pairs={{0,4},{4,8},{8,12},{12,16},{16,20},{20,24},{24,28},{1,5},{5,9},{9,... | collective-permute-start | bytes 786440 | tf_op jit(solution)/shard_map/ppermute | solution.py:13
  66.3 8.3 %collective-permute-start.3 = (f32[1,4,128,128]{3,2,1,0:T(8,128)S(1)}, f32[1,4,128,128]{3,2,1,0:T(8,128)S(1)}, u32[]{:S(2)}, u32[]{:S(2)}) collective-permute-start(f32[1,4,128,128]{3,2,1,0:T(8,128)S(1)} %pad_maximum_fusion), channel_id=1, source_target_pairs={{4,0},{8,4},{12,8},{16,12},{20,16},{24,20},{28,24},{5,1},{9,5},{13... | collective-permute-start | bytes 786440 | tf_op jit(solution)/shard_map/ppermute | solution.py:13
  74.5 7.9 %copy-start.2 = (f32[2,1,4,128,128]{4,3,2,1,0:T(8,128)S(1)}, f32[2,1,4,128,128]{4,3,2,1,0:T(8,128)}, u32[]{:S(2)}) copy-start(f32[2,1,4,128,128]{4,3,2,1,0:T(8,128)} %param.121) | copy-start | bytes 1572868
  74.6 7.8 %collective-permute-start.4 = (f32[1,4,128,128]{3,2,1,0:T(8,128)S(1)}, f32[1,4,128,128]{3,2,1,0:T(8,128)S(1)}, u32[]{:S(2)}, u32[]{:S(2)}) collective-permute-start(f32[1,4,128,128]{3,2,1,0:T(8,128)S(1)} %fusion.6), channel_id=1, source_target_pairs={{0,1},{1,2},{2,3},{4,5},{5,6},{6,7},{8,9},{9,10},{10,11},{12,13},{... | collective-permute-start | bytes 786440 | tf_op jit(solution)/shard_map/ppermute | solution.py:13
  82.5 9.2 %collective-permute-start.5 = (f32[1,4,128,128]{3,2,1,0:T(8,128)S(1)}, f32[1,4,128,128]{3,2,1,0:T(8,128)S(1)}, u32[]{:S(2)}, u32[]{:S(2)}) collective-permute-start(f32[1,4,128,128]{3,2,1,0:T(8,128)S(1)} %bitcast_select_fusion.1), channel_id=1, source_target_pairs={{0,4},{4,8},{8,12},{12,16},{16,20},{20,24},{24,28},{1,5},{5,9},{9,... | collective-permute-start | bytes 786440 | tf_op jit(solution)/shard_map/ppermute | solution.py:13
  105.3 11.1 %collective-permute-start.6 = (f32[1,4,128,128]{3,2,1,0:T(8,128)S(1)}, f32[1,4,128,128]{3,2,1,0:T(8,128)S(1)}, u32[]{:S(2)}, u32[]{:S(2)}) collective-permute-start(f32[1,4,128,128]{3,2,1,0:T(8,128)S(1)} %fusion.10), channel_id=1, source_target_pairs={{4,0},{8,4},{12,8},{16,12},{20,16},{24,20},{28,24},{5,1},{9,5},{13... | collective-permute-start | bytes 786440 | tf_op jit(solution)/shard_map/ppermute | solution.py:13
  116.5 9.2 %collective-permute-start.7 = (f32[1,4,128,128]{3,2,1,0:T(8,128)S(1)}, f32[1,4,128,128]{3,2,1,0:T(8,128)S(1)}, u32[]{:S(2)}, u32[]{:S(2)}) collective-permute-start(f32[1,4,128,128]{3,2,1,0:T(8,128)S(1)} %fusion.9), channel_id=1, source_target_pairs={{0,4},{4,8},{8,12},{12,16},{16,20},{20,24},{24,28},{1,5},{5,9},{9,... | collective-permute-start | bytes 786440 | tf_op jit(solution)/shard_map/ppermute | solution.py:13
  136.7 8.3 %collective-permute-start.8 = (f32[1,4,128,128]{3,2,1,0:T(8,128)S(1)}, f32[1,4,128,128]{3,2,1,0:T(8,128)S(1)}, u32[]{:S(2)}, u32[]{:S(2)}) collective-permute-start(f32[1,4,128,128]{3,2,1,0:T(8,128)S(1)} %pad_maximum_fusion.1), channel_id=1, source_target_pairs={{4,0},{8,4},{12,8},{16,12},{20,16},{24,20},{28,24},{5,1},{9,5},{13... | collective-permute-start | bytes 786440 | tf_op jit(solution)/shard_map/ppermute | solution.py:13
  145.0 7.7 %collective-permute-start.9 = (f32[1,4,128,128]{3,2,1,0:T(8,128)S(1)}, f32[1,4,128,128]{3,2,1,0:T(8,128)S(1)}, u32[]{:S(2)}, u32[]{:S(2)}) collective-permute-start(f32[1,4,128,128]{3,2,1,0:T(8,128)S(1)} %fusion.13), channel_id=1, source_target_pairs={{0,1},{1,2},{2,3},{4,5},{5,6},{6,7},{8,9},{9,10},{10,11},{12,13},{... | collective-permute-start | bytes 786440 | tf_op jit(solution)/shard_map/ppermute | solution.py:13
  152.7 9.2 %collective-permute-start.10 = (f32[1,4,128,128]{3,2,1,0:T(8,128)S(1)}, f32[1,4,128,128]{3,2,1,0:T(8,128)S(1)}, u32[]{:S(2)}, u32[]{:S(2)}) collective-permute-start(f32[1,4,128,128]{3,2,1,0:T(8,128)S(1)} %bitcast_select_fusion), channel_id=1, source_target_pairs={{0,4},{4,8},{8,12},{12,16},{16,20},{20,24},{24,28},{1,5},{5,9},{9,... | collective-permute-start | bytes 786440 | tf_op jit(solution)/shard_map/ppermute | solution.py:13
  173.0 0.7 copy-start.3
  173.7 11.1 %collective-permute-start.11 = (f32[1,4,128,128]{3,2,1,0:T(8,128)S(1)}, f32[1,4,128,128]{3,2,1,0:T(8,128)S(1)}, u32[]{:S(2)}, u32[]{:S(2)}) collective-permute-start(f32[1,4,128,128]{3,2,1,0:T(8,128)S(1)} %fusion.17), channel_id=1, source_target_pairs={{4,0},{8,4},{12,8},{16,12},{20,16},{24,20},{28,24},{5,1},{9,5},{13... | collective-permute-start | bytes 786440 | tf_op jit(solution)/shard_map/ppermute | solution.py:13
  184.9 9.2 %collective-permute-start.12 = (f32[1,4,128,128]{3,2,1,0:T(8,128)S(1)}, f32[1,4,128,128]{3,2,1,0:T(8,128)S(1)}, u32[]{:S(2)}, u32[]{:S(2)}) collective-permute-start(f32[1,4,128,128]{3,2,1,0:T(8,128)S(1)} %fusion.16), channel_id=1, source_target_pairs={{0,4},{4,8},{8,12},{12,16},{16,20},{20,24},{24,28},{1,5},{5,9},{9,... | collective-permute-start | bytes 786440 | tf_op jit(solution)/shard_map/ppermute | solution.py:13
  205.0 8.3 %collective-permute-start.13 = (f32[1,4,128,128]{3,2,1,0:T(8,128)S(1)}, f32[1,4,128,128]{3,2,1,0:T(8,128)S(1)}, u32[]{:S(2)}, u32[]{:S(2)}) collective-permute-start(f32[1,4,128,128]{3,2,1,0:T(8,128)S(1)} %pad_maximum_fusion.2), channel_id=1, source_target_pairs={{4,0},{8,4},{12,8},{16,12},{20,16},{24,20},{28,24},{5,1},{9,5},{13... | collective-permute-start | bytes 786440 | tf_op jit(solution)/shard_map/ppermute | solution.py:13
where the time goes:
time: 215 us; the launch traced here: 214 us
  other arithmetic  85.5 us (40%)
  waiting for transfers between devices  83.1 us (39%)
  starting transfers between devices  38.8 us (18%)
  local copies, waits for them, and re-layouts  3.7 us (2%)
  between operations  2.94 us (1%)
    ppermute x14, waiting for transfers between devices, shifted(): lax.ppermute(value, axis, [(source, source + steps) for source in range(l...  83.1 us
    ppermute x14, starting transfers between devices, shifted(): lax.ppermute(value, axis, [(source, source + steps) for source in range(l...  38.8 us
    mul x11, other arithmetic, neumann(): rhs = capacity * psi  31.7 us
    mul x11, other arithmetic, dirichlet(): rhs = capacity * state  29.4 us
    div x52, other arithmetic, relax(): value = (rhs + near) / diag  8.49 us
    mul x68, other arithmetic, relax(): face_z * value[:, :, :, :-1]  6.79 us
  transfers between devices with their start and end apart: 14, of which 13 were waited for; matrix products, arithmetic and copies ran while one was open for 6% of the time, Pallas kernels for 0%

commit v1 on v0

v1 whole, which is shorter than its diff:
```python
import functools

import jax
import jax.numpy as jnp
from jax import lax
from jax.experimental import pallas as pl
from jax.experimental.pallas import tpu as pltpu
from jax.sharding import PartitionSpec as P

SWEEPS = 3
AXES = ("sub", "iter")
F32 = jnp.float32
PAD = 8
SPLIT = 1
LIMIT = 8 << 20


def vmem(shape, dtype=F32):
    return pltpu.VMEM(shape, dtype)


def near(value):
    return pltpu.with_memory_space_constraint(value, pltpu.VMEM)


def harmonic(first, second):
    return 2.0 * first * second / (first + second)


class Layout:
    def __init__(self, slabs, groups):
        assert slabs % 2 == 0 and groups % 2 == 0
        self.slabs, self.groups = slabs, groups
        every = [(s, p) for s in range(slabs) for p in range(groups)]
        at = self.at
        self.core = [(at(s, p), at(s ^ 1, p)) for s, p in every]
        self.chip = []
        for s, p in every:
            t = s + 1 if s % 2 else s - 1
            self.chip.append((at(s, p), at(t, p) if 0 <= t < slabs else at(s, (p + 2) % groups)))
        self.field = [(at(s, p), at(s, (p - 1) % groups)) for s, p in every]
        self.enter = []
        self.guess = []
        for s, g in every:
            here = s * groups + g
            if s % 2 != g % 2:
                there = (s ^ 1) * groups + (g ^ 1)
            else:
                there = s * groups + (g + 2) % groups
            self.enter.append((here, there))
            self.guess.append((here, (s ^ 1) * groups + g))

    def at(self, s, p):
        return (2 * (s // 2) + p % 2) * self.groups + 2 * (p // 2) + s % 2

    def home(self, ticks):
        every = [(s, p) for s in range(self.slabs) for p in range(self.groups)]
        return [(self.at(s, p), s * self.groups + (p + ticks - 1) % self.groups) for s, p in every]


def place():
    sub, it = lax.axis_index("sub"), lax.axis_index("iter")
    parity = lax.rem(it, 2)
    slab = 2 * (sub // 2) + parity
    position = 2 * (it // 2) + lax.rem(sub, 2)
    return parity, slab, position


def has_far():
    parity, slab, _ = place()
    last = lax.axis_size("sub") - 1
    return jnp.logical_not(jnp.where(parity == 0, slab == 0, slab == last))


def stays():
    return lax.rem(lax.axis_index("sub"), 2) == lax.rem(lax.axis_index("iter"), 2)


def flipped(plane, planes, parity):
    return plane + parity * (planes - 1 - 2 * plane)


def row_cap(p):
    return 5 * p


def row_face(planes, f):
    return 5 * planes + 2 * f


def row_end(planes, role_a):
    return 5 * planes + 2 * (planes - 1) + role_a


def rows(planes):
    return 5 * planes + 2 * (planes - 1) + 2


def setup_kernel(cond_ref, cap_ref, mine_ref, other_ref, dir_ref, neu_ref, end_ref):
    planes, ny, nz = mine_ref.shape
    parity, _, _ = place()
    keep = stays()
    far = has_far()
    row = lax.broadcasted_iota(jnp.int32, (ny, nz), 0)
    col = lax.broadcasted_iota(jnp.int32, (ny, nz), 1)
    ks, cs = [], []
    for p in range(planes):
        at = flipped(p, planes, parity)
        label = jnp.where(keep, mine_ref[at], other_ref[at])
        k = jnp.zeros((ny, nz), F32)
        c = jnp.zeros((ny, nz), F32)
        for cls in range(cond_ref.shape[0]):
            hit = label == cls
            k = jnp.where(hit, cond_ref[cls], k)
            c = jnp.where(hit, cap_ref[cls], c)
        ks.append(k)
        cs.append(c)
    faces = [harmonic(ks[f], ks[f + 1]) for f in range(planes - 1)]
    end_ref[0] = 2.0 * ks[0]
    end_ref[1] = 2.0 * ks[-1]
    for p in range(planes):
        k = ks[p]
        down = harmonic(k, pltpu.roll(k, ny - 1, 0))
        up = pltpu.roll(down, 1, 0)
        right = harmonic(k, pltpu.roll(k, nz - 1, 1))
        left = pltpu.roll(right, 1, 1)
        edge = 2.0 * k
        total = cs[p]
        total = total + ((faces[p - 1] if p else edge) + (faces[p] if p < planes - 1 else edge))
        total = total + (jnp.where(row == 0, edge, up) + jnp.where(row == ny - 1, edge, down))
        total = total + (jnp.where(col == 0, edge, left) + jnp.where(col == nz - 1, edge, right))
        up = jnp.where(row == 0, 0.0, up)
        down = jnp.where(row == ny - 1, 0.0, down)
        left = jnp.where(col == 0, 0.0, left)
        right = jnp.where(col == nz - 1, 0.0, right)
        free = total
        if p == 0:
            free = free - jnp.where(far, edge, 0.0)
        if p == planes - 1:
            free = free - edge
        for out, diag in ((dir_ref, total), (neu_ref, free)):
            inverse = 1.0 / diag
            for n, value in enumerate((cs[p], up, down, left, right)):
                out[row_cap(p) + n] = value * inverse
            if p < planes - 1:
                out[row_face(planes, p)] = faces[p] * inverse
            if p:
                out[row_face(planes, p - 1) + 1] = faces[p - 1] * inverse
            weight = edge * inverse if out is dir_ref else inverse
            if p == 0:
                out[row_end(planes, 0)] = weight
            if p == planes - 1:
                out[row_end(planes, 1)] = weight


def clear_pads(refs):
    for ref in refs:
        planes, tall, nz = ref.shape
        for p in range(planes):
            ref[p, 0:PAD, :] = jnp.zeros((PAD, nz), F32)
            ref[p, tall - PAD : tall, :] = jnp.zeros((PAD, nz), F32)


def sweep(coef, source, target, rhs):
    planes, tall, nz = source.shape
    for r in range(0, tall - 2 * PAD, 8):
        here = slice(r, r + 8)
        xs = [source[p, PAD + r : PAD + r + 8, :] for p in range(planes)]
        for p in range(planes):
            x = xs[p]
            base = row_cap(p)
            value = rhs(p, here, x)
            if p < planes - 1:
                value = value + coef[row_face(planes, p), here, :] * xs[p + 1]
            if p:
                value = value + coef[row_face(planes, p - 1) + 1, here, :] * xs[p - 1]
            side = coef[base + 1, here, :] * source[p, PAD + r - 1 : PAD + r + 7, :]
            side = side + coef[base + 2, here, :] * source[p, PAD + r + 1 : PAD + r + 9, :]
            value = value + side
            side = coef[base + 3, here, :] * pltpu.roll(x, 1, 1)
            side = side + coef[base + 4, here, :] * pltpu.roll(x, nz - 1, 1)
            target(p, here, value + side)


def padded(here):
    return slice(here.start + PAD, here.stop + PAD)


def solve(coef, buffers, hold, first_rhs, final, known_zero=False):
    planes, tall, nz = buffers[0].shape

    for n in range(SWEEPS):
        source, target = buffers

        def rhs(p, here, x):
            if n:
                return hold[p, here, :]
            value = first_rhs(p, here, x)
            hold[p, here, :] = value
            return value

        def put(p, here, value):
            target[p, padded(here), :] = value
            if n == SWEEPS - 1:
                final(p, here, value)

        if n == 0 and known_zero:
            for r in range(0, tall - 2 * PAD, 8):
                for p in range(planes):
                    here = slice(r, r + 8)
                    put(p, here, rhs(p, here, None))
        else:
            sweep(coef, source, put, rhs)
        buffers = buffers[::-1]
    return buffers


def dirichlet_kernel(lo, start, enter, fresh, out_native, *refs):
    refs = list(refs)
    take = lambda n: [refs.pop(0) for _ in range(n)]
    coef, end = take(2)
    parity, _, position = place()
    far = has_far()
    if enter:
        keep = stays()
        mine, other = take(2)
    else:
        (field,) = take(1)
    if start:
        held, from_core, from_chip = take(3)
    else:
        old_a, old_b, psi_a, psi_b, got_a, got_b, ng, gy = take(8)
    out_field, out_qa, out_qb, out_ha, out_hb, va, vb, hold = take(8)
    planes = va.shape[0]
    steps = out_qa.shape[0]
    ny = out_qa.shape[1]
    clear_pads((va, vb))
    for p in range(planes):
        if enter:
            at = flipped(p, planes, parity)
            value = jnp.where(keep, mine[0, at], other[0, at])
        else:
            value = field[p]
        va[p, PAD : PAD + ny, :] = value
    for n in range(steps):
        if start:
            h_a = jnp.where(parity == 0, held[n], from_core[n])
            h_b = jnp.where(parity == 0, from_chip[n], held[n])
        else:
            h_a = old_a[n] + 0.25 * (psi_a[n] + got_a[n])
            h_b = old_b[n] + 0.25 * (psi_b[n] + got_b[n])
            groups = lax.axis_size("iter")
            begins = (groups - fresh) % groups
            new = position == begins
            local, crossed = ng[fresh - 1, 0, lo + n], gy[lo + n]
            near_a, near_b = (crossed, local) if begins % 2 else (local, crossed)
            h_a = jnp.where(new, near_a, h_a)
            h_b = jnp.where(new, jnp.where(parity == 1, near_b, got_b[n]), h_b)
        out_ha[n] = h_a
        out_hb[n] = jnp.where(far, h_b, 0.0)
    buffers = [va, vb]
    for n in range(steps):

        def first_rhs(p, here, x):
            value = coef[row_cap(p), here, :] * x
            if p == 0:
                value = value + coef[row_end(planes, 0), here, :] * out_hb[n, here, :]
            if p == planes - 1:
                value = value + coef[row_end(planes, 1), here, :] * out_ha[n, here, :]
            return value

        def final(p, here, value):
            if p == 0:
                out_qb[n, here, :] = end[0, here, :] * (value - out_hb[n, here, :])
            if p == planes - 1:
                out_qa[n, here, :] = end[1, here, :] * (value - out_ha[n, here, :])

        buffers = solve(coef, buffers, hold, first_rhs, final)
    for p in range(planes):
        value = buffers[0][p, PAD : PAD + ny, :]
        if out_native:
            out_field[flipped(p, planes, parity)] = value
        else:
            out_field[p] = value


def neumann_kernel(lo, first, fresh, *refs):
    refs = list(refs)
    take = lambda n: [refs.pop(0) for _ in range(n)]
    (coef,) = take(1)
    parity, _, position = place()
    far = has_far()
    q_a, q_b, got_a, got_b = take(4)
    if not first:
        (state,) = take(1)
    if fresh:
        ng, gy = take(2)
    out_state, out_a, out_b, va, vb, hold = take(6)
    planes = va.shape[0]
    steps, ny, nz = out_a.shape
    clear_pads((va, vb))
    if not first:
        for p in range(planes):
            va[p, PAD : PAD + ny, :] = state[p]
    buffers = [va, vb]
    for n in range(steps):
        zero = first and n == 0

        def first_rhs(p, here, x):
            value = jnp.zeros((8, nz), F32) if zero else coef[row_cap(p), here, :] * x
            if p == 0:
                jump = jnp.where(far, q_b[n, here, :] + got_b[n, here, :], 0.0)
                value = value + coef[row_end(planes, 0), here, :] * jump
            if p == planes - 1:
                jump = q_a[n, here, :] + got_a[n, here, :]
                value = value + coef[row_end(planes, 1), here, :] * jump
            return value

        def final(p, here, value):
            if p == 0:
                out_b[n, here, :] = value
            if p == planes - 1:
                out_a[n, here, :] = value

        buffers = solve(coef, buffers, hold, first_rhs, final, known_zero=zero)
    for p in range(planes):
        out_state[p] = buffers[0][p, PAD : PAD + ny, :]
    if fresh:
        groups = lax.axis_size("iter")
        begins = (groups - fresh) % groups

        @pl.when(position == begins)
        def _():
            for n in range(steps):
                out_b[n] = ng[fresh - 1, 0, lo + n] if begins % 2 else gy[lo + n]


def correct_kernel(h_a, h_b, psi_a, psi_b, got_a, got_b, out):
    parity, _, _ = place()
    far = has_far()

    @pl.when(parity == 0)
    def _():
        out[...] = h_a[...] + 0.25 * (psi_a[...] + got_a[...])

    @pl.when(parity == 1)
    def _():
        out[...] = jnp.where(far, h_b[...] + 0.25 * (psi_b[...] + got_b[...]), 0.0)


def hold_kernel(mine, other, out):
    keep = stays()
    out[...] = jnp.where(keep, mine[0, 0], other[0, 0])


def run(kernel, outs, args, scratch=(), name=None, smem=0):
    specs = [pl.BlockSpec(memory_space=pltpu.SMEM)] * smem
    specs += [pl.BlockSpec(memory_space=pltpu.VMEM)] * (len(args) - smem)
    many = isinstance(outs, tuple)
    return pl.pallas_call(
        kernel,
        out_shape=outs,
        in_specs=specs,
        out_specs=tuple([pl.BlockSpec(memory_space=pltpu.VMEM)] * len(outs)) if many else specs[-1],
        scratch_shapes=list(scratch),
        compiler_params=pltpu.CompilerParams(vmem_limit_bytes=LIMIT),
        name=name,
    )(*args[:smem], *[near(a) for a in args[smem:]])


def local(layout, fields, labels, traces, new_guess, cond_table, cap_table):
    move = lambda value, pairs: lax.ppermute(value, AXES, pairs)
    planes, ny, nz = labels.shape
    steps = traces.shape[2]
    ticks = new_guess.shape[0] + 1
    groups = layout.groups
    odd = lax.rem(lax.axis_index("sub"), 2)
    size = max(1, steps // SPLIT)
    chunks = [(lo, min(lo + size, steps)) for lo in range(0, steps, size)]
    scratch = [vmem((planes, ny + 2 * PAD, nz))] * 2 + [vmem((planes, ny, nz))]

    got_traces = move(traces, layout.enter)
    got_labels = move(labels, layout.enter)
    got_fields = move(fields, layout.enter)
    held = run(hold_kernel, vmem((steps, ny, nz)), [traces, got_traces], name="held")
    from_core = move(held, layout.core)
    from_chip = move(held, layout.chip)
    count = rows(planes)
    dir_coef, neu_coef, end = run(
        setup_kernel,
        (vmem((count, ny, nz)), vmem((count, ny, nz)), vmem((2, ny, nz))),
        [cond_table, cap_table, labels, got_labels],
        name="setup",
        smem=2,
    )

    starts = {t: (groups - t) % groups for t in range(1, ticks)}
    odds = [t for t in starts if starts[t] % 2]
    evens = [t for t in starts if starts[t] % 2 == 0]
    crossed = {}
    for n in range(max(len(odds), len(evens))):
        ours = odds[n] if n < len(odds) else evens[n]
        theirs = evens[n] if n < len(evens) else odds[n]
        message = jnp.where(odd == 0, new_guess[ours - 1, 0], new_guess[theirs - 1, 0])
        arrived = move(message, layout.guess)
        crossed[ours] = crossed[theirs] = arrived

    field = None
    state = None
    waves = None
    for tick in range(ticks):
        last = tick == ticks - 1
        sent = []
        for lo, hi in chunks:
            m = hi - lo
            args = [dir_coef, end]
            enter = tick == 0 and lo == 0
            args += [fields, got_fields] if enter else [field]
            if tick == 0:
                args += [a[lo:hi] for a in (held, from_core, from_chip)] if len(chunks) > 1 else [held, from_core, from_chip]
            else:
                args += [*waves[lo], new_guess, crossed[tick]]
            plane = vmem((m, ny, nz))
            field, q_a, q_b, h_a, h_b = run(
                functools.partial(dirichlet_kernel, lo, tick == 0, enter, tick, last and hi == steps),
                (vmem((planes, ny, nz)), plane, plane, plane, plane),
                args,
                scratch,
                name=f"dirichlet_{tick}_{lo}",
            )
            sent.append((q_a, q_b, move(q_a, layout.core), move(q_b, layout.chip), h_a, h_b))
        field = move(field[None] if last else field, layout.home(ticks) if last else layout.field)
        fresh = 0 if last else tick + 1
        waves = {}
        state = None
        ends = []
        for (lo, hi), (q_a, q_b, got_a, got_b, h_a, h_b) in zip(chunks, sent):
            m = hi - lo
            args = [neu_coef, q_a, q_b, got_a, got_b]
            if lo:
                args.append(state)
            if fresh:
                args += [new_guess, crossed[fresh]]
            plane = vmem((m, ny, nz))
            state, psi_a, psi_b = run(
                functools.partial(neumann_kernel, lo, lo == 0, fresh),
                (vmem((planes, ny, nz)), plane, plane),
                args,
                scratch,
                name=f"neumann_{tick}_{lo}",
            )
            in_a = move(psi_a, layout.core)
            in_b = move(psi_b, layout.chip)
            waves[lo] = (h_a, h_b, psi_a, psi_b, in_a, in_b)
            if last:
                done = run(correct_kernel, plane, list(waves[lo]), name=f"correct_{lo}")
                ends.append(move(done, layout.home(ticks)))
    corrected = ends[0] if len(ends) == 1 else jnp.concatenate(ends, axis=0)
    return field, corrected[None, None]


def solution(mesh):
    layout = Layout(mesh.shape["sub"], mesh.shape["iter"])
    return jax.shard_map(
        functools.partial(local, layout),
        mesh=mesh,
        in_specs=(
            P("iter", "sub", None, None),
            P("sub", None, None),
            P("iter", "sub", None, None, None),
            P(None, "sub", None, None, None),
            P(),
            P(),
        ),
        out_specs=(P("iter", "sub", None, None), P("iter", "sub", None, None, None)),
        check_vma=False,
    )
```

time: 215 us -> 84.5 us (0.39)
  the two profiles are of different devices: /device:TPU:10 before, /device:TPU:1 now
where the time goes in v1:
time: 84.5 us; the launch traced here: 84.4 us
  waiting for transfers between devices  50 us (59%)
  starting transfers between devices  22.1 us (26%)
  Pallas kernels  9.19 us (11%)
  local copies, waits for them, and re-layouts  2.33 us (3%)
    ppermute x22, waiting for transfers between devices, local(): move = lambda value, pairs: lax.ppermute(value, AXES, pairs)  50 us
    ppermute x22, starting transfers between devices, local(): move = lambda value, pairs: lax.ppermute(value, AXES, pairs)  22.1 us
    pallas_call x9, Pallas kernels, run(): pl.pallas_call(kernel, out_shape=outs, in_specs=specs, out_specs=tuple([p...  9.19 us
    unnamed x14, local copies, waits for them, and re-layouts  2.33 us
  transfers between devices with their start and end apart: 22, of which 14 were waited for; matrix products, arithmetic and copies ran while one was open for 0% of the time, Pallas kernels for 2%

profile of v1, /device:TPU:1, one launch (start us, length us, event | category | flops | bytes accessed | tf_op | source)
XLA Modules:
  0.0 84.4 jit_solution(12875529946555633209)
XLA Ops:
  0.6 2.7 %collective-permute-start.2 = (f32[1,1,4,128,128]{4,3,2,1,0:T(8,128)}, f32[1,1,4,128,128]{4,3,2,1,0:T(8,128)S(1)}, u32[]{:S(2)}, u32[]{:S(2)}) collective-permute-start(f32[1,1,4,128,128]{4,3,2,1,0:T(8,128)} %mine.1), channel_id=1, source_target_pairs={{0,2},{1,4},{2,0},{3,6},{4,1},{5,7},{6,3},{7,5},{8,10},{9,12},{10,... | collective-permute-start | bytes 786440 | tf_op jit(solution)/shard_map/ppermute | solution.py:372
  3.3 4.5 %collective-permute-done.2.other = f32[1,1,4,128,128]{4,3,2,1,0:T(8,128)S(1)} collective-permute-done((f32[1,1,4,128,128]{4,3,2,1,0:T(8,128)}, f32[1,1,4,128,128]{4,3,2,1,0:T(8,128)S(1)}, u32[]{:S(2)}, u32[]{:S(2)}) %collective-permute-start.2) | collective-permute-done | bytes 262176 | tf_op jit(solution)/shard_map/ppermute | solution.py:372
  7.9 0.9 %copy-done.1 = f32[1,1,4,128,128]{4,3,2,1,0:T(8,128)S(1)} copy-done((f32[1,1,4,128,128]{4,3,2,1,0:T(8,128)S(1)}, f32[1,1,4,128,128]{4,3,2,1,0:T(8,128)}, u32[]{:S(2)}) %copy-start.1) | copy-done | bytes 262168
  8.9 2.2 %collective-permute-start.4 = (f32[4,128,128]{2,1,0:T(8,128)S(1)}, f32[4,128,128]{2,1,0:T(8,128)S(1)}, u32[]{:S(2)}, u32[]{:S(2)}) collective-permute-start(f32[4,128,128]{2,1,0:T(8,128)S(1)} %held.1.refs_4_), channel_id=1, source_target_pairs={{0,2},{4,6},{2,0},{6,4},{1,8},{5,12},{3,10},{7,14},{8,1},{12,5},{1... | collective-permute-start | bytes 786440 | tf_op jit(solution)/shard_map/ppermute | solution.py:372
  11.0 0.3 collective-permute-start.3
  11.3 0.8 collective-permute-start.1
  12.1 1.0 %collective-permute-start = (s32[2,128,128]{2,1,0:T(8,128)S(1)}, s32[2,128,128]{2,1,0:T(8,128)S(1)}, u32[]{:S(2)}, u32[]{:S(2)}) collective-permute-start(s32[2,128,128]{2,1,0:T(8,128)S(1)} %copy-done.3), channel_id=1, source_target_pairs={{0,2},{1,4},{2,0},{3,6},{4,1},{5,7},{6,3},{7,5},{8,10},{9,12},{10,... | collective-permute-start | bytes 393224 | tf_op jit(solution)/shard_map/ppermute | solution.py:372
  13.1 0.5 collective-permute-start.8
  13.6 5.1 %collective-permute-done.other_ref = s32[2,128,128]{2,1,0:T(8,128)S(1)} collective-permute-done((s32[2,128,128]{2,1,0:T(8,128)S(1)}, s32[2,128,128]{2,1,0:T(8,128)S(1)}, u32[]{:S(2)}, u32[]{:S(2)}) %collective-permute-start) | collective-permute-done | bytes 131104 | tf_op jit(solution)/shard_map/ppermute | solution.py:372
  18.7 0.9 %setup.1 = (f32[14,128,128]{2,1,0:T(8,128)S(1)}, f32[14,128,128]{2,1,0:T(8,128)S(1)}, f32[2,128,128]{2,1,0:T(8,128)S(1)}) custom-call(f32[4]{0:T(128)S(1)} %copy-done.4, f32[4]{0:T(128)S(1)} %copy-done.5, s32[2,128,128]{2,1,0:T(8,128)S(1)} %copy-done.3, s32[2,128,128]{2,1,0:T(8,128)S(1)} %collective-permute-done.other_ref), custom_call_target="tpu_custom_call" | custom-call | tf_op jit(solution)/shard_map/setup/pallas_call | solution.py:360
  19.6 0.0 collective-permute-done.1.refs_3_
  19.6 1.0 %dirichlet_0_0.1 = (f32[2,128,128]{2,1,0:T(8,128)S(1)}, f32[4,128,128]{2,1,0:T(8,128)S(1)}, f32[4,128,128]{2,1,0:T(8,128)S(1)}, f32[4,128,128]{2,1,0:T(8,128)S(1)}, f32[4,128,128]{2,1,0:T(8,128)S(1)}) custom-call(f32[14,128,128]{2,1,0:T(8,128)S(1)} %get-tuple-element.26.refs_0_, f32[2,128,128]{2,1,0:T(8,128)S(1)} %get-tuple-element.27.refs_1_, ...), custom_call_target="tpu_custom_call" | custom-call | tf_op jit(solution)/shard_map/dirichlet_0_0/pallas_call | solution.py:360
  20.6 0.1 collective-permute-start.6
  20.7 1.4 %collective-permute-start.7 = (f32[4,128,128]{2,1,0:T(8,128)S(1)}, f32[4,128,128]{2,1,0:T(8,128)S(1)}, u32[]{:S(2)}, u32[]{:S(2)}) collective-permute-start(f32[4,128,128]{2,1,0:T(8,128)S(1)} %get-tuple-element.33.refs_2_), channel_id=1, source_target_pairs={{0,2},{4,6},{2,0},{6,4},{1,8},{5,12},{3,10},{7,14},{8,1},{12,5},{1... | collective-permute-start | bytes 786440 | tf_op jit(solution)/shard_map/ppermute | solution.py:372
  22.1 0.0 collective-permute-done.8.refs_6_.refs_10_
  22.1 0.1 collective-permute-done.6.refs_3_
  22.2 4.6 %collective-permute-done.7.refs_4_ = f32[4,128,128]{2,1,0:T(8,128)S(1)} collective-permute-done((f32[4,128,128]{2,1,0:T(8,128)S(1)}, f32[4,128,128]{2,1,0:T(8,128)S(1)}, u32[]{:S(2)}, u32[]{:S(2)}) %collective-permute-start.7) | collective-permute-done | bytes 262176 | tf_op jit(solution)/shard_map/ppermute | solution.py:372
  26.9 1.7 %neumann_0_0.1 = (f32[2,128,128]{2,1,0:T(8,128)}, f32[4,128,128]{2,1,0:T(8,128)S(1)}, f32[4,128,128]{2,1,0:T(8,128)S(1)}) custom-call(f32[14,128,128]{2,1,0:T(8,128)S(1)} %get-tuple-element.31.refs_0_, f32[4,128,128]{2,1,0:T(8,128)S(1)} %get-tuple-element.32.refs_1_, f32[4,128,128]{2,1,0:T(8,128)S(1)} %get-tuple-element.33.refs_2_, ...), custom_call_target="tpu_custom_call" | custom-call | tf_op jit(solution)/shard_map/neumann_0_0/pallas_call | solution.py:360
  28.6 0.7 collective-permute-start.9
  29.3 0.4 collective-permute-start.10
  29.7 1.2 %collective-permute-start.5 = (f32[2,128,128]{2,1,0:T(8,128)S(1)}, f32[2,128,128]{2,1,0:T(8,128)S(1)}, u32[]{:S(2)}, u32[]{:S(2)}) collective-permute-start(f32[2,128,128]{2,1,0:T(8,128)S(1)} %get-tuple-element.28), channel_id=1, source_target_pairs={{0,6},{4,0},{2,4},{6,2},{1,7},{5,1},{3,5},{7,3},{8,14},{12,8},{10,... | collective-permute-start | bytes 393224 | tf_op jit(solution)/shard_map/ppermute | solution.py:372
  30.8 3.1 %collective-permute-done.5.refs_2_ = f32[2,128,128]{2,1,0:T(8,128)S(1)} collective-permute-done((f32[2,128,128]{2,1,0:T(8,128)S(1)}, f32[2,128,128]{2,1,0:T(8,128)S(1)}, u32[]{:S(2)}, u32[]{:S(2)}) %collective-permute-start.5) | collective-permute-done | bytes 131104 | tf_op jit(solution)/shard_map/ppermute | solution.py:372
  34.0 1.4 %collective-permute-done.10.refs_8_ = f32[4,128,128]{2,1,0:T(8,128)S(1)} collective-permute-done((f32[4,128,128]{2,1,0:T(8,128)S(1)}, f32[4,128,128]{2,1,0:T(8,128)S(1)}, u32[]{:S(2)}, u32[]{:S(2)}) %collective-permute-start.10) | collective-permute-done | bytes 262176 | tf_op jit(solution)/shard_map/ppermute | solution.py:372
  35.4 1.1 %dirichlet_1_0.1 = (f32[2,128,128]{2,1,0:T(8,128)S(1)}, f32[4,128,128]{2,1,0:T(8,128)S(1)}, f32[4,128,128]{2,1,0:T(8,128)S(1)}, f32[4,128,128]{2,1,0:T(8,128)S(1)}, f32[4,128,128]{2,1,0:T(8,128)S(1)}) custom-call(f32[14,128,128]{2,1,0:T(8,128)S(1)} %get-tuple-element.26.refs_0_, f32[2,128,128]{2,1,0:T(8,128)S(1)} %get-tuple-element.27.refs_1_, ...), custom_call_target="tpu_custom_call" | custom-call | tf_op jit(solution)/shard_map/dirichlet_1_0/pallas_call | solution.py:360
  36.4 2.1 %collective-permute-start.12 = (f32[4,128,128]{2,1,0:T(8,128)S(1)}, f32[4,128,128]{2,1,0:T(8,128)S(1)}, u32[]{:S(2)}, u32[]{:S(2)}) collective-permute-start(f32[4,128,128]{2,1,0:T(8,128)S(1)} %get-tuple-element.39.refs_1_), channel_id=1, source_target_pairs={{0,1},{4,5},{2,3},{6,7},{1,0},{5,4},{3,2},{7,6},{8,9},{12,13},{10,... | collective-permute-start | bytes 786440 | tf_op jit(solution)/shard_map/ppermute | solution.py:372
  38.5 0.0 collective-permute-start.13
  38.5 1.2 %collective-permute-done.12.refs_3_ = f32[4,128,128]{2,1,0:T(8,128)S(1)} collective-permute-done((f32[4,128,128]{2,1,0:T(8,128)S(1)}, f32[4,128,128]{2,1,0:T(8,128)S(1)}, u32[]{:S(2)}, u32[]{:S(2)}) %collective-permute-start.12) | collective-permute-done | bytes 262176 | tf_op jit(solution)/shard_map/ppermute | solution.py:372
  39.7 4.9 %collective-permute-done.13.refs_4_ = f32[4,128,128]{2,1,0:T(8,128)S(1)} collective-permute-done((f32[4,128,128]{2,1,0:T(8,128)S(1)}, f32[4,128,128]{2,1,0:T(8,128)S(1)}, u32[]{:S(2)}, u32[]{:S(2)}) %collective-permute-start.13) | collective-permute-done | bytes 262176 | tf_op jit(solution)/shard_map/ppermute | solution.py:372
  44.6 1.7 %neumann_1_0.1 = (f32[2,128,128]{2,1,0:T(8,128)}, f32[4,128,128]{2,1,0:T(8,128)S(1)}, f32[4,128,128]{2,1,0:T(8,128)S(1)}) custom-call(f32[14,128,128]{2,1,0:T(8,128)S(1)} %get-tuple-element.31.refs_0_, f32[4,128,128]{2,1,0:T(8,128)S(1)} %get-tuple-element.39.refs_1_, f32[4,128,128]{2,1,0:T(8,128)S(1)} %get-tuple-element.40.refs_2_, ...), custom_call_target="tpu_custom_call" | custom-call | tf_op jit(solution)/shard_map/neumann_1_0/pallas_call | solution.py:360
  46.3 0.4 collective-permute-start.14
  46.7 3.1 %collective-permute-start.11 = (f32[2,128,128]{2,1,0:T(8,128)S(1)}, f32[2,128,128]{2,1,0:T(8,128)S(1)}, u32[]{:S(2)}, u32[]{:S(2)}) collective-permute-start(f32[2,128,128]{2,1,0:T(8,128)S(1)} %get-tuple-element.36), channel_id=1, source_target_pairs={{0,6},{4,0},{2,4},{6,2},{1,7},{5,1},{3,5},{7,3},{8,14},{12,8},{10,... | collective-permute-start | bytes 393224 | tf_op jit(solution)/shard_map/ppermute | solution.py:372
  49.8 3.3 %collective-permute-done.11.refs_2_ = f32[2,128,128]{2,1,0:T(8,128)S(1)} collective-permute-done((f32[2,128,128]{2,1,0:T(8,128)S(1)}, f32[2,128,128]{2,1,0:T(8,128)S(1)}, u32[]{:S(2)}, u32[]{:S(2)}) %collective-permute-start.11) | collective-permute-done | bytes 131104 | tf_op jit(solution)/shard_map/ppermute | solution.py:372
  53.1 0.0 collective-permute-done.15.refs_8_
  53.1 1.1 %dirichlet_2_0.1 = (f32[2,128,128]{2,1,0:T(8,128)S(1)}, f32[4,128,128]{2,1,0:T(8,128)S(1)}, f32[4,128,128]{2,1,0:T(8,128)S(1)}, f32[4,128,128]{2,1,0:T(8,128)S(1)}, f32[4,128,128]{2,1,0:T(8,128)S(1)}) custom-call(f32[14,128,128]{2,1,0:T(8,128)S(1)} %get-tuple-element.26.refs_0_, f32[2,128,128]{2,1,0:T(8,128)S(1)} %get-tuple-element.27.refs_1_, ...), custom_call_target="tpu_custom_call" | custom-call | tf_op jit(solution)/shard_map/dirichlet_2_0/pallas_call | solution.py:360
  54.2 1.5 %collective-permute-start.17 = (f32[4,128,128]{2,1,0:T(8,128)S(1)}, f32[4,128,128]{2,1,0:T(8,128)S(1)}, u32[]{:S(2)}, u32[]{:S(2)}) collective-permute-start(f32[4,128,128]{2,1,0:T(8,128)S(1)} %get-tuple-element.46.refs_1_), channel_id=1, source_target_pairs={{0,1},{4,5},{2,3},{6,7},{1,0},{5,4},{3,2},{7,6},{8,9},{12,13},{10,... | collective-permute-start | bytes 786440 | tf_op jit(solution)/shard_map/ppermute | solution.py:372
  55.7 1.2 %collective-permute-done.17.refs_3_ = f32[4,128,128]{2,1,0:T(8,128)S(1)} collective-permute-done((f32[4,128,128]{2,1,0:T(8,128)S(1)}, f32[4,128,128]{2,1,0:T(8,128)S(1)}, u32[]{:S(2)}, u32[]{:S(2)}) %collective-permute-start.17) | collective-permute-done | bytes 262176 | tf_op jit(solution)/shard_map/ppermute | solution.py:372
  56.9 4.9 %collective-permute-done.18.refs_4_ = f32[4,128,128]{2,1,0:T(8,128)S(1)} collective-permute-done((f32[4,128,128]{2,1,0:T(8,128)S(1)}, f32[4,128,128]{2,1,0:T(8,128)S(1)}, u32[]{:S(2)}, u32[]{:S(2)}) %collective-permute-start.18) | collective-permute-done | bytes 262176 | tf_op jit(solution)/shard_map/ppermute | solution.py:372
  61.8 1.6 %neumann_2_0.1 = (f32[2,128,128]{2,1,0:T(8,128)}, f32[4,128,128]{2,1,0:T(8,128)S(1)}, f32[4,128,128]{2,1,0:T(8,128)S(1)}) custom-call(f32[14,128,128]{2,1,0:T(8,128)S(1)} %get-tuple-element.31.refs_0_, f32[4,128,128]{2,1,0:T(8,128)S(1)} %get-tuple-element.46.refs_1_, f32[4,128,128]{2,1,0:T(8,128)S(1)} %get-tuple-element.47.refs_2_, ...), custom_call_target="tpu_custom_call" | custom-call | tf_op jit(solution)/shard_map/neumann_2_0/pallas_call | solution.py:360
  63.4 0.4 collective-permute-start.19
  63.8 0.0 collective-permute-start.20
  63.8 1.2 %collective-permute-done.19.got_a = f32[4,128,128]{2,1,0:T(8,128)S(1)} collective-permute-done((f32[4,128,128]{2,1,0:T(8,128)S(1)}, f32[4,128,128]{2,1,0:T(8,128)S(1)}, u32[]{:S(2)}, u32[]{:S(2)}) %collective-permute-start.19) | collective-permute-done | bytes 262176 | tf_op jit(solution)/shard_map/ppermute | solution.py:372
  65.0 4.9 %collective-permute-done.20.got_b = f32[4,128,128]{2,1,0:T(8,128)S(1)} collective-permute-done((f32[4,128,128]{2,1,0:T(8,128)S(1)}, f32[4,128,128]{2,1,0:T(8,128)S(1)}, u32[]{:S(2)}, u32[]{:S(2)}) %collective-permute-start.20) | collective-permute-done | bytes 262176 | tf_op jit(solution)/shard_map/ppermute | solution.py:372
  70.0 3.5 %collective-permute-start.21 = (f32[4,128,128]{2,1,0:T(8,128)S(1)}, f32[4,128,128]{2,1,0:T(8,128)S(1)}, u32[]{:S(2)}, u32[]{:S(2)}) collective-permute-start(f32[4,128,128]{2,1,0:T(8,128)S(1)} %correct_0.1), channel_id=1, source_target_pairs={{0,2},{4,3},{2,0},{6,1},{1,6},{5,7},{3,4},{7,5},{8,10},{12,11},{10... | collective-permute-start | bytes 786440 | tf_op jit(solution)/shard_map/ppermute | solution.py:372
  73.4 0.1 collective-permute-start.16
  73.5 9.5 %collective-permute-done.16 = f32[1,2,128,128]{3,2,1,0:T(8,128)S(1)} collective-permute-done((f32[1,2,128,128]{3,2,1,0:T(8,128)S(1)}, f32[1,2,128,128]{3,2,1,0:T(8,128)S(1)}, u32[]{:S(2)}, u32[]{:S(2)}) %collective-permute-start.16) | collective-permute-done | bytes 131104 | tf_op jit(solution)/shard_map/ppermute | solution.py:372
  83.0 0.0 collective-permute-done.21
  83.0 0.7 copy.10
  83.7 0.7 copy.11
  (20 shorter events, 0.1 us)
Async XLA Ops:
  0.6 12.5 %copy-start = (f32[2,1,4,128,128]{4,3,2,1,0:T(8,128)S(1)}, f32[2,1,4,128,128]{4,3,2,1,0:T(8,128)}, u32[]{:S(2)}) copy-start(f32[2,1,4,128,128]{4,3,2,1,0:T(8,128)} %refs_9_.3) | copy-start | bytes 1572868
  0.6 7.2 %collective-permute-start.2 = (f32[1,1,4,128,128]{4,3,2,1,0:T(8,128)}, f32[1,1,4,128,128]{4,3,2,1,0:T(8,128)S(1)}, u32[]{:S(2)}, u32[]{:S(2)}) collective-permute-start(f32[1,1,4,128,128]{4,3,2,1,0:T(8,128)} %mine.1), channel_id=1, source_target_pairs={{0,2},{1,4},{2,0},{3,6},{4,1},{5,7},{6,3},{7,5},{8,10},{9,12},{10,... | collective-permute-start | bytes 786440 | tf_op jit(solution)/shard_map/ppermute | solution.py:372
  7.9 1.0 %copy-start.1 = (f32[1,1,4,128,128]{4,3,2,1,0:T(8,128)S(1)}, f32[1,1,4,128,128]{4,3,2,1,0:T(8,128)}, u32[]{:S(2)}) copy-start(f32[1,1,4,128,128]{4,3,2,1,0:T(8,128)} %mine.1) | copy-start | bytes 786436
  8.8 2.5 %copy-start.2 = (f32[1,2,128,128]{3,2,1,0:T(8,128)S(1)}, f32[1,2,128,128]{3,2,1,0:T(8,128)}, u32[]{:S(2)}) copy-start(f32[1,2,128,128]{3,2,1,0:T(8,128)} %refs_2_.1) | copy-start | bytes 393220
  8.8 3.3 %copy-start.3 = (s32[2,128,128]{2,1,0:T(8,128)S(1)}, s32[2,128,128]{2,1,0:T(8,128)}, u32[]{:S(2)}) copy-start(s32[2,128,128]{2,1,0:T(8,128)} %mine_ref.1) | copy-start | bytes 393220
  8.9 10.7 %collective-permute-start.4 = (f32[4,128,128]{2,1,0:T(8,128)S(1)}, f32[4,128,128]{2,1,0:T(8,128)S(1)}, u32[]{:S(2)}, u32[]{:S(2)}) collective-permute-start(f32[4,128,128]{2,1,0:T(8,128)S(1)} %held.1.refs_4_), channel_id=1, source_target_pairs={{0,2},{4,6},{2,0},{6,4},{1,8},{5,12},{3,10},{7,14},{8,1},{12,5},{1... | collective-permute-start | bytes 786440 | tf_op jit(solution)/shard_map/ppermute | solution.py:372
  11.0 8.6 %collective-permute-start.3 = (f32[4,128,128]{2,1,0:T(8,128)S(1)}, f32[4,128,128]{2,1,0:T(8,128)S(1)}, u32[]{:S(2)}, u32[]{:S(2)}) collective-permute-start(f32[4,128,128]{2,1,0:T(8,128)S(1)} %held.1.refs_4_), channel_id=1, source_target_pairs={{0,1},{4,5},{2,3},{6,7},{1,0},{5,4},{3,2},{7,6},{8,9},{12,13},{10,... | collective-permute-start | bytes 786440 | tf_op jit(solution)/shard_map/ppermute | solution.py:372
  11.3 8.3 %collective-permute-start.1 = (f32[1,2,128,128]{3,2,1,0:T(8,128)S(1)}, f32[1,2,128,128]{3,2,1,0:T(8,128)S(1)}, u32[]{:S(2)}, u32[]{:S(2)}) collective-permute-start(f32[1,2,128,128]{3,2,1,0:T(8,128)S(1)} %copy-done.2), channel_id=1, source_target_pairs={{0,2},{1,4},{2,0},{3,6},{4,1},{5,7},{6,3},{7,5},{8,10},{9,12},{10,... | collective-permute-start | bytes 393224 | tf_op jit(solution)/shard_map/ppermute | solution.py:372
  12.1 6.6 %collective-permute-start = (s32[2,128,128]{2,1,0:T(8,128)S(1)}, s32[2,128,128]{2,1,0:T(8,128)S(1)}, u32[]{:S(2)}, u32[]{:S(2)}) collective-permute-start(s32[2,128,128]{2,1,0:T(8,128)S(1)} %copy-done.3), channel_id=1, source_target_pairs={{0,2},{1,4},{2,0},{3,6},{4,1},{5,7},{6,3},{7,5},{8,10},{9,12},{10,... | collective-permute-start | bytes 393224 | tf_op jit(solution)/shard_map/ppermute | solution.py:372
  13.1 5.6 %copy-start.4 = (f32[4]{0:T(128)S(1)}, f32[4]{0:T(128)}, u32[]{:S(2)}) copy-start(f32[4]{0:T(128)} %cond_ref.1) | copy-start | bytes 52
  13.1 5.6 %copy-start.5 = (f32[4]{0:T(128)S(1)}, f32[4]{0:T(128)}, u32[]{:S(2)}) copy-start(f32[4]{0:T(128)} %cap_ref.1) | copy-start | bytes 52
  13.1 9.0 %collective-permute-start.8 = (f32[4,128,128]{2,1,0:T(8,128)S(1)}, f32[4,128,128]{2,1,0:T(8,128)S(1)}, u32[]{:S(2)}, u32[]{:S(2)}) collective-permute-start(f32[4,128,128]{2,1,0:T(8,128)S(1)} %select_bitcast_fusion), channel_id=1, source_target_pairs={{0,4},{1,5},{2,6},{3,7},{4,0},{5,1},{6,2},{7,3},{8,12},{9,13},{10,... | collective-permute-start | bytes 786440 | tf_op jit(solution)/shard_map/ppermute | solution.py:372
  20.6 1.6 %collective-permute-start.6 = (f32[4,128,128]{2,1,0:T(8,128)S(1)}, f32[4,128,128]{2,1,0:T(8,128)S(1)}, u32[]{:S(2)}, u32[]{:S(2)}) collective-permute-start(f32[4,128,128]{2,1,0:T(8,128)S(1)} %get-tuple-element.32.refs_1_), channel_id=1, source_target_pairs={{0,1},{4,5},{2,3},{6,7},{1,0},{5,4},{3,2},{7,6},{8,9},{12,13},{10,... | collective-permute-start | bytes 786440 | tf_op jit(solution)/shard_map/ppermute | solution.py:372
  20.7 6.2 %collective-permute-start.7 = (f32[4,128,128]{2,1,0:T(8,128)S(1)}, f32[4,128,128]{2,1,0:T(8,128)S(1)}, u32[]{:S(2)}, u32[]{:S(2)}) collective-permute-start(f32[4,128,128]{2,1,0:T(8,128)S(1)} %get-tuple-element.33.refs_2_), channel_id=1, source_target_pairs={{0,2},{4,6},{2,0},{6,4},{1,8},{5,12},{3,10},{7,14},{8,1},{12,5},{1... | collective-permute-start | bytes 786440 | tf_op jit(solution)/shard_map/ppermute | solution.py:372
  28.6 5.4 %collective-permute-start.9 = (f32[4,128,128]{2,1,0:T(8,128)S(1)}, f32[4,128,128]{2,1,0:T(8,128)S(1)}, u32[]{:S(2)}, u32[]{:S(2)}) collective-permute-start(f32[4,128,128]{2,1,0:T(8,128)S(1)} %get-tuple-element.34.refs_5_), channel_id=1, source_target_pairs={{0,1},{4,5},{2,3},{6,7},{1,0},{5,4},{3,2},{7,6},{8,9},{12,13},{10,... | collective-permute-start | bytes 786440 | tf_op jit(solution)/shard_map/ppermute | solution.py:372
  29.3 6.1 %collective-permute-start.10 = (f32[4,128,128]{2,1,0:T(8,128)S(1)}, f32[4,128,128]{2,1,0:T(8,128)S(1)}, u32[]{:S(2)}, u32[]{:S(2)}) collective-permute-start(f32[4,128,128]{2,1,0:T(8,128)S(1)} %get-tuple-element.35.refs_6_), channel_id=1, source_target_pairs={{0,2},{4,6},{2,0},{6,4},{1,8},{5,12},{3,10},{7,14},{8,1},{12,5},{1... | collective-permute-start | bytes 786440 | tf_op jit(solution)/shard_map/ppermute | solution.py:372
  29.7 4.3 %collective-permute-start.5 = (f32[2,128,128]{2,1,0:T(8,128)S(1)}, f32[2,128,128]{2,1,0:T(8,128)S(1)}, u32[]{:S(2)}, u32[]{:S(2)}) collective-permute-start(f32[2,128,128]{2,1,0:T(8,128)S(1)} %get-tuple-element.28), channel_id=1, source_target_pairs={{0,6},{4,0},{2,4},{6,2},{1,7},{5,1},{3,5},{7,3},{8,14},{12,8},{10,... | collective-permute-start | bytes 393224 | tf_op jit(solution)/shard_map/ppermute | solution.py:372
  36.4 3.2 %collective-permute-start.12 = (f32[4,128,128]{2,1,0:T(8,128)S(1)}, f32[4,128,128]{2,1,0:T(8,128)S(1)}, u32[]{:S(2)}, u32[]{:S(2)}) collective-permute-start(f32[4,128,128]{2,1,0:T(8,128)S(1)} %get-tuple-element.39.refs_1_), channel_id=1, source_target_pairs={{0,1},{4,5},{2,3},{6,7},{1,0},{5,4},{3,2},{7,6},{8,9},{12,13},{10,... | collective-permute-start | bytes 786440 | tf_op jit(solution)/shard_map/ppermute | solution.py:372
  38.5 6.1 %collective-permute-start.13 = (f32[4,128,128]{2,1,0:T(8,128)S(1)}, f32[4,128,128]{2,1,0:T(8,128)S(1)}, u32[]{:S(2)}, u32[]{:S(2)}) collective-permute-start(f32[4,128,128]{2,1,0:T(8,128)S(1)} %get-tuple-element.40.refs_2_), channel_id=1, source_target_pairs={{0,2},{4,6},{2,0},{6,4},{1,8},{5,12},{3,10},{7,14},{8,1},{12,5},{1... | collective-permute-start | bytes 786440 | tf_op jit(solution)/shard_map/ppermute | solution.py:372
  46.3 6.8 %collective-permute-start.14 = (f32[4,128,128]{2,1,0:T(8,128)S(1)}, f32[4,128,128]{2,1,0:T(8,128)S(1)}, u32[]{:S(2)}, u32[]{:S(2)}) collective-permute-start(f32[4,128,128]{2,1,0:T(8,128)S(1)} %get-tuple-element.41.refs_5_), channel_id=1, source_target_pairs={{0,1},{4,5},{2,3},{6,7},{1,0},{5,4},{3,2},{7,6},{8,9},{12,13},{10,... | collective-permute-start | bytes 786440 | tf_op jit(solution)/shard_map/ppermute | solution.py:372
  46.7 6.4 %collective-permute-start.15 = (f32[4,128,128]{2,1,0:T(8,128)S(1)}, f32[4,128,128]{2,1,0:T(8,128)S(1)}, u32[]{:S(2)}, u32[]{:S(2)}) collective-permute-start(f32[4,128,128]{2,1,0:T(8,128)S(1)} %get-tuple-element.42.refs_6_), channel_id=1, source_target_pairs={{0,2},{4,6},{2,0},{6,4},{1,8},{5,12},{3,10},{7,14},{8,1},{12,5},{1... | collective-permute-start | bytes 786440 | tf_op jit(solution)/shard_map/ppermute | solution.py:372
  46.7 6.4 %collective-permute-start.11 = (f32[2,128,128]{2,1,0:T(8,128)S(1)}, f32[2,128,128]{2,1,0:T(8,128)S(1)}, u32[]{:S(2)}, u32[]{:S(2)}) collective-permute-start(f32[2,128,128]{2,1,0:T(8,128)S(1)} %get-tuple-element.36), channel_id=1, source_target_pairs={{0,6},{4,0},{2,4},{6,2},{1,7},{5,1},{3,5},{7,3},{8,14},{12,8},{10,... | collective-permute-start | bytes 393224 | tf_op jit(solution)/shard_map/ppermute | solution.py:372
  54.2 2.7 %collective-permute-start.17 = (f32[4,128,128]{2,1,0:T(8,128)S(1)}, f32[4,128,128]{2,1,0:T(8,128)S(1)}, u32[]{:S(2)}, u32[]{:S(2)}) collective-permute-start(f32[4,128,128]{2,1,0:T(8,128)S(1)} %get-tuple-element.46.refs_1_), channel_id=1, source_target_pairs={{0,1},{4,5},{2,3},{6,7},{1,0},{5,4},{3,2},{7,6},{8,9},{12,13},{10,... | collective-permute-start | bytes 786440 | tf_op jit(solution)/shard_map/ppermute | solution.py:372
  55.7 6.1 %collective-permute-start.18 = (f32[4,128,128]{2,1,0:T(8,128)S(1)}, f32[4,128,128]{2,1,0:T(8,128)S(1)}, u32[]{:S(2)}, u32[]{:S(2)}) collective-permute-start(f32[4,128,128]{2,1,0:T(8,128)S(1)} %get-tuple-element.47.refs_2_), channel_id=1, source_target_pairs={{0,2},{4,6},{2,0},{6,4},{1,8},{5,12},{3,10},{7,14},{8,1},{12,5},{1... | collective-permute-start | bytes 786440 | tf_op jit(solution)/shard_map/ppermute | solution.py:372
  63.4 1.6 %collective-permute-start.19 = (f32[4,128,128]{2,1,0:T(8,128)S(1)}, f32[4,128,128]{2,1,0:T(8,128)S(1)}, u32[]{:S(2)}, u32[]{:S(2)}) collective-permute-start(f32[4,128,128]{2,1,0:T(8,128)S(1)} %get-tuple-element.48.psi_a), channel_id=1, source_target_pairs={{0,1},{4,5},{2,3},{6,7},{1,0},{5,4},{3,2},{7,6},{8,9},{12,13},{10,... | collective-permute-start | bytes 786440 | tf_op jit(solution)/shard_map/ppermute | solution.py:372
  63.8 6.1 %collective-permute-start.20 = (f32[4,128,128]{2,1,0:T(8,128)S(1)}, f32[4,128,128]{2,1,0:T(8,128)S(1)}, u32[]{:S(2)}, u32[]{:S(2)}) collective-permute-start(f32[4,128,128]{2,1,0:T(8,128)S(1)} %get-tuple-element.49.psi_b), channel_id=1, source_target_pairs={{0,2},{4,6},{2,0},{6,4},{1,8},{5,12},{3,10},{7,14},{8,1},{12,5},{1... | collective-permute-start | bytes 786440 | tf_op jit(solution)/shard_map/ppermute | solution.py:372
  70.0 13.0 %collective-permute-start.21 = (f32[4,128,128]{2,1,0:T(8,128)S(1)}, f32[4,128,128]{2,1,0:T(8,128)S(1)}, u32[]{:S(2)}, u32[]{:S(2)}) collective-permute-start(f32[4,128,128]{2,1,0:T(8,128)S(1)} %correct_0.1), channel_id=1, source_target_pairs={{0,2},{4,3},{2,0},{6,1},{1,6},{5,7},{3,4},{7,5},{8,10},{12,11},{10... | collective-permute-start | bytes 786440 | tf_op jit(solution)/shard_map/ppermute | solution.py:372
  73.4 9.6 %collective-permute-start.16 = (f32[1,2,128,128]{3,2,1,0:T(8,128)S(1)}, f32[1,2,128,128]{3,2,1,0:T(8,128)S(1)}, u32[]{:S(2)}, u32[]{:S(2)}) collective-permute-start(f32[1,2,128,128]{3,2,1,0:T(8,128)S(1)} %bitcast.4), channel_id=1, source_target_pairs={{0,2},{4,3},{2,0},{6,1},{1,6},{5,7},{3,4},{7,5},{8,10},{12,11},{10... | collective-permute-start | bytes 393224 | tf_op jit(solution)/shard_map/ppermute | solution.py:372

commit v2 on v1

--- a/solution.py
+++ b/solution.py
@@ -7,11 +7,12 @@
 from jax.experimental.pallas import tpu as pltpu
 from jax.sharding import PartitionSpec as P
 
+
 SWEEPS = 3
 AXES = ("sub", "iter")
 F32 = jnp.float32
 PAD = 8
-SPLIT = 1
+SPLIT = 2
 LIMIT = 8 << 20
 
 
@@ -39,23 +40,18 @@
             t = s + 1 if s % 2 else s - 1
             self.chip.append((at(s, p), at(t, p) if 0 <= t < slabs else at(s, (p + 2) % groups)))
         self.field = [(at(s, p), at(s, (p - 1) % groups)) for s, p in every]
-        self.enter = []
+        self.enter = [(s * groups + g, at(s, (g - 1) % groups)) for s, g in every]
         self.guess = []
         for s, g in every:
-            here = s * groups + g
-            if s % 2 != g % 2:
-                there = (s ^ 1) * groups + (g ^ 1)
-            else:
-                there = s * groups + (g + 2) % groups
-            self.enter.append((here, there))
-            self.guess.append((here, (s ^ 1) * groups + g))
+            there = s + 1 if s % 2 == 0 else (s - 1 if g % 2 else (s + 1) % slabs)
+            self.guess.append((s * groups + g, there * groups + g))
 
     def at(self, s, p):
         return (2 * (s // 2) + p % 2) * self.groups + 2 * (p // 2) + s % 2
 
     def home(self, ticks):
         every = [(s, p) for s in range(self.slabs) for p in range(self.groups)]
-        return [(self.at(s, p), s * self.groups + (p + ticks - 1) % self.groups) for s, p in every]
+        return [(self.at(s, p), s * self.groups + (p + ticks) % self.groups) for s, p in every]
 
 
 def place():
@@ -72,10 +68,6 @@
     return jnp.logical_not(jnp.where(parity == 0, slab == 0, slab == last))
 
 
-def stays():
-    return lax.rem(lax.axis_index("sub"), 2) == lax.rem(lax.axis_index("iter"), 2)
-
-
 def flipped(plane, planes, parity):
     return plane + parity * (planes - 1 - 2 * plane)
 
@@ -96,17 +88,16 @@
     return 5 * planes + 2 * (planes - 1) + 2
 
 
-def setup_kernel(cond_ref, cap_ref, mine_ref, other_ref, dir_ref, neu_ref, end_ref):
-    planes, ny, nz = mine_ref.shape
+def setup_kernel(cond_ref, cap_ref, label_ref, dir_ref, neu_ref, end_ref):
+    planes, ny, nz = label_ref.shape
     parity, _, _ = place()
-    keep = stays()
     far = has_far()
     row = lax.broadcasted_iota(jnp.int32, (ny, nz), 0)
     col = lax.broadcasted_iota(jnp.int32, (ny, nz), 1)
     ks, cs = [], []
     for p in range(planes):
         at = flipped(p, planes, parity)
-        label = jnp.where(keep, mine_ref[at], other_ref[at])
+        label = label_ref[at]
         k = jnp.zeros((ny, nz), F32)
         c = jnp.zeros((ny, nz), F32)
         for cls in range(cond_ref.shape[0]):
@@ -148,7 +139,7 @@
                 out[row_face(planes, p - 1) + 1] = faces[p - 1] * inverse
             weight = edge * inverse if out is dir_ref else inverse
             if p == 0:
-                out[row_end(planes, 0)] = weight
+                out[row_end(planes, 0)] = jnp.where(far, weight, 0.0)
             if p == planes - 1:
                 out[row_end(planes, 1)] = weight
 
@@ -187,7 +178,7 @@
 
 
 def solve(coef, buffers, hold, first_rhs, final, known_zero=False):
-    planes, tall, nz = buffers[0].shape
+    planes, tall, _ = buffers[0].shape
 
     for n in range(SWEEPS):
         source, target = buffers
@@ -221,11 +212,7 @@
     coef, end = take(2)
     parity, _, position = place()
     far = has_far()
-    if enter:
-        keep = stays()
-        mine, other = take(2)
-    else:
-        (field,) = take(1)
+    (field,) = take(1)
     if start:
         held, from_core, from_chip = take(3)
     else:
@@ -237,8 +224,7 @@
     clear_pads((va, vb))
     for p in range(planes):
         if enter:
-            at = flipped(p, planes, parity)
-            value = jnp.where(keep, mine[0, at], other[0, at])
+            value = field[0, flipped(p, planes, parity)]
         else:
             value = field[p]
         va[p, PAD : PAD + ny, :] = value
@@ -250,12 +236,14 @@
             h_a = old_a[n] + 0.25 * (psi_a[n] + got_a[n])
             h_b = old_b[n] + 0.25 * (psi_b[n] + got_b[n])
             groups = lax.axis_size("iter")
-            begins = (groups - fresh) % groups
+            begins = (-fresh - 1) % groups
             new = position == begins
             local, crossed = ng[fresh - 1, 0, lo + n], gy[lo + n]
             near_a, near_b = (crossed, local) if begins % 2 else (local, crossed)
             h_a = jnp.where(new, near_a, h_a)
-            h_b = jnp.where(new, jnp.where(parity == 1, near_b, got_b[n]), h_b)
+            if begins % 2:
+                near_b = jnp.where(parity == 1, near_b, got_b[n])
+            h_b = jnp.where(new, near_b, h_b)
         out_ha[n] = h_a
         out_hb[n] = jnp.where(far, h_b, 0.0)
     buffers = [va, vb]
@@ -284,18 +272,19 @@
             out_field[p] = value
 
 
-def neumann_kernel(lo, first, fresh, *refs):
+def neumann_kernel(lo, first, more, fresh, *refs):
     refs = list(refs)
     take = lambda n: [refs.pop(0) for _ in range(n)]
     (coef,) = take(1)
-    parity, _, position = place()
-    far = has_far()
+    _, _, position = place()
     q_a, q_b, got_a, got_b = take(4)
     if not first:
         (state,) = take(1)
     if fresh:
-        ng, gy = take(2)
-    out_state, out_a, out_b, va, vb, hold = take(6)
+        (ng,) = take(1)
+    if more:
+        (out_state,) = take(1)
+    out_a, out_b, va, vb, hold = take(5)
     planes = va.shape[0]
     steps, ny, nz = out_a.shape
     clear_pads((va, vb))
@@ -309,7 +298,7 @@
         def first_rhs(p, here, x):
             value = jnp.zeros((8, nz), F32) if zero else coef[row_cap(p), here, :] * x
             if p == 0:
-                jump = jnp.where(far, q_b[n, here, :] + got_b[n, here, :], 0.0)
+                jump = q_b[n, here, :] + got_b[n, here, :]
                 value = value + coef[row_end(planes, 0), here, :] * jump
             if p == planes - 1:
                 jump = q_a[n, here, :] + got_a[n, here, :]
@@ -323,16 +312,17 @@
                 out_a[n, here, :] = value
 
         buffers = solve(coef, buffers, hold, first_rhs, final, known_zero=zero)
-    for p in range(planes):
-        out_state[p] = buffers[0][p, PAD : PAD + ny, :]
+    if more:
+        for p in range(planes):
+            out_state[p] = buffers[0][p, PAD : PAD + ny, :]
     if fresh:
         groups = lax.axis_size("iter")
-        begins = (groups - fresh) % groups
+        begins = (-fresh - 1) % groups
 
         @pl.when(position == begins)
         def _():
             for n in range(steps):
-                out_b[n] = ng[fresh - 1, 0, lo + n] if begins % 2 else gy[lo + n]
+                out_b[n] = ng[fresh - 1, 0, lo + n]
 
 
 def correct_kernel(h_a, h_b, psi_a, psi_b, got_a, got_b, out):
@@ -348,12 +338,15 @@
         out[...] = jnp.where(far, h_b[...] + 0.25 * (psi_b[...] + got_b[...]), 0.0)
 
 
-def hold_kernel(mine, other, out):
-    keep = stays()
-    out[...] = jnp.where(keep, mine[0, 0], other[0, 0])
-
-
-def run(kernel, outs, args, scratch=(), name=None, smem=0):
+def cut_kernel(whole, *outs):
+    lo = 0
+    for out in outs:
+        for n in range(out.shape[0]):
+            out[n] = whole[0, 0, lo + n]
+        lo += out.shape[0]
+
+
+def run(kernel, outs, args, scratch=(), smem=0):
     specs = [pl.BlockSpec(memory_space=pltpu.SMEM)] * smem
     specs += [pl.BlockSpec(memory_space=pltpu.VMEM)] * (len(args) - smem)
     many = isinstance(outs, tuple)
@@ -364,37 +357,41 @@
         out_specs=tuple([pl.BlockSpec(memory_space=pltpu.VMEM)] * len(outs)) if many else specs[-1],
         scratch_shapes=list(scratch),
         compiler_params=pltpu.CompilerParams(vmem_limit_bytes=LIMIT),
-        name=name,
     )(*args[:smem], *[near(a) for a in args[smem:]])
 
 
 def local(layout, fields, labels, traces, new_guess, cond_table, cap_table):
-    move = lambda value, pairs: lax.ppermute(value, AXES, pairs)
+    return steps_of(layout, fields, labels, traces, new_guess, cond_table, cap_table)
+
+
+def steps_of(layout, fields, labels, traces, new_guess, cond_table, cap_table):
+    def move(value, pairs):
+        return lax.ppermute(value, AXES, pairs)
+
     planes, ny, nz = labels.shape
     steps = traces.shape[2]
     ticks = new_guess.shape[0] + 1
     groups = layout.groups
     odd = lax.rem(lax.axis_index("sub"), 2)
-    size = max(1, steps // SPLIT)
-    chunks = [(lo, min(lo + size, steps)) for lo in range(0, steps, size)]
+    chunks = cuts(steps)
     scratch = [vmem((planes, ny + 2 * PAD, nz))] * 2 + [vmem((planes, ny, nz))]
 
-    got_traces = move(traces, layout.enter)
-    got_labels = move(labels, layout.enter)
-    got_fields = move(fields, layout.enter)
-    held = run(hold_kernel, vmem((steps, ny, nz)), [traces, got_traces], name="held")
-    from_core = move(held, layout.core)
-    from_chip = move(held, layout.chip)
+    held = move(traces, layout.enter)
+    labels = move(labels, layout.enter)
+    field = move(fields, layout.enter)
+    pieces = run(cut_kernel, tuple(vmem((hi - lo, ny, nz)) for lo, hi in chunks), [held])
+    waves = {}
+    for (lo, hi), piece in zip(chunks, pieces):
+        waves[lo] = (piece, move(piece, layout.core), move(piece, layout.chip))
     count = rows(planes)
     dir_coef, neu_coef, end = run(
         setup_kernel,
         (vmem((count, ny, nz)), vmem((count, ny, nz)), vmem((2, ny, nz))),
-        [cond_table, cap_table, labels, got_labels],
-        name="setup",
+        [cond_table, cap_table, labels],
         smem=2,
     )
 
-    starts = {t: (groups - t) % groups for t in range(1, ticks)}
+    starts = {t: (-t - 1) % groups for t in range(1, ticks)}
     odds = [t for t in starts if starts[t] % 2]
     evens = [t for t in starts if starts[t] % 2 == 0]
     crossed = {}
@@ -405,58 +402,48 @@
         arrived = move(message, layout.guess)
         crossed[ours] = crossed[theirs] = arrived
 
-    field = None
-    state = None
-    waves = None
     for tick in range(ticks):
         last = tick == ticks - 1
         sent = []
         for lo, hi in chunks:
-            m = hi - lo
-            args = [dir_coef, end]
-            enter = tick == 0 and lo == 0
-            args += [fields, got_fields] if enter else [field]
-            if tick == 0:
-                args += [a[lo:hi] for a in (held, from_core, from_chip)] if len(chunks) > 1 else [held, from_core, from_chip]
-            else:
-                args += [*waves[lo], new_guess, crossed[tick]]
-            plane = vmem((m, ny, nz))
+            plane = vmem((hi - lo, ny, nz))
             field, q_a, q_b, h_a, h_b = run(
-                functools.partial(dirichlet_kernel, lo, tick == 0, enter, tick, last and hi == steps),
+                functools.partial(dirichlet_kernel, lo, tick == 0, tick == 0 and lo == 0, tick, last and hi == steps),
                 (vmem((planes, ny, nz)), plane, plane, plane, plane),
-                args,
+                [dir_coef, end, field, *waves[lo]] + ([new_guess, crossed[tick]] if tick else []),
                 scratch,
-                name=f"dirichlet_{tick}_{lo}",
             )
-            sent.append((q_a, q_b, move(q_a, layout.core), move(q_b, layout.chip), h_a, h_b))
-        field = move(field[None] if last else field, layout.home(ticks) if last else layout.field)
+            in_a, in_b = move(q_a, layout.core), move(q_b, layout.chip)
+            sent.append((q_a, q_b, in_a, in_b, h_a, h_b))
+        if last:
+            field = move(field[None], layout.home(ticks))
+        else:
+            field = move(field, layout.field)
         fresh = 0 if last else tick + 1
-        waves = {}
-        state = None
+        state = []
         ends = []
-        for (lo, hi), (q_a, q_b, got_a, got_b, h_a, h_b) in zip(chunks, sent):
-            m = hi - lo
-            args = [neu_coef, q_a, q_b, got_a, got_b]
-            if lo:
-                args.append(state)
-            if fresh:
-                args += [new_guess, crossed[fresh]]
-            plane = vmem((m, ny, nz))
-            state, psi_a, psi_b = run(
-                functools.partial(neumann_kernel, lo, lo == 0, fresh),
-                (vmem((planes, ny, nz)), plane, plane),
-                args,
+        for n, ((lo, hi), (q_a, q_b, in_a, in_b, h_a, h_b)) in enumerate(zip(chunks, sent)):
+            plane = vmem((hi - lo, ny, nz))
+            more = n + 1 < len(chunks)
+            swap = fresh if fresh and starts[fresh] % 2 else 0
+            *state, psi_a, psi_b = run(
+                functools.partial(neumann_kernel, lo, lo == 0, more, swap),
+                ((vmem((planes, ny, nz)),) if more else ()) + (plane, plane),
+                [neu_coef, q_a, q_b, in_a, in_b, *state] + ([new_guess] if swap else []),
                 scratch,
-                name=f"neumann_{tick}_{lo}",
             )
-            in_a = move(psi_a, layout.core)
-            in_b = move(psi_b, layout.chip)
+            in_a, in_b = move(psi_a, layout.core), move(psi_b, layout.chip)
             waves[lo] = (h_a, h_b, psi_a, psi_b, in_a, in_b)
             if last:
-                done = run(correct_kernel, plane, list(waves[lo]), name=f"correct_{lo}")
+                done = run(correct_kernel, plane, list(waves[lo]))
                 ends.append(move(done, layout.home(ticks)))
     corrected = ends[0] if len(ends) == 1 else jnp.concatenate(ends, axis=0)
     return field, corrected[None, None]
+
+
+def cuts(steps):
+    size = max(1, steps // SPLIT)
+    return [(lo, min(lo + size, steps)) for lo in range(0, steps, size)]
 
 
 def solution(mesh):

time: 84.5 us -> 65.4 us (0.77)
  waiting for transfers between devices: 50 us -> 25.5 us
  starting transfers between devices: 22.1 us -> 29.6 us
  Pallas kernels: 9.19 us -> 6.94 us
  other arithmetic: 0.03 us -> 1.78 us
  local copies, waits for them, and re-layouts: 2.33 us -> 0.67 us
    ppermute x22 -> x37, waiting for transfers between devices: 50 us -> 25.5 us  [move(): return lax.ppermute(value, AXES, pairs)]
    ppermute x22 -> x37, starting transfers between devices: 22.1 us -> 29.6 us  [move(): return lax.ppermute(value, AXES, pairs)]
    pallas_call x9 -> x16, Pallas kernels: 9.19 us -> 6.94 us  [run(): pl.pallas_call(kernel, out_shape=outs, in_specs=specs, out_specs=tuple([p...]
    unnamed x14 -> x7, local copies, waits for them, and re-layouts: 2.33 us -> 0.67 us
    select_n x1, other arithmetic: 0.03 us -> 1.06 us  [steps_of(): jnp.where(odd == 0, new_guess[ours - 1, 0], new_guess[theirs - 1, 0])]
  transfers between devices with their start and end apart: 22 -> 37, of which waited for: 14 -> 15; matrix products, arithmetic and copies ran while one was open for 0% -> 2% of each run, Pallas kernels for 2% -> 10%
where the time goes in v2:
time: 65.4 us; the launch traced here: 65.3 us
  starting transfers between devices  29.6 us (45%)
  waiting for transfers between devices  25.5 us (39%)
  Pallas kernels  6.94 us (11%)
  other arithmetic  1.78 us (3%)
  between operations  0.81 us (1%)
  local copies, waits for them, and re-layouts  0.67 us (1%)
    ppermute x37, starting transfers between devices, move(): return lax.ppermute(value, AXES, pairs)  29.6 us
    ppermute x37, waiting for transfers between devices, move(): return lax.ppermute(value, AXES, pairs)  25.5 us
    pallas_call x16, Pallas kernels, run(): pl.pallas_call(kernel, out_shape=outs, in_specs=specs, out_specs=tuple([p...  6.94 us
  transfers between devices with their start and end apart: 37, of which 15 were waited for; matrix products, arithmetic and copies ran while one was open for 2% of the time, Pallas kernels for 10%

profile of v2, /device:TPU:1, one launch (start us, length us, event | category | flops | bytes accessed | tf_op | source)
XLA Modules:
  0.0 65.3 jit_solution(13461115078027597184)
XLA Ops:
  0.7 3.9 %collective-permute-start = (s32[2,128,128]{2,1,0:T(8,128)}, s32[2,128,128]{2,1,0:T(8,128)S(1)}, u32[]{:S(2)}, u32[]{:S(2)}) collective-permute-start(s32[2,128,128]{2,1,0:T(8,128)} %param.7), channel_id=1, source_target_pairs={{0,6},{1,0},{2,4},{3,2},{4,7},{5,1},{6,5},{7,3},{8,14},{9,8},{10,1... | collective-permute-start | bytes 393224 | tf_op jit(solution)/shard_map/ppermute | solution.py:369
  4.7 2.0 %collective-permute-done.2.whole = f32[1,1,4,128,128]{4,3,2,1,0:T(8,128)S(1)} collective-permute-done((f32[1,1,4,128,128]{4,3,2,1,0:T(8,128)}, f32[1,1,4,128,128]{4,3,2,1,0:T(8,128)S(1)}, u32[]{:S(2)}, u32[]{:S(2)}) %collective-permute-start.2) | collective-permute-done | bytes 262176 | tf_op jit(solution)/shard_map/ppermute | solution.py:369
  6.7 2.2 %collective-permute-start.3 = (f32[2,128,128]{2,1,0:T(8,128)S(1)}, f32[2,128,128]{2,1,0:T(8,128)S(1)}, u32[]{:S(2)}, u32[]{:S(2)}) collective-permute-start(f32[2,128,128]{2,1,0:T(8,128)S(1)} %get-tuple-element.54.refs_3_), channel_id=1, source_target_pairs={{0,1},{4,5},{2,3},{6,7},{1,0},{5,4},{3,2},{7,6},{8,9},{12,13},{10,... | collective-permute-start | bytes 393224 | tf_op jit(solution)/shard_map/ppermute | solution.py:369
  8.9 1.3 %collective-permute-start.4 = (f32[2,128,128]{2,1,0:T(8,128)S(1)}, f32[2,128,128]{2,1,0:T(8,128)S(1)}, u32[]{:S(2)}, u32[]{:S(2)}) collective-permute-start(f32[2,128,128]{2,1,0:T(8,128)S(1)} %get-tuple-element.54.refs_3_), channel_id=1, source_target_pairs={{0,2},{4,6},{2,0},{6,4},{1,8},{5,12},{3,10},{7,14},{8,1},{12,5},{1... | collective-permute-start | bytes 393224 | tf_op jit(solution)/shard_map/ppermute | solution.py:369
  10.2 1.7 %collective-permute-start.6 = (f32[2,128,128]{2,1,0:T(8,128)S(1)}, f32[2,128,128]{2,1,0:T(8,128)S(1)}, u32[]{:S(2)}, u32[]{:S(2)}) collective-permute-start(f32[2,128,128]{2,1,0:T(8,128)S(1)} %get-tuple-element.56.refs_3_), channel_id=1, source_target_pairs={{0,2},{4,6},{2,0},{6,4},{1,8},{5,12},{3,10},{7,14},{8,1},{12,5},{1... | collective-permute-start | bytes 393224 | tf_op jit(solution)/shard_map/ppermute | solution.py:369
  11.9 1.1 %select_bitcast_fusion = f32[4,128,128]{2,1,0:T(8,128)S(1)} fusion(f32[2,1,4,128,128]{4,3,2,1,0:T(8,128)} %refs_9_.7, pred[]{:T(512)S(6)} %eq.3), kind=kLoop, calls=%fused_computation.1 | loop fusion | flops 65536 | bytes 786433 | tf_op jit(solution)/shard_map/jit(_where)/select_n | solution.py:401
  13.0 2.1 %collective-permute-start.12 = (f32[4,128,128]{2,1,0:T(8,128)S(1)}, f32[4,128,128]{2,1,0:T(8,128)S(1)}, u32[]{:S(2)}, u32[]{:S(2)}) collective-permute-start(f32[4,128,128]{2,1,0:T(8,128)S(1)} %select_bitcast_fusion), channel_id=1, source_target_pairs={{0,4},{1,5},{2,6},{3,7},{4,8},{5,1},{6,10},{7,3},{8,12},{9,13},{10... | collective-permute-start | bytes 786440 | tf_op jit(solution)/shard_map/ppermute | solution.py:369
  15.1 0.9 %shard_map.77 = (f32[14,128,128]{2,1,0:T(8,128)S(1)}, f32[14,128,128]{2,1,0:T(8,128)S(1)}, f32[2,128,128]{2,1,0:T(8,128)S(1)}) custom-call(f32[4]{0:T(128)S(1)} %copy-done.1, f32[4]{0:T(128)S(1)} %copy-done.2, s32[2,128,128]{2,1,0:T(8,128)S(1)} %collective-permute-done.label_ref), custom_call_target="tpu_custom_call" | custom-call | tf_op jit(solution)/shard_map/pallas_call | solution.py:353
  16.0 0.6 shard_map.79
  16.7 0.7 %collective-permute-start.8 = (f32[2,128,128]{2,1,0:T(8,128)S(1)}, f32[2,128,128]{2,1,0:T(8,128)S(1)}, u32[]{:S(2)}, u32[]{:S(2)}) collective-permute-start(f32[2,128,128]{2,1,0:T(8,128)S(1)} %get-tuple-element.61.refs_1_), channel_id=1, source_target_pairs={{0,1},{4,5},{2,3},{6,7},{1,0},{5,4},{3,2},{7,6},{8,9},{12,13},{10,... | collective-permute-start | bytes 393224 | tf_op jit(solution)/shard_map/ppermute | solution.py:369
  17.3 1.1 %collective-permute-start.9 = (f32[2,128,128]{2,1,0:T(8,128)S(1)}, f32[2,128,128]{2,1,0:T(8,128)S(1)}, u32[]{:S(2)}, u32[]{:S(2)}) collective-permute-start(f32[2,128,128]{2,1,0:T(8,128)S(1)} %get-tuple-element.62.refs_2_), channel_id=1, source_target_pairs={{0,2},{4,6},{2,0},{6,4},{1,8},{5,12},{3,10},{7,14},{8,1},{12,5},{1... | collective-permute-start | bytes 393224 | tf_op jit(solution)/shard_map/ppermute | solution.py:369
  18.4 0.5 shard_map.80
  19.3 1.3 %collective-permute-start.14 = (f32[2,128,128]{2,1,0:T(8,128)S(1)}, f32[2,128,128]{2,1,0:T(8,128)S(1)}, u32[]{:S(2)}, u32[]{:S(2)}) collective-permute-start(f32[2,128,128]{2,1,0:T(8,128)S(1)} %get-tuple-element.69.refs_2_), channel_id=1, source_target_pairs={{0,2},{4,6},{2,0},{6,4},{1,8},{5,12},{3,10},{7,14},{8,1},{12,5},{1... | collective-permute-start | bytes 393224 | tf_op jit(solution)/shard_map/ppermute | solution.py:369
  20.7 0.6 collective-permute-start.7
  21.3 0.7 %collective-permute-done.9.refs_4_ = f32[2,128,128]{2,1,0:T(8,128)S(1)} collective-permute-done((f32[2,128,128]{2,1,0:T(8,128)S(1)}, f32[2,128,128]{2,1,0:T(8,128)S(1)}, u32[]{:S(2)}, u32[]{:S(2)}) %collective-permute-start.9) | collective-permute-done | bytes 131104 | tf_op jit(solution)/shard_map/ppermute | solution.py:369
  22.4 0.5 collective-permute-start.10
  22.9 0.6 collective-permute-start.11
  23.5 0.5 collective-permute-done.14.refs_4_
  24.0 0.5 shard_map.83
  24.5 1.2 %collective-permute-start.15 = (f32[2,128,128]{2,1,0:T(8,128)S(1)}, f32[2,128,128]{2,1,0:T(8,128)S(1)}, u32[]{:S(2)}, u32[]{:S(2)}) collective-permute-start(f32[2,128,128]{2,1,0:T(8,128)S(1)} %get-tuple-element.71.refs_5_), channel_id=1, source_target_pairs={{0,1},{4,5},{2,3},{6,7},{1,0},{5,4},{3,2},{7,6},{8,9},{12,13},{10,... | collective-permute-start | bytes 393224 | tf_op jit(solution)/shard_map/ppermute | solution.py:369
  26.0 1.5 %collective-permute-done.11.refs_8_ = f32[2,128,128]{2,1,0:T(8,128)S(1)} collective-permute-done((f32[2,128,128]{2,1,0:T(8,128)S(1)}, f32[2,128,128]{2,1,0:T(8,128)S(1)}, u32[]{:S(2)}, u32[]{:S(2)}) %collective-permute-start.11) | collective-permute-done | bytes 131104 | tf_op jit(solution)/shard_map/ppermute | solution.py:369
  27.5 0.5 shard_map.82
  28.1 1.2 %collective-permute-start.18 = (f32[2,128,128]{2,1,0:T(8,128)S(1)}, f32[2,128,128]{2,1,0:T(8,128)S(1)}, u32[]{:S(2)}, u32[]{:S(2)}) collective-permute-start(f32[2,128,128]{2,1,0:T(8,128)S(1)} %get-tuple-element.76.refs_1_), channel_id=1, source_target_pairs={{0,1},{4,5},{2,3},{6,7},{1,0},{5,4},{3,2},{7,6},{8,9},{12,13},{10,... | collective-permute-start | bytes 393224 | tf_op jit(solution)/shard_map/ppermute | solution.py:369
  29.3 1.1 %collective-permute-done.16.refs_8_ = f32[2,128,128]{2,1,0:T(8,128)S(1)} collective-permute-done((f32[2,128,128]{2,1,0:T(8,128)S(1)}, f32[2,128,128]{2,1,0:T(8,128)S(1)}, u32[]{:S(2)}, u32[]{:S(2)}) %collective-permute-start.16) | collective-permute-done | bytes 131104 | tf_op jit(solution)/shard_map/ppermute | solution.py:369
  30.4 0.5 shard_map.84
  30.9 0.6 collective-permute-start.22
  31.7 2.3 %collective-permute-start.17 = (f32[2,128,128]{2,1,0:T(8,128)S(1)}, f32[2,128,128]{2,1,0:T(8,128)S(1)}, u32[]{:S(2)}, u32[]{:S(2)}) collective-permute-start(f32[2,128,128]{2,1,0:T(8,128)S(1)} %get-tuple-element.73), channel_id=1, source_target_pairs={{0,6},{4,0},{2,4},{6,2},{1,7},{5,1},{3,5},{7,3},{8,14},{12,8},{10,... | collective-permute-start | bytes 393224 | tf_op jit(solution)/shard_map/ppermute | solution.py:369
  34.5 0.7 %collective-permute-start.20 = (f32[2,128,128]{2,1,0:T(8,128)S(1)}, f32[2,128,128]{2,1,0:T(8,128)S(1)}, u32[]{:S(2)}, u32[]{:S(2)}) collective-permute-start(f32[2,128,128]{2,1,0:T(8,128)S(1)} %get-tuple-element.78.refs_5_), channel_id=1, source_target_pairs={{0,1},{4,5},{2,3},{6,7},{1,0},{5,4},{3,2},{7,6},{8,9},{12,13},{10,... | collective-permute-start | bytes 393224 | tf_op jit(solution)/shard_map/ppermute | solution.py:369
  35.6 0.5 collective-permute-done.23.refs_4_
  36.2 0.5 shard_map.87
  36.7 1.4 %collective-permute-start.24 = (f32[2,128,128]{2,1,0:T(8,128)S(1)}, f32[2,128,128]{2,1,0:T(8,128)S(1)}, u32[]{:S(2)}, u32[]{:S(2)}) collective-permute-start(f32[2,128,128]{2,1,0:T(8,128)S(1)} %get-tuple-element.86.refs_5_), channel_id=1, source_target_pairs={{0,1},{4,5},{2,3},{6,7},{1,0},{5,4},{3,2},{7,6},{8,9},{12,13},{10,... | collective-permute-start | bytes 393224 | tf_op jit(solution)/shard_map/ppermute | solution.py:369
  38.0 1.9 %collective-permute-done.21.refs_8_ = f32[2,128,128]{2,1,0:T(8,128)S(1)} collective-permute-done((f32[2,128,128]{2,1,0:T(8,128)S(1)}, f32[2,128,128]{2,1,0:T(8,128)S(1)}, u32[]{:S(2)}, u32[]{:S(2)}) %collective-permute-start.21) | collective-permute-done | bytes 131104 | tf_op jit(solution)/shard_map/ppermute | solution.py:369
  39.9 0.5 shard_map.86
  40.4 1.0 %collective-permute-start.27 = (f32[2,128,128]{2,1,0:T(8,128)S(1)}, f32[2,128,128]{2,1,0:T(8,128)S(1)}, u32[]{:S(2)}, u32[]{:S(2)}) collective-permute-start(f32[2,128,128]{2,1,0:T(8,128)S(1)} %get-tuple-element.91.refs_1_), channel_id=1, source_target_pairs={{0,1},{4,5},{2,3},{6,7},{1,0},{5,4},{3,2},{7,6},{8,9},{12,13},{10,... | collective-permute-start | bytes 393224 | tf_op jit(solution)/shard_map/ppermute | solution.py:369
  41.4 1.3 %collective-permute-done.25.refs_8_ = f32[2,128,128]{2,1,0:T(8,128)S(1)} collective-permute-done((f32[2,128,128]{2,1,0:T(8,128)S(1)}, f32[2,128,128]{2,1,0:T(8,128)S(1)}, u32[]{:S(2)}, u32[]{:S(2)}) %collective-permute-start.25) | collective-permute-done | bytes 131104 | tf_op jit(solution)/shard_map/ppermute | solution.py:369
  42.7 0.5 shard_map.88
  43.3 0.8 %collective-permute-start.32 = (f32[2,128,128]{2,1,0:T(8,128)S(1)}, f32[2,128,128]{2,1,0:T(8,128)S(1)}, u32[]{:S(2)}, u32[]{:S(2)}) collective-permute-start(f32[2,128,128]{2,1,0:T(8,128)S(1)} %get-tuple-element.97.refs_1_), channel_id=1, source_target_pairs={{0,1},{4,5},{2,3},{6,7},{1,0},{5,4},{3,2},{7,6},{8,9},{12,13},{10,... | collective-permute-start | bytes 393224 | tf_op jit(solution)/shard_map/ppermute | solution.py:369
  44.1 1.9 %collective-permute-done.28.refs_4_ = f32[2,128,128]{2,1,0:T(8,128)S(1)} collective-permute-done((f32[2,128,128]{2,1,0:T(8,128)S(1)}, f32[2,128,128]{2,1,0:T(8,128)S(1)}, u32[]{:S(2)}, u32[]{:S(2)}) %collective-permute-start.28) | collective-permute-done | bytes 131104 | tf_op jit(solution)/shard_map/ppermute | solution.py:369
  46.5 2.3 %collective-permute-done.33.refs_4_ = f32[2,128,128]{2,1,0:T(8,128)S(1)} collective-permute-done((f32[2,128,128]{2,1,0:T(8,128)S(1)}, f32[2,128,128]{2,1,0:T(8,128)S(1)}, u32[]{:S(2)}, u32[]{:S(2)}) %collective-permute-start.33) | collective-permute-done | bytes 131104 | tf_op jit(solution)/shard_map/ppermute | solution.py:369
  48.7 0.5 shard_map.91
  49.7 2.1 %collective-permute-start.29 = (f32[2,128,128]{2,1,0:T(8,128)S(1)}, f32[2,128,128]{2,1,0:T(8,128)S(1)}, u32[]{:S(2)}, u32[]{:S(2)}) collective-permute-start(f32[2,128,128]{2,1,0:T(8,128)S(1)} %get-tuple-element.93.psi_a), channel_id=1, source_target_pairs={{0,1},{4,5},{2,3},{6,7},{1,0},{5,4},{3,2},{7,6},{8,9},{12,13},{10,... | collective-permute-start | bytes 393224 | tf_op jit(solution)/shard_map/ppermute | solution.py:369
  51.8 2.6 %collective-permute-done.35.got_b = f32[2,128,128]{2,1,0:T(8,128)S(1)} collective-permute-done((f32[2,128,128]{2,1,0:T(8,128)S(1)}, f32[2,128,128]{2,1,0:T(8,128)S(1)}, u32[]{:S(2)}, u32[]{:S(2)}) %collective-permute-start.35) | collective-permute-done | bytes 131104 | tf_op jit(solution)/shard_map/ppermute | solution.py:369
  54.7 1.7 %collective-permute-done.30.got_b = f32[2,128,128]{2,1,0:T(8,128)S(1)} collective-permute-done((f32[2,128,128]{2,1,0:T(8,128)S(1)}, f32[2,128,128]{2,1,0:T(8,128)S(1)}, u32[]{:S(2)}, u32[]{:S(2)}) %collective-permute-start.30) | collective-permute-done | bytes 131104 | tf_op jit(solution)/shard_map/ppermute | solution.py:369
  56.5 3.3 %collective-permute-done.26 = f32[1,2,128,128]{3,2,1,0:T(8,128)S(1)} collective-permute-done((f32[1,2,128,128]{3,2,1,0:T(8,128)S(1)}, f32[1,2,128,128]{3,2,1,0:T(8,128)S(1)}, u32[]{:S(2)}, u32[]{:S(2)}) %collective-permute-start.26) | collective-permute-done | bytes 131104 | tf_op jit(solution)/shard_map/ppermute | solution.py:369
  59.8 2.8 %collective-permute-done.36 = f32[2,128,128]{2,1,0:T(8,128)S(1)} collective-permute-done((f32[2,128,128]{2,1,0:T(8,128)S(1)}, f32[2,128,128]{2,1,0:T(8,128)S(1)}, u32[]{:S(2)}, u32[]{:S(2)}) %collective-permute-start.36) | collective-permute-done | bytes 131104 | tf_op jit(solution)/shard_map/ppermute | solution.py:369
  62.6 1.3 %collective-permute-done.31 = f32[2,128,128]{2,1,0:T(8,128)S(1)} collective-permute-done((f32[2,128,128]{2,1,0:T(8,128)S(1)}, f32[2,128,128]{2,1,0:T(8,128)S(1)}, u32[]{:S(2)}, u32[]{:S(2)}) %collective-permute-start.31) | collective-permute-done | bytes 131104 | tf_op jit(solution)/shard_map/ppermute | solution.py:369
  63.9 0.7 %maximum_bitcast_fusion = f32[1,1,4,128,128]{4,3,2,1,0:T(8,128)} fusion(f32[2,128,128]{2,1,0:T(8,128)S(1)} %collective-permute-done.36, f32[2,128,128]{2,1,0:T(8,128)S(1)} %collective-permute-done.31), kind=kLoop, calls=%fused_computation | loop fusion | flops 65536 | bytes 524288 | tf_op jit(solution)/shard_map/broadcast_in_dim | solution.py:441
  64.6 0.7 %copy.9 = f32[1,2,128,128]{3,2,1,0:T(8,128)} copy(f32[1,2,128,128]{3,2,1,0:T(8,128)S(1)} %collective-permute-done.26) | data formatting | bytes 262144
  (51 shorter events, 3.8 us)
Async XLA Ops:
  0.6 6.1 %collective-permute-start.2 = (f32[1,1,4,128,128]{4,3,2,1,0:T(8,128)}, f32[1,1,4,128,128]{4,3,2,1,0:T(8,128)S(1)}, u32[]{:S(2)}, u32[]{:S(2)}) collective-permute-start(f32[1,1,4,128,128]{4,3,2,1,0:T(8,128)} %param.8), channel_id=1, source_target_pairs={{0,6},{1,0},{2,4},{3,2},{4,7},{5,1},{6,5},{7,3},{8,14},{9,8},{10,1... | collective-permute-start | bytes 786440 | tf_op jit(solution)/shard_map/ppermute | solution.py:369
  0.7 9.5 %collective-permute-start = (s32[2,128,128]{2,1,0:T(8,128)}, s32[2,128,128]{2,1,0:T(8,128)S(1)}, u32[]{:S(2)}, u32[]{:S(2)}) collective-permute-start(s32[2,128,128]{2,1,0:T(8,128)} %param.7), channel_id=1, source_target_pairs={{0,6},{1,0},{2,4},{3,2},{4,7},{5,1},{6,5},{7,3},{8,14},{9,8},{10,1... | collective-permute-start | bytes 393224 | tf_op jit(solution)/shard_map/ppermute | solution.py:369
  4.6 8.3 %collective-permute-start.1 = (f32[1,2,128,128]{3,2,1,0:T(8,128)}, f32[1,2,128,128]{3,2,1,0:T(8,128)S(1)}, u32[]{:S(2)}, u32[]{:S(2)}) collective-permute-start(f32[1,2,128,128]{3,2,1,0:T(8,128)} %param.6), channel_id=1, source_target_pairs={{0,6},{1,0},{2,4},{3,2},{4,7},{5,1},{6,5},{7,3},{8,14},{9,8},{10,1... | collective-permute-start | bytes 393224 | tf_op jit(solution)/shard_map/ppermute | solution.py:369
  6.7 9.3 %collective-permute-start.3 = (f32[2,128,128]{2,1,0:T(8,128)S(1)}, f32[2,128,128]{2,1,0:T(8,128)S(1)}, u32[]{:S(2)}, u32[]{:S(2)}) collective-permute-start(f32[2,128,128]{2,1,0:T(8,128)S(1)} %get-tuple-element.54.refs_3_), channel_id=1, source_target_pairs={{0,1},{4,5},{2,3},{6,7},{1,0},{5,4},{3,2},{7,6},{8,9},{12,13},{10,... | collective-permute-start | bytes 393224 | tf_op jit(solution)/shard_map/ppermute | solution.py:369
  8.9 7.1 %collective-permute-start.4 = (f32[2,128,128]{2,1,0:T(8,128)S(1)}, f32[2,128,128]{2,1,0:T(8,128)S(1)}, u32[]{:S(2)}, u32[]{:S(2)}) collective-permute-start(f32[2,128,128]{2,1,0:T(8,128)S(1)} %get-tuple-element.54.refs_3_), channel_id=1, source_target_pairs={{0,2},{4,6},{2,0},{6,4},{1,8},{5,12},{3,10},{7,14},{8,1},{12,5},{1... | collective-permute-start | bytes 393224 | tf_op jit(solution)/shard_map/ppermute | solution.py:369
  10.2 4.9 %copy-start.1 = (f32[4]{0:T(128)S(1)}, f32[4]{0:T(128)}, u32[]{:S(2)}) copy-start(f32[4]{0:T(128)} %cond_ref.1) | copy-start | bytes 52
  10.2 4.9 %copy-start.2 = (f32[4]{0:T(128)S(1)}, f32[4]{0:T(128)}, u32[]{:S(2)}) copy-start(f32[4]{0:T(128)} %cap_ref.1) | copy-start | bytes 52
  10.2 8.2 %collective-permute-start.5 = (f32[2,128,128]{2,1,0:T(8,128)S(1)}, f32[2,128,128]{2,1,0:T(8,128)S(1)}, u32[]{:S(2)}, u32[]{:S(2)}) collective-permute-start(f32[2,128,128]{2,1,0:T(8,128)S(1)} %get-tuple-element.56.refs_3_), channel_id=1, source_target_pairs={{0,1},{4,5},{2,3},{6,7},{1,0},{5,4},{3,2},{7,6},{8,9},{12,13},{10,... | collective-permute-start | bytes 393224 | tf_op jit(solution)/shard_map/ppermute | solution.py:369
  10.2 8.2 %collective-permute-start.6 = (f32[2,128,128]{2,1,0:T(8,128)S(1)}, f32[2,128,128]{2,1,0:T(8,128)S(1)}, u32[]{:S(2)}, u32[]{:S(2)}) collective-permute-start(f32[2,128,128]{2,1,0:T(8,128)S(1)} %get-tuple-element.56.refs_3_), channel_id=1, source_target_pairs={{0,2},{4,6},{2,0},{6,4},{1,8},{5,12},{3,10},{7,14},{8,1},{12,5},{1... | collective-permute-start | bytes 393224 | tf_op jit(solution)/shard_map/ppermute | solution.py:369
  13.0 12.7 %collective-permute-start.12 = (f32[4,128,128]{2,1,0:T(8,128)S(1)}, f32[4,128,128]{2,1,0:T(8,128)S(1)}, u32[]{:S(2)}, u32[]{:S(2)}) collective-permute-start(f32[4,128,128]{2,1,0:T(8,128)S(1)} %select_bitcast_fusion), channel_id=1, source_target_pairs={{0,4},{1,5},{2,6},{3,7},{4,8},{5,1},{6,10},{7,3},{8,12},{9,13},{10... | collective-permute-start | bytes 786440 | tf_op jit(solution)/shard_map/ppermute | solution.py:369
  16.7 4.0 %collective-permute-start.8 = (f32[2,128,128]{2,1,0:T(8,128)S(1)}, f32[2,128,128]{2,1,0:T(8,128)S(1)}, u32[]{:S(2)}, u32[]{:S(2)}) collective-permute-start(f32[2,128,128]{2,1,0:T(8,128)S(1)} %get-tuple-element.61.refs_1_), channel_id=1, source_target_pairs={{0,1},{4,5},{2,3},{6,7},{1,0},{5,4},{3,2},{7,6},{8,9},{12,13},{10,... | collective-permute-start | bytes 393224 | tf_op jit(solution)/shard_map/ppermute | solution.py:369
  17.3 4.7 %collective-permute-start.9 = (f32[2,128,128]{2,1,0:T(8,128)S(1)}, f32[2,128,128]{2,1,0:T(8,128)S(1)}, u32[]{:S(2)}, u32[]{:S(2)}) collective-permute-start(f32[2,128,128]{2,1,0:T(8,128)S(1)} %get-tuple-element.62.refs_2_), channel_id=1, source_target_pairs={{0,2},{4,6},{2,0},{6,4},{1,8},{5,12},{3,10},{7,14},{8,1},{12,5},{1... | collective-permute-start | bytes 393224 | tf_op jit(solution)/shard_map/ppermute | solution.py:369
  19.0 3.9 %collective-permute-start.13 = (f32[2,128,128]{2,1,0:T(8,128)S(1)}, f32[2,128,128]{2,1,0:T(8,128)S(1)}, u32[]{:S(2)}, u32[]{:S(2)}) collective-permute-start(f32[2,128,128]{2,1,0:T(8,128)S(1)} %get-tuple-element.68.refs_1_), channel_id=1, source_target_pairs={{0,1},{4,5},{2,3},{6,7},{1,0},{5,4},{3,2},{7,6},{8,9},{12,13},{10,... | collective-permute-start | bytes 393224 | tf_op jit(solution)/shard_map/ppermute | solution.py:369
  19.3 4.7 %collective-permute-start.14 = (f32[2,128,128]{2,1,0:T(8,128)S(1)}, f32[2,128,128]{2,1,0:T(8,128)S(1)}, u32[]{:S(2)}, u32[]{:S(2)}) collective-permute-start(f32[2,128,128]{2,1,0:T(8,128)S(1)} %get-tuple-element.69.refs_2_), channel_id=1, source_target_pairs={{0,2},{4,6},{2,0},{6,4},{1,8},{5,12},{3,10},{7,14},{8,1},{12,5},{1... | collective-permute-start | bytes 393224 | tf_op jit(solution)/shard_map/ppermute | solution.py:369
  20.7 5.3 %collective-permute-start.7 = (f32[2,128,128]{2,1,0:T(8,128)S(1)}, f32[2,128,128]{2,1,0:T(8,128)S(1)}, u32[]{:S(2)}, u32[]{:S(2)}) collective-permute-start(f32[2,128,128]{2,1,0:T(8,128)S(1)} %get-tuple-element.57), channel_id=1, source_target_pairs={{0,6},{4,0},{2,4},{6,2},{1,7},{5,1},{3,5},{7,3},{8,14},{12,8},{10,... | collective-permute-start | bytes 393224 | tf_op jit(solution)/shard_map/ppermute | solution.py:369
  22.4 3.6 %collective-permute-start.10 = (f32[2,128,128]{2,1,0:T(8,128)S(1)}, f32[2,128,128]{2,1,0:T(8,128)S(1)}, u32[]{:S(2)}, u32[]{:S(2)}) collective-permute-start(f32[2,128,128]{2,1,0:T(8,128)S(1)} %get-tuple-element.63.refs_5_), channel_id=1, source_target_pairs={{0,1},{4,5},{2,3},{6,7},{1,0},{5,4},{3,2},{7,6},{8,9},{12,13},{10,... | collective-permute-start | bytes 393224 | tf_op jit(solution)/shard_map/ppermute | solution.py:369
  22.9 4.7 %collective-permute-start.11 = (f32[2,128,128]{2,1,0:T(8,128)S(1)}, f32[2,128,128]{2,1,0:T(8,128)S(1)}, u32[]{:S(2)}, u32[]{:S(2)}) collective-permute-start(f32[2,128,128]{2,1,0:T(8,128)S(1)} %get-tuple-element.64.refs_6_), channel_id=1, source_target_pairs={{0,2},{4,6},{2,0},{6,4},{1,8},{5,12},{3,10},{7,14},{8,1},{12,5},{1... | collective-permute-start | bytes 393224 | tf_op jit(solution)/shard_map/ppermute | solution.py:369
  24.0 3.5 %copy-start = (f32[2,1,4,128,128]{4,3,2,1,0:T(8,128)S(1)}, f32[2,1,4,128,128]{4,3,2,1,0:T(8,128)}, u32[]{:S(2)}) copy-start(f32[2,1,4,128,128]{4,3,2,1,0:T(8,128)} %refs_9_.7) | copy-start | bytes 1572868
  24.5 4.8 %collective-permute-start.15 = (f32[2,128,128]{2,1,0:T(8,128)S(1)}, f32[2,128,128]{2,1,0:T(8,128)S(1)}, u32[]{:S(2)}, u32[]{:S(2)}) collective-permute-start(f32[2,128,128]{2,1,0:T(8,128)S(1)} %get-tuple-element.71.refs_5_), channel_id=1, source_target_pairs={{0,1},{4,5},{2,3},{6,7},{1,0},{5,4},{3,2},{7,6},{8,9},{12,13},{10,... | collective-permute-start | bytes 393224 | tf_op jit(solution)/shard_map/ppermute | solution.py:369
  25.7 4.7 %collective-permute-start.16 = (f32[2,128,128]{2,1,0:T(8,128)S(1)}, f32[2,128,128]{2,1,0:T(8,128)S(1)}, u32[]{:S(2)}, u32[]{:S(2)}) collective-permute-start(f32[2,128,128]{2,1,0:T(8,128)S(1)} %get-tuple-element.72.refs_6_), channel_id=1, source_target_pairs={{0,2},{4,6},{2,0},{6,4},{1,8},{5,12},{3,10},{7,14},{8,1},{12,5},{1... | collective-permute-start | bytes 393224 | tf_op jit(solution)/shard_map/ppermute | solution.py:369
  28.1 6.0 %collective-permute-start.18 = (f32[2,128,128]{2,1,0:T(8,128)S(1)}, f32[2,128,128]{2,1,0:T(8,128)S(1)}, u32[]{:S(2)}, u32[]{:S(2)}) collective-permute-start(f32[2,128,128]{2,1,0:T(8,128)S(1)} %get-tuple-element.76.refs_1_), channel_id=1, source_target_pairs={{0,1},{4,5},{2,3},{6,7},{1,0},{5,4},{3,2},{7,6},{8,9},{12,13},{10,... | collective-permute-start | bytes 393224 | tf_op jit(solution)/shard_map/ppermute | solution.py:369
  29.3 4.7 %collective-permute-start.19 = (f32[2,128,128]{2,1,0:T(8,128)S(1)}, f32[2,128,128]{2,1,0:T(8,128)S(1)}, u32[]{:S(2)}, u32[]{:S(2)}) collective-permute-start(f32[2,128,128]{2,1,0:T(8,128)S(1)} %get-tuple-element.77.refs_2_), channel_id=1, source_target_pairs={{0,2},{4,6},{2,0},{6,4},{1,8},{5,12},{3,10},{7,14},{8,1},{12,5},{1... | collective-permute-start | bytes 393224 | tf_op jit(solution)/shard_map/ppermute | solution.py:369
  30.9 4.7 %collective-permute-start.22 = (f32[2,128,128]{2,1,0:T(8,128)S(1)}, f32[2,128,128]{2,1,0:T(8,128)S(1)}, u32[]{:S(2)}, u32[]{:S(2)}) collective-permute-start(f32[2,128,128]{2,1,0:T(8,128)S(1)} %get-tuple-element.83.refs_1_), channel_id=1, source_target_pairs={{0,1},{4,5},{2,3},{6,7},{1,0},{5,4},{3,2},{7,6},{8,9},{12,13},{10,... | collective-permute-start | bytes 393224 | tf_op jit(solution)/shard_map/ppermute | solution.py:369
  31.5 4.7 %collective-permute-start.23 = (f32[2,128,128]{2,1,0:T(8,128)S(1)}, f32[2,128,128]{2,1,0:T(8,128)S(1)}, u32[]{:S(2)}, u32[]{:S(2)}) collective-permute-start(f32[2,128,128]{2,1,0:T(8,128)S(1)} %get-tuple-element.84.refs_2_), channel_id=1, source_target_pairs={{0,2},{4,6},{2,0},{6,4},{1,8},{5,12},{3,10},{7,14},{8,1},{12,5},{1... | collective-permute-start | bytes 393224 | tf_op jit(solution)/shard_map/ppermute | solution.py:369
  31.7 6.3 %collective-permute-start.17 = (f32[2,128,128]{2,1,0:T(8,128)S(1)}, f32[2,128,128]{2,1,0:T(8,128)S(1)}, u32[]{:S(2)}, u32[]{:S(2)}) collective-permute-start(f32[2,128,128]{2,1,0:T(8,128)S(1)} %get-tuple-element.73), channel_id=1, source_target_pairs={{0,6},{4,0},{2,4},{6,2},{1,7},{5,1},{3,5},{7,3},{8,14},{12,8},{10,... | collective-permute-start | bytes 393224 | tf_op jit(solution)/shard_map/ppermute | solution.py:369
  34.5 3.6 %collective-permute-start.20 = (f32[2,128,128]{2,1,0:T(8,128)S(1)}, f32[2,128,128]{2,1,0:T(8,128)S(1)}, u32[]{:S(2)}, u32[]{:S(2)}) collective-permute-start(f32[2,128,128]{2,1,0:T(8,128)S(1)} %get-tuple-element.78.refs_5_), channel_id=1, source_target_pairs={{0,1},{4,5},{2,3},{6,7},{1,0},{5,4},{3,2},{7,6},{8,9},{12,13},{10,... | collective-permute-start | bytes 393224 | tf_op jit(solution)/shard_map/ppermute | solution.py:369
  35.2 4.7 %collective-permute-start.21 = (f32[2,128,128]{2,1,0:T(8,128)S(1)}, f32[2,128,128]{2,1,0:T(8,128)S(1)}, u32[]{:S(2)}, u32[]{:S(2)}) collective-permute-start(f32[2,128,128]{2,1,0:T(8,128)S(1)} %get-tuple-element.79.refs_6_), channel_id=1, source_target_pairs={{0,2},{4,6},{2,0},{6,4},{1,8},{5,12},{3,10},{7,14},{8,1},{12,5},{1... | collective-permute-start | bytes 393224 | tf_op jit(solution)/shard_map/ppermute | solution.py:369
  36.7 4.7 %collective-permute-start.24 = (f32[2,128,128]{2,1,0:T(8,128)S(1)}, f32[2,128,128]{2,1,0:T(8,128)S(1)}, u32[]{:S(2)}, u32[]{:S(2)}) collective-permute-start(f32[2,128,128]{2,1,0:T(8,128)S(1)} %get-tuple-element.86.refs_5_), channel_id=1, source_target_pairs={{0,1},{4,5},{2,3},{6,7},{1,0},{5,4},{3,2},{7,6},{8,9},{12,13},{10,... | collective-permute-start | bytes 393224 | tf_op jit(solution)/shard_map/ppermute | solution.py:369
  38.0 4.7 %collective-permute-start.25 = (f32[2,128,128]{2,1,0:T(8,128)S(1)}, f32[2,128,128]{2,1,0:T(8,128)S(1)}, u32[]{:S(2)}, u32[]{:S(2)}) collective-permute-start(f32[2,128,128]{2,1,0:T(8,128)S(1)} %get-tuple-element.87.refs_6_), channel_id=1, source_target_pairs={{0,2},{4,6},{2,0},{6,4},{1,8},{5,12},{3,10},{7,14},{8,1},{12,5},{1... | collective-permute-start | bytes 393224 | tf_op jit(solution)/shard_map/ppermute | solution.py:369
  40.4 3.7 %collective-permute-start.27 = (f32[2,128,128]{2,1,0:T(8,128)S(1)}, f32[2,128,128]{2,1,0:T(8,128)S(1)}, u32[]{:S(2)}, u32[]{:S(2)}) collective-permute-start(f32[2,128,128]{2,1,0:T(8,128)S(1)} %get-tuple-element.91.refs_1_), channel_id=1, source_target_pairs={{0,1},{4,5},{2,3},{6,7},{1,0},{5,4},{3,2},{7,6},{8,9},{12,13},{10,... | collective-permute-start | bytes 393224 | tf_op jit(solution)/shard_map/ppermute | solution.py:369
  41.4 4.7 %collective-permute-start.28 = (f32[2,128,128]{2,1,0:T(8,128)S(1)}, f32[2,128,128]{2,1,0:T(8,128)S(1)}, u32[]{:S(2)}, u32[]{:S(2)}) collective-permute-start(f32[2,128,128]{2,1,0:T(8,128)S(1)} %get-tuple-element.92.refs_2_), channel_id=1, source_target_pairs={{0,2},{4,6},{2,0},{6,4},{1,8},{5,12},{3,10},{7,14},{8,1},{12,5},{1... | collective-permute-start | bytes 393224 | tf_op jit(solution)/shard_map/ppermute | solution.py:369
  43.3 3.2 %collective-permute-start.32 = (f32[2,128,128]{2,1,0:T(8,128)S(1)}, f32[2,128,128]{2,1,0:T(8,128)S(1)}, u32[]{:S(2)}, u32[]{:S(2)}) collective-permute-start(f32[2,128,128]{2,1,0:T(8,128)S(1)} %get-tuple-element.97.refs_1_), channel_id=1, source_target_pairs={{0,1},{4,5},{2,3},{6,7},{1,0},{5,4},{3,2},{7,6},{8,9},{12,13},{10,... | collective-permute-start | bytes 393224 | tf_op jit(solution)/shard_map/ppermute | solution.py:369
  44.1 4.7 %collective-permute-start.33 = (f32[2,128,128]{2,1,0:T(8,128)S(1)}, f32[2,128,128]{2,1,0:T(8,128)S(1)}, u32[]{:S(2)}, u32[]{:S(2)}) collective-permute-start(f32[2,128,128]{2,1,0:T(8,128)S(1)} %get-tuple-element.98.refs_2_), channel_id=1, source_target_pairs={{0,2},{4,6},{2,0},{6,4},{1,8},{5,12},{3,10},{7,14},{8,1},{12,5},{1... | collective-permute-start | bytes 393224 | tf_op jit(solution)/shard_map/ppermute | solution.py:369
  49.2 2.5 %collective-permute-start.34 = (f32[2,128,128]{2,1,0:T(8,128)S(1)}, f32[2,128,128]{2,1,0:T(8,128)S(1)}, u32[]{:S(2)}, u32[]{:S(2)}) collective-permute-start(f32[2,128,128]{2,1,0:T(8,128)S(1)} %get-tuple-element.100.psi_a), channel_id=1, source_target_pairs={{0,1},{4,5},{2,3},{6,7},{1,0},{5,4},{3,2},{7,6},{8,9},{12,13},{10,... | collective-permute-start | bytes 393224 | tf_op jit(solution)/shard_map/ppermute | solution.py:369
  49.7 4.7 %collective-permute-start.35 = (f32[2,128,128]{2,1,0:T(8,128)S(1)}, f32[2,128,128]{2,1,0:T(8,128)S(1)}, u32[]{:S(2)}, u32[]{:S(2)}) collective-permute-start(f32[2,128,128]{2,1,0:T(8,128)S(1)} %get-tuple-element.101.psi_b), channel_id=1, source_target_pairs={{0,2},{4,6},{2,0},{6,4},{1,8},{5,12},{3,10},{7,14},{8,1},{12,5},{1... | collective-permute-start | bytes 393224 | tf_op jit(solution)/shard_map/ppermute | solution.py:369
  49.7 5.1 %collective-permute-start.29 = (f32[2,128,128]{2,1,0:T(8,128)S(1)}, f32[2,128,128]{2,1,0:T(8,128)S(1)}, u32[]{:S(2)}, u32[]{:S(2)}) collective-permute-start(f32[2,128,128]{2,1,0:T(8,128)S(1)} %get-tuple-element.93.psi_a), channel_id=1, source_target_pairs={{0,1},{4,5},{2,3},{6,7},{1,0},{5,4},{3,2},{7,6},{8,9},{12,13},{10,... | collective-permute-start | bytes 393224 | tf_op jit(solution)/shard_map/ppermute | solution.py:369
  51.7 4.7 %collective-permute-start.30 = (f32[2,128,128]{2,1,0:T(8,128)S(1)}, f32[2,128,128]{2,1,0:T(8,128)S(1)}, u32[]{:S(2)}, u32[]{:S(2)}) collective-permute-start(f32[2,128,128]{2,1,0:T(8,128)S(1)} %get-tuple-element.94.psi_b), channel_id=1, source_target_pairs={{0,2},{4,6},{2,0},{6,4},{1,8},{5,12},{3,10},{7,14},{8,1},{12,5},{1... | collective-permute-start | bytes 393224 | tf_op jit(solution)/shard_map/ppermute | solution.py:369
  51.7 8.1 %collective-permute-start.26 = (f32[1,2,128,128]{3,2,1,0:T(8,128)S(1)}, f32[1,2,128,128]{3,2,1,0:T(8,128)S(1)}, u32[]{:S(2)}, u32[]{:S(2)}) collective-permute-start(f32[1,2,128,128]{3,2,1,0:T(8,128)S(1)} %bitcast.5), channel_id=1, source_target_pairs={{0,3},{4,0},{2,1},{6,2},{1,7},{5,4},{3,5},{7,6},{8,11},{12,8},{10,... | collective-permute-start | bytes 393224 | tf_op jit(solution)/shard_map/ppermute | solution.py:369
  54.4 8.2 %collective-permute-start.36 = (f32[2,128,128]{2,1,0:T(8,128)S(1)}, f32[2,128,128]{2,1,0:T(8,128)S(1)}, u32[]{:S(2)}, u32[]{:S(2)}) collective-permute-start(f32[2,128,128]{2,1,0:T(8,128)S(1)} %shard_map.92), channel_id=1, source_target_pairs={{0,3},{4,0},{2,1},{6,2},{1,7},{5,4},{3,5},{7,6},{8,11},{12,8},{10,... | collective-permute-start | bytes 393224 | tf_op jit(solution)/shard_map/ppermute | solution.py:369
  56.5 7.5 %collective-permute-start.31 = (f32[2,128,128]{2,1,0:T(8,128)S(1)}, f32[2,128,128]{2,1,0:T(8,128)S(1)}, u32[]{:S(2)}, u32[]{:S(2)}) collective-permute-start(f32[2,128,128]{2,1,0:T(8,128)S(1)} %shard_map.90), channel_id=1, source_target_pairs={{0,3},{4,0},{2,1},{6,2},{1,7},{5,4},{3,5},{7,6},{8,11},{12,8},{10,... | collective-permute-start | bytes 393224 | tf_op jit(solution)/shard_map/ppermute | solution.py:369

commit v3 on v2

--- a/solution.py
+++ b/solution.py
@@ -41,10 +41,6 @@
             self.chip.append((at(s, p), at(t, p) if 0 <= t < slabs else at(s, (p + 2) % groups)))
         self.field = [(at(s, p), at(s, (p - 1) % groups)) for s, p in every]
         self.enter = [(s * groups + g, at(s, (g - 1) % groups)) for s, g in every]
-        self.guess = []
-        for s, g in every:
-            there = s + 1 if s % 2 == 0 else (s - 1 if g % 2 else (s + 1) % slabs)
-            self.guess.append((s * groups + g, there * groups + g))
 
     def at(self, s, p):
         return (2 * (s // 2) + p % 2) * self.groups + 2 * (p // 2) + s % 2
@@ -209,41 +205,43 @@
 def dirichlet_kernel(lo, start, enter, fresh, out_native, *refs):
     refs = list(refs)
     take = lambda n: [refs.pop(0) for _ in range(n)]
-    coef, end = take(2)
+    coef, end, field = take(3)
     parity, _, position = place()
     far = has_far()
-    (field,) = take(1)
+    if lo:
+        (before,) = take(1)
     if start:
         held, from_core, from_chip = take(3)
     else:
         old_a, old_b, psi_a, psi_b, got_a, got_b, ng, gy = take(8)
     out_field, out_qa, out_qb, out_ha, out_hb, va, vb, hold = take(8)
     planes = va.shape[0]
-    steps = out_qa.shape[0]
-    ny = out_qa.shape[1]
+    steps, ny, _ = out_qb.shape
     clear_pads((va, vb))
     for p in range(planes):
-        if enter:
-            value = field[0, flipped(p, planes, parity)]
-        else:
-            value = field[p]
+        value = field[0, flipped(p, planes, parity)] if enter else field[p]
         va[p, PAD : PAD + ny, :] = value
+    for n in range(lo):
+        out_qa[n] = before[n]
     for n in range(steps):
         if start:
-            h_a = jnp.where(parity == 0, held[n], from_core[n])
-            h_b = jnp.where(parity == 0, from_chip[n], held[n])
+            h_a = jnp.where(parity == 0, held[0, 0, lo + n], from_core[0, 0, lo + n])
+            h_b = jnp.where(parity == 0, from_chip[n], held[0, 0, lo + n])
         else:
-            h_a = old_a[n] + 0.25 * (psi_a[n] + got_a[n])
+            h_a = old_a[n] + 0.25 * (psi_a[lo + n] + got_a[lo + n])
             h_b = old_b[n] + 0.25 * (psi_b[n] + got_b[n])
             groups = lax.axis_size("iter")
-            begins = (-fresh - 1) % groups
+            begins = (-1 - fresh) % groups
             new = position == begins
             local, crossed = ng[fresh - 1, 0, lo + n], gy[lo + n]
-            near_a, near_b = (crossed, local) if begins % 2 else (local, crossed)
-            h_a = jnp.where(new, near_a, h_a)
             if begins % 2:
-                near_b = jnp.where(parity == 1, near_b, got_b[n])
-            h_b = jnp.where(new, near_b, h_b)
+                new_a = jnp.where(parity == 0, crossed, got_a[lo + n])
+                new_b = jnp.where(parity == 1, local, got_b[n])
+            else:
+                new_a = local
+                new_b = jnp.where(parity == 1, crossed, got_b[n])
+            h_a = jnp.where(new, new_a, h_a)
+            h_b = jnp.where(new, new_b, h_b)
         out_ha[n] = h_a
         out_hb[n] = jnp.where(far, h_b, 0.0)
     buffers = [va, vb]
@@ -261,7 +259,7 @@
             if p == 0:
                 out_qb[n, here, :] = end[0, here, :] * (value - out_hb[n, here, :])
             if p == planes - 1:
-                out_qa[n, here, :] = end[1, here, :] * (value - out_ha[n, here, :])
+                out_qa[lo + n, here, :] = end[1, here, :] * (value - out_ha[n, here, :])
 
         buffers = solve(coef, buffers, hold, first_rhs, final)
     for p in range(planes):
@@ -272,28 +270,29 @@
             out_field[p] = value
 
 
-def neumann_kernel(lo, first, more, fresh, *refs):
+def neumann_kernel(lo, more, fresh, *refs):
     refs = list(refs)
     take = lambda n: [refs.pop(0) for _ in range(n)]
-    (coef,) = take(1)
+    coef, q_a, q_b, got_a, got_b = take(5)
     _, _, position = place()
-    q_a, q_b, got_a, got_b = take(4)
-    if not first:
-        (state,) = take(1)
+    if lo:
+        state, before = take(2)
     if fresh:
-        (ng,) = take(1)
+        ng, gy = take(2)
     if more:
         (out_state,) = take(1)
     out_a, out_b, va, vb, hold = take(5)
     planes = va.shape[0]
-    steps, ny, nz = out_a.shape
+    steps, ny, nz = out_b.shape
     clear_pads((va, vb))
-    if not first:
+    if lo:
         for p in range(planes):
             va[p, PAD : PAD + ny, :] = state[p]
+        for n in range(lo):
+            out_a[n] = before[n]
     buffers = [va, vb]
     for n in range(steps):
-        zero = first and n == 0
+        zero = lo == 0 and n == 0
 
         def first_rhs(p, here, x):
             value = jnp.zeros((8, nz), F32) if zero else coef[row_cap(p), here, :] * x
@@ -301,7 +300,7 @@
                 jump = q_b[n, here, :] + got_b[n, here, :]
                 value = value + coef[row_end(planes, 0), here, :] * jump
             if p == planes - 1:
-                jump = q_a[n, here, :] + got_a[n, here, :]
+                jump = q_a[lo + n, here, :] + got_a[lo + n, here, :]
                 value = value + coef[row_end(planes, 1), here, :] * jump
             return value
 
@@ -309,7 +308,7 @@
             if p == 0:
                 out_b[n, here, :] = value
             if p == planes - 1:
-                out_a[n, here, :] = value
+                out_a[lo + n, here, :] = value
 
         buffers = solve(coef, buffers, hold, first_rhs, final, known_zero=zero)
     if more:
@@ -317,25 +316,31 @@
             out_state[p] = buffers[0][p, PAD : PAD + ny, :]
     if fresh:
         groups = lax.axis_size("iter")
-        begins = (-fresh - 1) % groups
+        begins = (-1 - fresh) % groups
 
         @pl.when(position == begins)
         def _():
             for n in range(steps):
-                out_b[n] = ng[fresh - 1, 0, lo + n]
-
-
-def correct_kernel(h_a, h_b, psi_a, psi_b, got_a, got_b, out):
+                if begins % 2:
+                    out_a[lo + n] = gy[lo + n]
+                    out_b[n] = ng[fresh - 1, 0, lo + n]
+                else:
+                    out_b[n] = gy[lo + n]
+
+
+def correct_kernel(lo, h_a, h_b, psi_a, psi_b, got_a, got_b, out):
     parity, _, _ = place()
     far = has_far()
 
     @pl.when(parity == 0)
     def _():
-        out[...] = h_a[...] + 0.25 * (psi_a[...] + got_a[...])
+        for n in range(out.shape[0]):
+            out[n] = h_a[n] + 0.25 * (psi_a[lo + n] + got_a[lo + n])
 
     @pl.when(parity == 1)
     def _():
-        out[...] = jnp.where(far, h_b[...] + 0.25 * (psi_b[...] + got_b[...]), 0.0)
+        for n in range(out.shape[0]):
+            out[n] = jnp.where(far, h_b[n] + 0.25 * (psi_b[n] + got_b[n]), 0.0)
 
 
 def cut_kernel(whole, *outs):
@@ -346,7 +351,41 @@
         lo += out.shape[0]
 
 
-def run(kernel, outs, args, scratch=(), smem=0):
+def pick_kernel(picks, guess, *messages):
+    even = lax.rem(lax.axis_index("iter"), 2)
+    for (for_odd, for_even), message in zip(picks, messages):
+        for parity, tick in ((0, for_odd), (1, for_even)):
+
+            @pl.when(even == parity)
+            def _():
+                message[...] = guess[tick - 1, 0]
+
+
+def land_kernel(*refs):
+    *pieces, out, sem = refs
+    copies = []
+    lo = 0
+    for n, piece in enumerate(pieces):
+        copies.append(pltpu.make_async_copy(piece, out.at[lo : lo + piece.shape[0]], sem.at[n]))
+        copies[-1].start()
+        lo += piece.shape[0]
+    for copy in copies:
+        copy.wait()
+
+
+def land(pieces):
+    shape = (sum(piece.shape[0] for piece in pieces),) + pieces[0].shape[1:]
+    return pl.pallas_call(
+        land_kernel,
+        out_shape=jax.ShapeDtypeStruct(shape, F32),
+        in_specs=[pl.BlockSpec(memory_space=pltpu.VMEM)] * len(pieces),
+        out_specs=pl.BlockSpec(memory_space=pl.ANY),
+        scratch_shapes=[pltpu.SemaphoreType.DMA((len(pieces),))],
+        compiler_params=pltpu.CompilerParams(vmem_limit_bytes=LIMIT),
+    )(*[near(piece) for piece in pieces])
+
+
+def run(kernel, outs, args, scratch=(), smem=0, bring=True):
     specs = [pl.BlockSpec(memory_space=pltpu.SMEM)] * smem
     specs += [pl.BlockSpec(memory_space=pltpu.VMEM)] * (len(args) - smem)
     many = isinstance(outs, tuple)
@@ -357,7 +396,7 @@
         out_specs=tuple([pl.BlockSpec(memory_space=pltpu.VMEM)] * len(outs)) if many else specs[-1],
         scratch_shapes=list(scratch),
         compiler_params=pltpu.CompilerParams(vmem_limit_bytes=LIMIT),
-    )(*args[:smem], *[near(a) for a in args[smem:]])
+    )(*args[:smem], *[near(a) if bring else a for a in args[smem:]])
 
 
 def local(layout, fields, labels, traces, new_guess, cond_table, cap_table):
@@ -372,17 +411,18 @@
     steps = traces.shape[2]
     ticks = new_guess.shape[0] + 1
     groups = layout.groups
-    odd = lax.rem(lax.axis_index("sub"), 2)
     chunks = cuts(steps)
     scratch = [vmem((planes, ny + 2 * PAD, nz))] * 2 + [vmem((planes, ny, nz))]
 
     held = move(traces, layout.enter)
     labels = move(labels, layout.enter)
     field = move(fields, layout.enter)
-    pieces = run(cut_kernel, tuple(vmem((hi - lo, ny, nz)) for lo, hi in chunks), [held])
-    waves = {}
-    for (lo, hi), piece in zip(chunks, pieces):
-        waves[lo] = (piece, move(piece, layout.core), move(piece, layout.chip))
+    if len(chunks) > 1:
+        pieces = run(cut_kernel, tuple(vmem((hi - lo, ny, nz)) for lo, hi in chunks), [held])
+    else:
+        pieces = [held[0, 0]]
+    from_chip = {lo: move(piece, layout.chip) for (lo, _), piece in zip(chunks, pieces)}
+    from_core = move(held, layout.core)
     count = rows(planes)
     dir_coef, neu_coef, end = run(
         setup_kernel,
@@ -391,54 +431,61 @@
         smem=2,
     )
 
-    starts = {t: (-t - 1) % groups for t in range(1, ticks)}
+    starts = {t: (-1 - t) % groups for t in range(1, ticks)}
     odds = [t for t in starts if starts[t] % 2]
     evens = [t for t in starts if starts[t] % 2 == 0]
+    picks = []
+    for n in range(max(len(odds), len(evens))):
+        picks.append((odds[n] if n < len(odds) else evens[n], evens[n] if n < len(evens) else odds[n]))
     crossed = {}
-    for n in range(max(len(odds), len(evens))):
-        ours = odds[n] if n < len(odds) else evens[n]
-        theirs = evens[n] if n < len(evens) else odds[n]
-        message = jnp.where(odd == 0, new_guess[ours - 1, 0], new_guess[theirs - 1, 0])
-        arrived = move(message, layout.guess)
-        crossed[ours] = crossed[theirs] = arrived
-
+    messages = run(functools.partial(pick_kernel, picks), tuple(vmem((steps, ny, nz)) for _ in picks), [new_guess])
+    for served, message in zip(picks, messages):
+        arrived = move(message, layout.enter)
+        for t in served:
+            crossed[t] = arrived
+
+    waves = {}
     for tick in range(ticks):
         last = tick == ticks - 1
         sent = []
+        q_a = None
         for lo, hi in chunks:
             plane = vmem((hi - lo, ny, nz))
+            traces_in = [held, from_core, from_chip[lo]] if tick == 0 else [*waves[lo], new_guess, crossed[tick]]
             field, q_a, q_b, h_a, h_b = run(
                 functools.partial(dirichlet_kernel, lo, tick == 0, tick == 0 and lo == 0, tick, last and hi == steps),
-                (vmem((planes, ny, nz)), plane, plane, plane, plane),
-                [dir_coef, end, field, *waves[lo]] + ([new_guess, crossed[tick]] if tick else []),
+                (vmem((planes, ny, nz)), vmem((hi, ny, nz)), plane, plane, plane),
+                [dir_coef, end, field] + ([q_a] if lo else []) + traces_in,
                 scratch,
             )
-            in_a, in_b = move(q_a, layout.core), move(q_b, layout.chip)
-            sent.append((q_a, q_b, in_a, in_b, h_a, h_b))
+            sent.append((q_b, move(q_b, layout.chip), h_a, h_b))
+        in_a = move(q_a, layout.core)
         if last:
-            field = move(field[None], layout.home(ticks))
+            field = move(field, layout.home(ticks))
         else:
             field = move(field, layout.field)
         fresh = 0 if last else tick + 1
         state = []
-        ends = []
-        for n, ((lo, hi), (q_a, q_b, in_a, in_b, h_a, h_b)) in enumerate(zip(chunks, sent)):
+        psi = []
+        for (lo, hi), (q_b, in_b, h_a, h_b) in zip(chunks, sent):
             plane = vmem((hi - lo, ny, nz))
-            more = n + 1 < len(chunks)
-            swap = fresh if fresh and starts[fresh] % 2 else 0
+            more = hi < steps
             *state, psi_a, psi_b = run(
-                functools.partial(neumann_kernel, lo, lo == 0, more, swap),
-                ((vmem((planes, ny, nz)),) if more else ()) + (plane, plane),
-                [neu_coef, q_a, q_b, in_a, in_b, *state] + ([new_guess] if swap else []),
+                functools.partial(neumann_kernel, lo, more, fresh),
+                ((vmem((planes, ny, nz)),) if more else ()) + (vmem((hi, ny, nz)), plane),
+                [neu_coef, q_a, q_b, in_a, in_b] + (state + [psi_a] if lo else []) + ([new_guess, crossed[fresh]] if fresh else []),
                 scratch,
             )
-            in_a, in_b = move(psi_a, layout.core), move(psi_b, layout.chip)
-            waves[lo] = (h_a, h_b, psi_a, psi_b, in_a, in_b)
+            psi.append((psi_b, move(psi_b, layout.chip), h_a, h_b))
+        got_a = move(psi_a, layout.core)
+        ends = []
+        for (lo, hi), (psi_b, got_b, h_a, h_b) in zip(chunks, psi):
+            waves[lo] = (h_a, h_b, psi_a, psi_b, got_a, got_b)
             if last:
-                done = run(correct_kernel, plane, list(waves[lo]))
+                plane = vmem((hi - lo, ny, nz))
+                done = run(functools.partial(correct_kernel, lo), plane, list(waves[lo]))
                 ends.append(move(done, layout.home(ticks)))
-    corrected = ends[0] if len(ends) == 1 else jnp.concatenate(ends, axis=0)
-    return field, corrected[None, None]
+    return land([field])[None], land(ends)[None, None]
 
 
 def cuts(steps):

time: 65.4 us -> 75.3 us (1.15)
  waiting for transfers between devices: 25.5 us -> 35.9 us
  other arithmetic: 1.78 us -> 0 us
  Pallas kernels: 6.94 us -> 8.48 us
    ppermute x37 -> x30, waiting for transfers between devices: 25.5 us -> 35.9 us  [move(): return lax.ppermute(value, AXES, pairs)]
    pallas_call x0 -> x2, Pallas kernels: none -> 1.38 us  [land(): pl.pallas_call(land_kernel, out_shape=jax.ShapeDtypeStruct(shape, F32), i...]
    select_n x1 -> x0, other arithmetic: 1.06 us -> none  [steps_of(): jnp.where(odd == 0, new_guess[ours - 1, 0], new_guess[theirs - 1, 0])]
    ppermute x37 -> x30, starting transfers between devices: 29.6 us -> 28.9 us  [move(): return lax.ppermute(value, AXES, pairs)]
    pallas_call x16 -> x17, Pallas kernels: 6.94 us -> 7.11 us  [run(): pl.pallas_call(kernel, out_shape=outs, in_specs=specs, out_specs=tuple([p...]
  transfers between devices with their start and end apart: 37 -> 30, of which waited for: 15 -> 18; matrix products, arithmetic and copies ran while one was open for 2% -> 0% of each run, Pallas kernels for 10% -> 7%
where the time goes in v3:
time: 75.3 us; the launch traced here: 75.2 us
  waiting for transfers between devices  35.9 us (48%)
  starting transfers between devices  28.9 us (38%)
  Pallas kernels  8.48 us (11%)
  local copies, waits for them, and re-layouts  1.05 us (1%)
  between operations  0.8 us (1%)
    ppermute x30, waiting for transfers between devices, move(): return lax.ppermute(value, AXES, pairs)  35.9 us
    ppermute x30, starting transfers between devices, move(): return lax.ppermute(value, AXES, pairs)  28.9 us
    pallas_call x17, Pallas kernels, run(): pl.pallas_call(kernel, out_shape=outs, in_specs=specs, out_specs=tuple([p...  7.11 us
  transfers between devices with their start and end apart: 30, of which 18 were waited for; matrix products, arithmetic and copies ran while one was open for 0% of the time, Pallas kernels for 7%

profile of v3, /device:TPU:1, one launch (start us, length us, event | category | flops | bytes accessed | tf_op | source)
XLA Modules:
  0.0 75.2 jit_solution(4798568565795697244)
XLA Ops:
  0.7 6.0 %collective-permute-done.2.whole.refs_3_.refs_4_ = f32[1,1,4,128,128]{4,3,2,1,0:T(8,128)S(1)} collective-permute-done((f32[1,1,4,128,128]{4,3,2,1,0:T(8,128)}, f32[1,1,4,128,128]{4,3,2,1,0:T(8,128)S(1)}, u32[]{:S(2)}, u32[]{:S(2)}) %collective-permute-start.2) | collective-permute-done | bytes 262176 | tf_op jit(solution)/shard_map/ppermute | solution.py:408
  6.7 2.1 %collective-permute-start.3 = (f32[1,1,4,128,128]{4,3,2,1,0:T(8,128)S(1)}, f32[1,1,4,128,128]{4,3,2,1,0:T(8,128)S(1)}, u32[]{:S(2)}, u32[]{:S(2)}) collective-permute-start(f32[1,1,4,128,128]{4,3,2,1,0:T(8,128)S(1)} %collective-permute-done.2.whole.refs_3_.refs_4_), channel_id=1, source_target_pairs={{0,1},{4,5},{2,3},{6,7},{1,0},{5,4},{3,2},{7,6},{8,9},{12,13},{10,... | collective-permute-start | bytes 786440 | tf_op jit(solution)/shard_map/ppermute | solution.py:408
  8.8 3.3 %collective-permute-start.1 = (f32[1,2,128,128]{3,2,1,0:T(8,128)}, f32[1,2,128,128]{3,2,1,0:T(8,128)S(1)}, u32[]{:S(2)}, u32[]{:S(2)}) collective-permute-start(f32[1,2,128,128]{3,2,1,0:T(8,128)} %param.6), channel_id=1, source_target_pairs={{0,6},{1,0},{2,4},{3,2},{4,7},{5,1},{6,5},{7,3},{8,14},{9,8},{10,1... | collective-permute-start | bytes 393224 | tf_op jit(solution)/shard_map/ppermute | solution.py:408
  12.1 1.9 %collective-permute-start.4 = (f32[2,128,128]{2,1,0:T(8,128)S(1)}, f32[2,128,128]{2,1,0:T(8,128)S(1)}, u32[]{:S(2)}, u32[]{:S(2)}) collective-permute-start(f32[2,128,128]{2,1,0:T(8,128)S(1)} %get-tuple-element.54), channel_id=1, source_target_pairs={{0,2},{4,6},{2,0},{6,4},{1,8},{5,12},{3,10},{7,14},{8,1},{12,5},{1... | collective-permute-start | bytes 393224 | tf_op jit(solution)/shard_map/ppermute | solution.py:408
  14.1 1.0 %copy-done = f32[2,1,4,128,128]{4,3,2,1,0:T(8,128)S(1)} copy-done((f32[2,1,4,128,128]{4,3,2,1,0:T(8,128)S(1)}, f32[2,1,4,128,128]{4,3,2,1,0:T(8,128)}, u32[]{:S(2)}) %copy-start) | copy-done | bytes 524312
  15.2 0.8 %collective-permute-start.10 = (f32[4,128,128]{2,1,0:T(8,128)S(1)}, f32[4,128,128]{2,1,0:T(8,128)S(1)}, u32[]{:S(2)}, u32[]{:S(2)}) collective-permute-start(f32[4,128,128]{2,1,0:T(8,128)S(1)} %shard_map.81), channel_id=1, source_target_pairs={{0,6},{1,0},{2,4},{3,2},{4,7},{5,1},{6,5},{7,3},{8,14},{9,8},{10,1... | collective-permute-start | bytes 786440 | tf_op jit(solution)/shard_map/ppermute | solution.py:408
  16.0 0.9 %shard_map.77 = (f32[14,128,128]{2,1,0:T(8,128)S(1)}, f32[14,128,128]{2,1,0:T(8,128)S(1)}, f32[2,128,128]{2,1,0:T(8,128)S(1)}) custom-call(f32[4]{0:T(128)S(1)} %copy-done.2, f32[4]{0:T(128)S(1)} %copy-done.3, s32[2,128,128]{2,1,0:T(8,128)S(1)} %collective-permute-done.label_ref), custom_call_target="tpu_custom_call" | custom-call | tf_op jit(solution)/shard_map/pallas_call | solution.py:392
  17.0 0.6 shard_map.79
  17.6 1.1 %collective-permute-done.5.refs_6_ = f32[2,128,128]{2,1,0:T(8,128)S(1)} collective-permute-done((f32[2,128,128]{2,1,0:T(8,128)S(1)}, f32[2,128,128]{2,1,0:T(8,128)S(1)}, u32[]{:S(2)}, u32[]{:S(2)}) %collective-permute-start.5) | collective-permute-done | bytes 131104 | tf_op jit(solution)/shard_map/ppermute | solution.py:408
  18.7 0.5 shard_map.80
  19.2 1.6 %collective-permute-start.7 = (f32[4,128,128]{2,1,0:T(8,128)S(1)}, f32[4,128,128]{2,1,0:T(8,128)S(1)}, u32[]{:S(2)}, u32[]{:S(2)}) collective-permute-start(f32[4,128,128]{2,1,0:T(8,128)S(1)} %get-tuple-element.62.refs_1_), channel_id=1, source_target_pairs={{0,1},{4,5},{2,3},{6,7},{1,0},{5,4},{3,2},{7,6},{8,9},{12,13},{10,... | collective-permute-start | bytes 786440 | tf_op jit(solution)/shard_map/ppermute | solution.py:408
  20.8 0.9 %collective-permute-start.9 = (f32[2,128,128]{2,1,0:T(8,128)S(1)}, f32[2,128,128]{2,1,0:T(8,128)S(1)}, u32[]{:S(2)}, u32[]{:S(2)}) collective-permute-start(f32[2,128,128]{2,1,0:T(8,128)S(1)} %get-tuple-element.64.refs_2_), channel_id=1, source_target_pairs={{0,2},{4,6},{2,0},{6,4},{1,8},{5,12},{3,10},{7,14},{8,1},{12,5},{1... | collective-permute-start | bytes 393224 | tf_op jit(solution)/shard_map/ppermute | solution.py:408
  21.7 0.9 %collective-permute-start.8 = (f32[2,128,128]{2,1,0:T(8,128)S(1)}, f32[2,128,128]{2,1,0:T(8,128)S(1)}, u32[]{:S(2)}, u32[]{:S(2)}) collective-permute-start(f32[2,128,128]{2,1,0:T(8,128)S(1)} %get-tuple-element.63.refs_2_), channel_id=1, source_target_pairs={{0,2},{4,6},{2,0},{6,4},{1,8},{5,12},{3,10},{7,14},{8,1},{12,5},{1... | collective-permute-start | bytes 393224 | tf_op jit(solution)/shard_map/ppermute | solution.py:408
  22.6 2.9 %collective-permute-done.9.refs_4_ = f32[2,128,128]{2,1,0:T(8,128)S(1)} collective-permute-done((f32[2,128,128]{2,1,0:T(8,128)S(1)}, f32[2,128,128]{2,1,0:T(8,128)S(1)}, u32[]{:S(2)}, u32[]{:S(2)}) %collective-permute-start.9) | collective-permute-done | bytes 131104 | tf_op jit(solution)/shard_map/ppermute | solution.py:408
  25.9 0.9 %collective-permute-done.8.refs_4_ = f32[2,128,128]{2,1,0:T(8,128)S(1)} collective-permute-done((f32[2,128,128]{2,1,0:T(8,128)S(1)}, f32[2,128,128]{2,1,0:T(8,128)S(1)}, u32[]{:S(2)}, u32[]{:S(2)}) %collective-permute-start.8) | collective-permute-done | bytes 131104 | tf_op jit(solution)/shard_map/ppermute | solution.py:408
  26.9 0.5 shard_map.83
  27.8 1.1 %collective-permute-start.6 = (f32[2,128,128]{2,1,0:T(8,128)S(1)}, f32[2,128,128]{2,1,0:T(8,128)S(1)}, u32[]{:S(2)}, u32[]{:S(2)}) collective-permute-start(f32[2,128,128]{2,1,0:T(8,128)S(1)} %get-tuple-element.58), channel_id=1, source_target_pairs={{0,6},{4,0},{2,4},{6,2},{1,7},{5,1},{3,5},{7,3},{8,14},{12,8},{10,... | collective-permute-start | bytes 393224 | tf_op jit(solution)/shard_map/ppermute | solution.py:408
  29.0 1.7 %collective-permute-start.13 = (f32[2,128,128]{2,1,0:T(8,128)S(1)}, f32[2,128,128]{2,1,0:T(8,128)S(1)}, u32[]{:S(2)}, u32[]{:S(2)}) collective-permute-start(f32[2,128,128]{2,1,0:T(8,128)S(1)} %get-tuple-element.73.refs_7_), channel_id=1, source_target_pairs={{0,2},{4,6},{2,0},{6,4},{1,8},{5,12},{3,10},{7,14},{8,1},{12,5},{1... | collective-permute-start | bytes 393224 | tf_op jit(solution)/shard_map/ppermute | solution.py:408
  30.7 2.1 %collective-permute-done.6.refs_2_ = f32[2,128,128]{2,1,0:T(8,128)S(1)} collective-permute-done((f32[2,128,128]{2,1,0:T(8,128)S(1)}, f32[2,128,128]{2,1,0:T(8,128)S(1)}, u32[]{:S(2)}, u32[]{:S(2)}) %collective-permute-start.6) | collective-permute-done | bytes 131104 | tf_op jit(solution)/shard_map/ppermute | solution.py:408
  32.8 0.9 %collective-permute-done.12.refs_8_ = f32[2,128,128]{2,1,0:T(8,128)S(1)} collective-permute-done((f32[2,128,128]{2,1,0:T(8,128)S(1)}, f32[2,128,128]{2,1,0:T(8,128)S(1)}, u32[]{:S(2)}, u32[]{:S(2)}) %collective-permute-start.12) | collective-permute-done | bytes 131104 | tf_op jit(solution)/shard_map/ppermute | solution.py:408
  33.6 0.5 shard_map.84
  34.2 0.8 %collective-permute-done.13.refs_9_ = f32[2,128,128]{2,1,0:T(8,128)S(1)} collective-permute-done((f32[2,128,128]{2,1,0:T(8,128)S(1)}, f32[2,128,128]{2,1,0:T(8,128)S(1)}, u32[]{:S(2)}, u32[]{:S(2)}) %collective-permute-start.13) | collective-permute-done | bytes 131104 | tf_op jit(solution)/shard_map/ppermute | solution.py:408
  35.0 0.5 shard_map.85
  35.6 1.6 %collective-permute-start.15 = (f32[4,128,128]{2,1,0:T(8,128)S(1)}, f32[4,128,128]{2,1,0:T(8,128)S(1)}, u32[]{:S(2)}, u32[]{:S(2)}) collective-permute-start(f32[4,128,128]{2,1,0:T(8,128)S(1)} %get-tuple-element.77.refs_1_), channel_id=1, source_target_pairs={{0,1},{4,5},{2,3},{6,7},{1,0},{5,4},{3,2},{7,6},{8,9},{12,13},{10,... | collective-permute-start | bytes 786440 | tf_op jit(solution)/shard_map/ppermute | solution.py:408
  37.2 1.1 %collective-permute-start.17 = (f32[2,128,128]{2,1,0:T(8,128)S(1)}, f32[2,128,128]{2,1,0:T(8,128)S(1)}, u32[]{:S(2)}, u32[]{:S(2)}) collective-permute-start(f32[2,128,128]{2,1,0:T(8,128)S(1)} %get-tuple-element.79.refs_2_), channel_id=1, source_target_pairs={{0,2},{4,6},{2,0},{6,4},{1,8},{5,12},{3,10},{7,14},{8,1},{12,5},{1... | collective-permute-start | bytes 393224 | tf_op jit(solution)/shard_map/ppermute | solution.py:408
  38.2 0.7 collective-permute-start.16
  38.9 2.9 %collective-permute-done.17.refs_4_ = f32[2,128,128]{2,1,0:T(8,128)S(1)} collective-permute-done((f32[2,128,128]{2,1,0:T(8,128)S(1)}, f32[2,128,128]{2,1,0:T(8,128)S(1)}, u32[]{:S(2)}, u32[]{:S(2)}) %collective-permute-start.17) | collective-permute-done | bytes 131104 | tf_op jit(solution)/shard_map/ppermute | solution.py:408
  42.3 0.9 %collective-permute-done.16.refs_4_ = f32[2,128,128]{2,1,0:T(8,128)S(1)} collective-permute-done((f32[2,128,128]{2,1,0:T(8,128)S(1)}, f32[2,128,128]{2,1,0:T(8,128)S(1)}, u32[]{:S(2)}, u32[]{:S(2)}) %collective-permute-start.16) | collective-permute-done | bytes 131104 | tf_op jit(solution)/shard_map/ppermute | solution.py:408
  44.4 1.4 %collective-permute-start.19 = (f32[2,128,128]{2,1,0:T(8,128)S(1)}, f32[2,128,128]{2,1,0:T(8,128)S(1)}, u32[]{:S(2)}, u32[]{:S(2)}) collective-permute-start(f32[2,128,128]{2,1,0:T(8,128)S(1)} %get-tuple-element.83.refs_6_), channel_id=1, source_target_pairs={{0,2},{4,6},{2,0},{6,4},{1,8},{5,12},{3,10},{7,14},{8,1},{12,5},{1... | collective-permute-start | bytes 393224 | tf_op jit(solution)/shard_map/ppermute | solution.py:408
  46.2 3.0 %collective-permute-done.14.refs_2_ = f32[2,128,128]{2,1,0:T(8,128)S(1)} collective-permute-done((f32[2,128,128]{2,1,0:T(8,128)S(1)}, f32[2,128,128]{2,1,0:T(8,128)S(1)}, u32[]{:S(2)}, u32[]{:S(2)}) %collective-permute-start.14) | collective-permute-done | bytes 131104 | tf_op jit(solution)/shard_map/ppermute | solution.py:408
  49.1 0.6 shard_map.88
  49.7 0.8 %collective-permute-done.20.refs_9_ = f32[2,128,128]{2,1,0:T(8,128)S(1)} collective-permute-done((f32[2,128,128]{2,1,0:T(8,128)S(1)}, f32[2,128,128]{2,1,0:T(8,128)S(1)}, u32[]{:S(2)}, u32[]{:S(2)}) %collective-permute-start.20) | collective-permute-done | bytes 131104 | tf_op jit(solution)/shard_map/ppermute | solution.py:408
  50.5 0.6 shard_map.89
  51.1 2.1 %collective-permute-start.22 = (f32[4,128,128]{2,1,0:T(8,128)S(1)}, f32[4,128,128]{2,1,0:T(8,128)S(1)}, u32[]{:S(2)}, u32[]{:S(2)}) collective-permute-start(f32[4,128,128]{2,1,0:T(8,128)S(1)} %get-tuple-element.92.refs_1_), channel_id=1, source_target_pairs={{0,1},{4,5},{2,3},{6,7},{1,0},{5,4},{3,2},{7,6},{8,9},{12,13},{10,... | collective-permute-start | bytes 786440 | tf_op jit(solution)/shard_map/ppermute | solution.py:408
  53.3 1.7 %collective-permute-start.23 = (f32[2,128,128]{2,1,0:T(8,128)S(1)}, f32[2,128,128]{2,1,0:T(8,128)S(1)}, u32[]{:S(2)}, u32[]{:S(2)}) collective-permute-start(f32[2,128,128]{2,1,0:T(8,128)S(1)} %get-tuple-element.93.refs_2_), channel_id=1, source_target_pairs={{0,2},{4,6},{2,0},{6,4},{1,8},{5,12},{3,10},{7,14},{8,1},{12,5},{1... | collective-permute-start | bytes 393224 | tf_op jit(solution)/shard_map/ppermute | solution.py:408
  55.0 2.9 %collective-permute-done.24.refs_4_ = f32[2,128,128]{2,1,0:T(8,128)S(1)} collective-permute-done((f32[2,128,128]{2,1,0:T(8,128)S(1)}, f32[2,128,128]{2,1,0:T(8,128)S(1)}, u32[]{:S(2)}, u32[]{:S(2)}) %collective-permute-start.24) | collective-permute-done | bytes 131104 | tf_op jit(solution)/shard_map/ppermute | solution.py:408
  58.3 0.9 %collective-permute-done.23.refs_4_ = f32[2,128,128]{2,1,0:T(8,128)S(1)} collective-permute-done((f32[2,128,128]{2,1,0:T(8,128)S(1)}, f32[2,128,128]{2,1,0:T(8,128)S(1)}, u32[]{:S(2)}, u32[]{:S(2)}) %collective-permute-start.23) | collective-permute-done | bytes 131104 | tf_op jit(solution)/shard_map/ppermute | solution.py:408
  60.2 1.7 %collective-permute-start.28 = (f32[2,128,128]{2,1,0:T(8,128)S(1)}, f32[2,128,128]{2,1,0:T(8,128)S(1)}, u32[]{:S(2)}, u32[]{:S(2)}) collective-permute-start(f32[2,128,128]{2,1,0:T(8,128)S(1)} %get-tuple-element.101.psi_b), channel_id=1, source_target_pairs={{0,2},{4,6},{2,0},{6,4},{1,8},{5,12},{3,10},{7,14},{8,1},{12,5},{1... | collective-permute-start | bytes 393224 | tf_op jit(solution)/shard_map/ppermute | solution.py:408
  62.0 0.7 collective-permute-start.21
  62.7 2.2 %collective-permute-done.26.got_b = f32[2,128,128]{2,1,0:T(8,128)S(1)} collective-permute-done((f32[2,128,128]{2,1,0:T(8,128)S(1)}, f32[2,128,128]{2,1,0:T(8,128)S(1)}, u32[]{:S(2)}, u32[]{:S(2)}) %collective-permute-start.26) | collective-permute-done | bytes 131104 | tf_op jit(solution)/shard_map/ppermute | solution.py:408
  64.9 0.8 %collective-permute-start.27 = (f32[2,128,128]{2,1,0:T(8,128)S(1)}, f32[2,128,128]{2,1,0:T(8,128)S(1)}, u32[]{:S(2)}, u32[]{:S(2)}) collective-permute-start(f32[2,128,128]{2,1,0:T(8,128)S(1)} %shard_map.93), channel_id=1, source_target_pairs={{0,3},{4,0},{2,1},{6,2},{1,7},{5,4},{3,5},{7,6},{8,11},{12,8},{10,... | collective-permute-start | bytes 393224 | tf_op jit(solution)/shard_map/ppermute | solution.py:408
  65.7 0.6 collective-permute-done.28.got_b
  66.3 0.8 %collective-permute-start.29 = (f32[2,128,128]{2,1,0:T(8,128)S(1)}, f32[2,128,128]{2,1,0:T(8,128)S(1)}, u32[]{:S(2)}, u32[]{:S(2)}) collective-permute-start(f32[2,128,128]{2,1,0:T(8,128)S(1)} %shard_map.94), channel_id=1, source_target_pairs={{0,3},{4,0},{2,1},{6,2},{1,7},{5,4},{3,5},{7,6},{8,11},{12,8},{10,... | collective-permute-start | bytes 393224 | tf_op jit(solution)/shard_map/ppermute | solution.py:408
  67.1 3.6 %collective-permute-done.21.refs_0_ = f32[2,128,128]{2,1,0:T(8,128)S(1)} collective-permute-done((f32[2,128,128]{2,1,0:T(8,128)S(1)}, f32[2,128,128]{2,1,0:T(8,128)S(1)}, u32[]{:S(2)}, u32[]{:S(2)}) %collective-permute-start.21) | collective-permute-done | bytes 131104 | tf_op jit(solution)/shard_map/ppermute | solution.py:408
  70.7 0.7 shard_map.90
  71.3 1.9 %collective-permute-done.27.refs_0_ = f32[2,128,128]{2,1,0:T(8,128)S(1)} collective-permute-done((f32[2,128,128]{2,1,0:T(8,128)S(1)}, f32[2,128,128]{2,1,0:T(8,128)S(1)}, u32[]{:S(2)}, u32[]{:S(2)}) %collective-permute-start.27) | collective-permute-done | bytes 131104 | tf_op jit(solution)/shard_map/ppermute | solution.py:408
  73.2 1.2 %collective-permute-done.29.refs_1_ = f32[2,128,128]{2,1,0:T(8,128)S(1)} collective-permute-done((f32[2,128,128]{2,1,0:T(8,128)S(1)}, f32[2,128,128]{2,1,0:T(8,128)S(1)}, u32[]{:S(2)}, u32[]{:S(2)}) %collective-permute-start.29) | collective-permute-done | bytes 131104 | tf_op jit(solution)/shard_map/ppermute | solution.py:408
  74.4 0.7 shard_map.95
  (39 shorter events, 4.7 us)
Async XLA Ops:
  0.6 6.1 %collective-permute-start.2 = (f32[1,1,4,128,128]{4,3,2,1,0:T(8,128)}, f32[1,1,4,128,128]{4,3,2,1,0:T(8,128)S(1)}, u32[]{:S(2)}, u32[]{:S(2)}) collective-permute-start(f32[1,1,4,128,128]{4,3,2,1,0:T(8,128)} %param.8), channel_id=1, source_target_pairs={{0,6},{1,0},{2,4},{3,2},{4,7},{5,1},{6,5},{7,3},{8,14},{9,8},{10,1... | collective-permute-start | bytes 786440 | tf_op jit(solution)/shard_map/ppermute | solution.py:408
  6.7 10.2 %collective-permute-start.3 = (f32[1,1,4,128,128]{4,3,2,1,0:T(8,128)S(1)}, f32[1,1,4,128,128]{4,3,2,1,0:T(8,128)S(1)}, u32[]{:S(2)}, u32[]{:S(2)}) collective-permute-start(f32[1,1,4,128,128]{4,3,2,1,0:T(8,128)S(1)} %collective-permute-done.2.whole.refs_3_.refs_4_), channel_id=1, source_target_pairs={{0,1},{4,5},{2,3},{6,7},{1,0},{5,4},{3,2},{7,6},{8,9},{12,13},{10,... | collective-permute-start | bytes 786440 | tf_op jit(solution)/shard_map/ppermute | solution.py:408
  8.8 6.3 %collective-permute-start = (s32[2,128,128]{2,1,0:T(8,128)}, s32[2,128,128]{2,1,0:T(8,128)S(1)}, u32[]{:S(2)}, u32[]{:S(2)}) collective-permute-start(s32[2,128,128]{2,1,0:T(8,128)} %param.7), channel_id=1, source_target_pairs={{0,6},{1,0},{2,4},{3,2},{4,7},{5,1},{6,5},{7,3},{8,14},{9,8},{10,1... | collective-permute-start | bytes 393224 | tf_op jit(solution)/shard_map/ppermute | solution.py:408
  8.8 8.1 %collective-permute-start.1 = (f32[1,2,128,128]{3,2,1,0:T(8,128)}, f32[1,2,128,128]{3,2,1,0:T(8,128)S(1)}, u32[]{:S(2)}, u32[]{:S(2)}) collective-permute-start(f32[1,2,128,128]{3,2,1,0:T(8,128)} %param.6), channel_id=1, source_target_pairs={{0,6},{1,0},{2,4},{3,2},{4,7},{5,1},{6,5},{7,3},{8,14},{9,8},{10,1... | collective-permute-start | bytes 393224 | tf_op jit(solution)/shard_map/ppermute | solution.py:408
  12.1 4.8 %collective-permute-start.4 = (f32[2,128,128]{2,1,0:T(8,128)S(1)}, f32[2,128,128]{2,1,0:T(8,128)S(1)}, u32[]{:S(2)}, u32[]{:S(2)}) collective-permute-start(f32[2,128,128]{2,1,0:T(8,128)S(1)} %get-tuple-element.54), channel_id=1, source_target_pairs={{0,2},{4,6},{2,0},{6,4},{1,8},{5,12},{3,10},{7,14},{8,1},{12,5},{1... | collective-permute-start | bytes 393224 | tf_op jit(solution)/shard_map/ppermute | solution.py:408
  14.0 4.7 %collective-permute-start.5 = (f32[2,128,128]{2,1,0:T(8,128)S(1)}, f32[2,128,128]{2,1,0:T(8,128)S(1)}, u32[]{:S(2)}, u32[]{:S(2)}) collective-permute-start(f32[2,128,128]{2,1,0:T(8,128)S(1)} %get-tuple-element.57), channel_id=1, source_target_pairs={{0,2},{4,6},{2,0},{6,4},{1,8},{5,12},{3,10},{7,14},{8,1},{12,5},{1... | collective-permute-start | bytes 393224 | tf_op jit(solution)/shard_map/ppermute | solution.py:408
  14.1 1.0 %copy-start = (f32[2,1,4,128,128]{4,3,2,1,0:T(8,128)S(1)}, f32[2,1,4,128,128]{4,3,2,1,0:T(8,128)}, u32[]{:S(2)}) copy-start(f32[2,1,4,128,128]{4,3,2,1,0:T(8,128)} %refs_10_.3) | copy-start | bytes 1572868
  15.2 0.9 %copy-start.2 = (f32[4]{0:T(128)S(1)}, f32[4]{0:T(128)}, u32[]{:S(2)}) copy-start(f32[4]{0:T(128)} %cond_ref.1) | copy-start | bytes 52
  15.2 0.9 %copy-start.3 = (f32[4]{0:T(128)S(1)}, f32[4]{0:T(128)}, u32[]{:S(2)}) copy-start(f32[4]{0:T(128)} %cap_ref.1) | copy-start | bytes 52
  15.2 7.4 %collective-permute-start.10 = (f32[4,128,128]{2,1,0:T(8,128)S(1)}, f32[4,128,128]{2,1,0:T(8,128)S(1)}, u32[]{:S(2)}, u32[]{:S(2)}) collective-permute-start(f32[4,128,128]{2,1,0:T(8,128)S(1)} %shard_map.81), channel_id=1, source_target_pairs={{0,6},{1,0},{2,4},{3,2},{4,7},{5,1},{6,5},{7,3},{8,14},{9,8},{10,1... | collective-permute-start | bytes 786440 | tf_op jit(solution)/shard_map/ppermute | solution.py:408
  18.7 6.8 %copy-start.1 = (f32[2,1,4,128,128]{4,3,2,1,0:T(8,128)S(1)}, f32[2,1,4,128,128]{4,3,2,1,0:T(8,128)}, u32[]{:S(2)}) copy-start(f32[2,1,4,128,128]{4,3,2,1,0:T(8,128)} %refs_10_.3) | copy-start | bytes 1572868
  19.2 6.3 %collective-permute-start.7 = (f32[4,128,128]{2,1,0:T(8,128)S(1)}, f32[4,128,128]{2,1,0:T(8,128)S(1)}, u32[]{:S(2)}, u32[]{:S(2)}) collective-permute-start(f32[4,128,128]{2,1,0:T(8,128)S(1)} %get-tuple-element.62.refs_1_), channel_id=1, source_target_pairs={{0,1},{4,5},{2,3},{6,7},{1,0},{5,4},{3,2},{7,6},{8,9},{12,13},{10,... | collective-permute-start | bytes 786440 | tf_op jit(solution)/shard_map/ppermute | solution.py:408
  20.8 4.7 %collective-permute-start.9 = (f32[2,128,128]{2,1,0:T(8,128)S(1)}, f32[2,128,128]{2,1,0:T(8,128)S(1)}, u32[]{:S(2)}, u32[]{:S(2)}) collective-permute-start(f32[2,128,128]{2,1,0:T(8,128)S(1)} %get-tuple-element.64.refs_2_), channel_id=1, source_target_pairs={{0,2},{4,6},{2,0},{6,4},{1,8},{5,12},{3,10},{7,14},{8,1},{12,5},{1... | collective-permute-start | bytes 393224 | tf_op jit(solution)/shard_map/ppermute | solution.py:408
  21.7 5.2 %collective-permute-start.8 = (f32[2,128,128]{2,1,0:T(8,128)S(1)}, f32[2,128,128]{2,1,0:T(8,128)S(1)}, u32[]{:S(2)}, u32[]{:S(2)}) collective-permute-start(f32[2,128,128]{2,1,0:T(8,128)S(1)} %get-tuple-element.63.refs_2_), channel_id=1, source_target_pairs={{0,2},{4,6},{2,0},{6,4},{1,8},{5,12},{3,10},{7,14},{8,1},{12,5},{1... | collective-permute-start | bytes 393224 | tf_op jit(solution)/shard_map/ppermute | solution.py:408
  27.4 6.3 %collective-permute-start.11 = (f32[4,128,128]{2,1,0:T(8,128)S(1)}, f32[4,128,128]{2,1,0:T(8,128)S(1)}, u32[]{:S(2)}, u32[]{:S(2)}) collective-permute-start(f32[4,128,128]{2,1,0:T(8,128)S(1)} %get-tuple-element.67.refs_5_.refs_6_), channel_id=1, source_target_pairs={{0,1},{4,5},{2,3},{6,7},{1,0},{5,4},{3,2},{7,6},{8,9},{12,13},{10,... | collective-permute-start | bytes 786440 | tf_op jit(solution)/shard_map/ppermute | solution.py:408
  27.8 4.9 %collective-permute-start.6 = (f32[2,128,128]{2,1,0:T(8,128)S(1)}, f32[2,128,128]{2,1,0:T(8,128)S(1)}, u32[]{:S(2)}, u32[]{:S(2)}) collective-permute-start(f32[2,128,128]{2,1,0:T(8,128)S(1)} %get-tuple-element.58), channel_id=1, source_target_pairs={{0,6},{4,0},{2,4},{6,2},{1,7},{5,1},{3,5},{7,3},{8,14},{12,8},{10,... | collective-permute-start | bytes 393224 | tf_op jit(solution)/shard_map/ppermute | solution.py:408
  28.9 4.7 %collective-permute-start.12 = (f32[2,128,128]{2,1,0:T(8,128)S(1)}, f32[2,128,128]{2,1,0:T(8,128)S(1)}, u32[]{:S(2)}, u32[]{:S(2)}) collective-permute-start(f32[2,128,128]{2,1,0:T(8,128)S(1)} %get-tuple-element.68.refs_6_), channel_id=1, source_target_pairs={{0,2},{4,6},{2,0},{6,4},{1,8},{5,12},{3,10},{7,14},{8,1},{12,5},{1... | collective-permute-start | bytes 393224 | tf_op jit(solution)/shard_map/ppermute | solution.py:408
  29.0 6.0 %collective-permute-start.13 = (f32[2,128,128]{2,1,0:T(8,128)S(1)}, f32[2,128,128]{2,1,0:T(8,128)S(1)}, u32[]{:S(2)}, u32[]{:S(2)}) collective-permute-start(f32[2,128,128]{2,1,0:T(8,128)S(1)} %get-tuple-element.73.refs_7_), channel_id=1, source_target_pairs={{0,2},{4,6},{2,0},{6,4},{1,8},{5,12},{3,10},{7,14},{8,1},{12,5},{1... | collective-permute-start | bytes 393224 | tf_op jit(solution)/shard_map/ppermute | solution.py:408
  35.6 6.3 %collective-permute-start.15 = (f32[4,128,128]{2,1,0:T(8,128)S(1)}, f32[4,128,128]{2,1,0:T(8,128)S(1)}, u32[]{:S(2)}, u32[]{:S(2)}) collective-permute-start(f32[4,128,128]{2,1,0:T(8,128)S(1)} %get-tuple-element.77.refs_1_), channel_id=1, source_target_pairs={{0,1},{4,5},{2,3},{6,7},{1,0},{5,4},{3,2},{7,6},{8,9},{12,13},{10,... | collective-permute-start | bytes 786440 | tf_op jit(solution)/shard_map/ppermute | solution.py:408
  37.2 4.7 %collective-permute-start.17 = (f32[2,128,128]{2,1,0:T(8,128)S(1)}, f32[2,128,128]{2,1,0:T(8,128)S(1)}, u32[]{:S(2)}, u32[]{:S(2)}) collective-permute-start(f32[2,128,128]{2,1,0:T(8,128)S(1)} %get-tuple-element.79.refs_2_), channel_id=1, source_target_pairs={{0,2},{4,6},{2,0},{6,4},{1,8},{5,12},{3,10},{7,14},{8,1},{12,5},{1... | collective-permute-start | bytes 393224 | tf_op jit(solution)/shard_map/ppermute | solution.py:408
  38.2 5.0 %collective-permute-start.16 = (f32[2,128,128]{2,1,0:T(8,128)S(1)}, f32[2,128,128]{2,1,0:T(8,128)S(1)}, u32[]{:S(2)}, u32[]{:S(2)}) collective-permute-start(f32[2,128,128]{2,1,0:T(8,128)S(1)} %get-tuple-element.78.refs_2_), channel_id=1, source_target_pairs={{0,2},{4,6},{2,0},{6,4},{1,8},{5,12},{3,10},{7,14},{8,1},{12,5},{1... | collective-permute-start | bytes 393224 | tf_op jit(solution)/shard_map/ppermute | solution.py:408
  43.7 5.4 %collective-permute-start.18 = (f32[4,128,128]{2,1,0:T(8,128)S(1)}, f32[4,128,128]{2,1,0:T(8,128)S(1)}, u32[]{:S(2)}, u32[]{:S(2)}) collective-permute-start(f32[4,128,128]{2,1,0:T(8,128)S(1)} %get-tuple-element.82.refs_5_.refs_6_), channel_id=1, source_target_pairs={{0,1},{4,5},{2,3},{6,7},{1,0},{5,4},{3,2},{7,6},{8,9},{12,13},{10,... | collective-permute-start | bytes 786440 | tf_op jit(solution)/shard_map/ppermute | solution.py:408
  44.2 4.9 %collective-permute-start.14 = (f32[2,128,128]{2,1,0:T(8,128)S(1)}, f32[2,128,128]{2,1,0:T(8,128)S(1)}, u32[]{:S(2)}, u32[]{:S(2)}) collective-permute-start(f32[2,128,128]{2,1,0:T(8,128)S(1)} %get-tuple-element.74), channel_id=1, source_target_pairs={{0,6},{4,0},{2,4},{6,2},{1,7},{5,1},{3,5},{7,3},{8,14},{12,8},{10,... | collective-permute-start | bytes 393224 | tf_op jit(solution)/shard_map/ppermute | solution.py:408
  44.4 4.7 %collective-permute-start.19 = (f32[2,128,128]{2,1,0:T(8,128)S(1)}, f32[2,128,128]{2,1,0:T(8,128)S(1)}, u32[]{:S(2)}, u32[]{:S(2)}) collective-permute-start(f32[2,128,128]{2,1,0:T(8,128)S(1)} %get-tuple-element.83.refs_6_), channel_id=1, source_target_pairs={{0,2},{4,6},{2,0},{6,4},{1,8},{5,12},{3,10},{7,14},{8,1},{12,5},{1... | collective-permute-start | bytes 393224 | tf_op jit(solution)/shard_map/ppermute | solution.py:408
  45.8 4.7 %collective-permute-start.20 = (f32[2,128,128]{2,1,0:T(8,128)S(1)}, f32[2,128,128]{2,1,0:T(8,128)S(1)}, u32[]{:S(2)}, u32[]{:S(2)}) collective-permute-start(f32[2,128,128]{2,1,0:T(8,128)S(1)} %get-tuple-element.88.refs_7_), channel_id=1, source_target_pairs={{0,2},{4,6},{2,0},{6,4},{1,8},{5,12},{3,10},{7,14},{8,1},{12,5},{1... | collective-permute-start | bytes 393224 | tf_op jit(solution)/shard_map/ppermute | solution.py:408
  51.1 6.8 %collective-permute-start.22 = (f32[4,128,128]{2,1,0:T(8,128)S(1)}, f32[4,128,128]{2,1,0:T(8,128)S(1)}, u32[]{:S(2)}, u32[]{:S(2)}) collective-permute-start(f32[4,128,128]{2,1,0:T(8,128)S(1)} %get-tuple-element.92.refs_1_), channel_id=1, source_target_pairs={{0,1},{4,5},{2,3},{6,7},{1,0},{5,4},{3,2},{7,6},{8,9},{12,13},{10,... | collective-permute-start | bytes 786440 | tf_op jit(solution)/shard_map/ppermute | solution.py:408
  53.2 4.7 %collective-permute-start.24 = (f32[2,128,128]{2,1,0:T(8,128)S(1)}, f32[2,128,128]{2,1,0:T(8,128)S(1)}, u32[]{:S(2)}, u32[]{:S(2)}) collective-permute-start(f32[2,128,128]{2,1,0:T(8,128)S(1)} %get-tuple-element.94.refs_2_), channel_id=1, source_target_pairs={{0,2},{4,6},{2,0},{6,4},{1,8},{5,12},{3,10},{7,14},{8,1},{12,5},{1... | collective-permute-start | bytes 393224 | tf_op jit(solution)/shard_map/ppermute | solution.py:408
  53.3 6.0 %collective-permute-start.23 = (f32[2,128,128]{2,1,0:T(8,128)S(1)}, f32[2,128,128]{2,1,0:T(8,128)S(1)}, u32[]{:S(2)}, u32[]{:S(2)}) collective-permute-start(f32[2,128,128]{2,1,0:T(8,128)S(1)} %get-tuple-element.93.refs_2_), channel_id=1, source_target_pairs={{0,2},{4,6},{2,0},{6,4},{1,8},{5,12},{3,10},{7,14},{8,1},{12,5},{1... | collective-permute-start | bytes 393224 | tf_op jit(solution)/shard_map/ppermute | solution.py:408
  59.8 5.2 %collective-permute-start.25 = (f32[4,128,128]{2,1,0:T(8,128)S(1)}, f32[4,128,128]{2,1,0:T(8,128)S(1)}, u32[]{:S(2)}, u32[]{:S(2)}) collective-permute-start(f32[4,128,128]{2,1,0:T(8,128)S(1)} %get-tuple-element.97.psi_a), channel_id=1, source_target_pairs={{0,1},{4,5},{2,3},{6,7},{1,0},{5,4},{3,2},{7,6},{8,9},{12,13},{10,... | collective-permute-start | bytes 786440 | tf_op jit(solution)/shard_map/ppermute | solution.py:408
  60.2 4.7 %collective-permute-start.26 = (f32[2,128,128]{2,1,0:T(8,128)S(1)}, f32[2,128,128]{2,1,0:T(8,128)S(1)}, u32[]{:S(2)}, u32[]{:S(2)}) collective-permute-start(f32[2,128,128]{2,1,0:T(8,128)S(1)} %get-tuple-element.98.psi_b), channel_id=1, source_target_pairs={{0,2},{4,6},{2,0},{6,4},{1,8},{5,12},{3,10},{7,14},{8,1},{12,5},{1... | collective-permute-start | bytes 393224 | tf_op jit(solution)/shard_map/ppermute | solution.py:408
  60.2 6.1 %collective-permute-start.28 = (f32[2,128,128]{2,1,0:T(8,128)S(1)}, f32[2,128,128]{2,1,0:T(8,128)S(1)}, u32[]{:S(2)}, u32[]{:S(2)}) collective-permute-start(f32[2,128,128]{2,1,0:T(8,128)S(1)} %get-tuple-element.101.psi_b), channel_id=1, source_target_pairs={{0,2},{4,6},{2,0},{6,4},{1,8},{5,12},{3,10},{7,14},{8,1},{12,5},{1... | collective-permute-start | bytes 393224 | tf_op jit(solution)/shard_map/ppermute | solution.py:408
  62.0 8.7 %collective-permute-start.21 = (f32[2,128,128]{2,1,0:T(8,128)S(1)}, f32[2,128,128]{2,1,0:T(8,128)S(1)}, u32[]{:S(2)}, u32[]{:S(2)}) collective-permute-start(f32[2,128,128]{2,1,0:T(8,128)S(1)} %get-tuple-element.89), channel_id=1, source_target_pairs={{0,3},{4,0},{2,1},{6,2},{1,7},{5,4},{3,5},{7,6},{8,11},{12,8},{10,... | collective-permute-start | bytes 393224 | tf_op jit(solution)/shard_map/ppermute | solution.py:408
  64.9 8.3 %collective-permute-start.27 = (f32[2,128,128]{2,1,0:T(8,128)S(1)}, f32[2,128,128]{2,1,0:T(8,128)S(1)}, u32[]{:S(2)}, u32[]{:S(2)}) collective-permute-start(f32[2,128,128]{2,1,0:T(8,128)S(1)} %shard_map.93), channel_id=1, source_target_pairs={{0,3},{4,0},{2,1},{6,2},{1,7},{5,4},{3,5},{7,6},{8,11},{12,8},{10,... | collective-permute-start | bytes 393224 | tf_op jit(solution)/shard_map/ppermute | solution.py:408
  66.3 8.1 %collective-permute-start.29 = (f32[2,128,128]{2,1,0:T(8,128)S(1)}, f32[2,128,128]{2,1,0:T(8,128)S(1)}, u32[]{:S(2)}, u32[]{:S(2)}) collective-permute-start(f32[2,128,128]{2,1,0:T(8,128)S(1)} %shard_map.94), channel_id=1, source_target_pairs={{0,3},{4,0},{2,1},{6,2},{1,7},{5,4},{3,5},{7,6},{8,11},{12,8},{10,... | collective-permute-start | bytes 393224 | tf_op jit(solution)/shard_map/ppermute | solution.py:408
